TPU v7x, 32 devices: a whole 2x2x4 slice. The times are simulated.
32 devices in a mesh: team: 4 (over x, core), blk: 8 (over z, y).
Axes of the slice: x: 2, y: 2, z: 4, core: 2. Of those that a mesh axis runs over, the one named last changes fastest.
Arguments:
- queries: bfloat16 [4096, 512], P(('blk', 'team')), may hold values from -6 to 6
- keys: bfloat16 [4096, 64], P(('blk', 'team')), may hold values from -6 to 6
- values: bfloat16 [4096, 64], P(('blk', 'team')), may hold values from -6 to 6
- attn_out: bfloat16 [4096, 512], P(('blk', 'team')), may hold values from -6 to 6
- out_grad: bfloat16 [4096, 512], P(('blk', 'team')), may hold values from -18 to 18
- log_norm: float32 [8, 4096], P(None, ('blk', 'team')), may hold values from 0 to 10
- doc_start: int32 [4096], P(('blk', 'team')), may hold values from 0 to 4095, as said below
Outputs:
- query_grad: bfloat16 [4096, 512], P(('blk', 'team'))
- key_grad: bfloat16 [4096, 64], P(('blk', 'team'))
- value_grad: bfloat16 [4096, 64], P(('blk', 'team'))
Inputs may be any that keep to these rules, and one draw needn't show every extreme that they name: `doc_start`: documents are runs of consecutive positions, each at most 512 long and one exactly 512; every value is the first position of its run, never after the position itself.
All inputs are finite; a program needn't handle non-finite values.
Results may differ from a plain program's by a relative error of at most 0.0058.
Values may be sent and summed in bfloat16 or wider, within the bound.
No kernel may reach another device: no remote copies, remote signals or barrier semaphores. Data moves between devices by JAX's collectives and lax.ppermute only.
A program may use at most 64 MiB of HBM per device.

v0:
```python
import math

import jax
import jax.numpy as jnp
from jax import lax
from jax.sharding import PartitionSpec as P


def passed_along(x, axis, by):
    count = lax.axis_size(axis)
    pairs = [(i, i + by) for i in range(count) if 0 <= i + by < count]
    return lax.ppermute(x, axis, pairs)


def visible_pairs(query_pos, query_begin, key_pos):
    return (key_pos[None, :] <= query_pos[:, None]) & (key_pos[None, :] >= query_begin[:, None])


def grad_terms(query_rows, grad_rows, log_rows, delta_rows, key_block, value_block, allowed):
    row_count = query_rows.shape[0]
    head_count = log_rows.shape[0]
    head_width = key_block.shape[1]
    factor = 1.0 / math.sqrt(head_width)
    query_heads = query_rows.reshape(row_count, head_count, head_width)
    grad_heads = grad_rows.reshape(row_count, head_count, head_width)
    scores = (
        jnp.einsum("rhd,cd->hrc", query_heads, key_block, preferred_element_type=jnp.float32)
        * factor
    )
    weights = jnp.where(allowed[None], jnp.exp(scores - log_rows[:, :, None]), jnp.float32(0.0))
    value_grad = jnp.einsum(
        "hrc,rhd->cd", weights.astype(jnp.bfloat16), grad_heads, preferred_element_type=jnp.float32
    )
    prob_grad = jnp.einsum(
        "rhd,cd->hrc", grad_heads, value_block, preferred_element_type=jnp.float32
    )
    score_grad = (weights * (prob_grad - delta_rows[:, :, None])).astype(jnp.bfloat16)
    query_grad = jnp.einsum(
        "hrc,cd->rhd", score_grad, key_block, preferred_element_type=jnp.float32
    )
    query_grad = query_grad.reshape(row_count, head_count * head_width) * factor
    key_grad = (
        jnp.einsum("hrc,rhd->cd", score_grad, query_heads, preferred_element_type=jnp.float32)
        * factor
    )
    return (query_grad, key_grad, value_grad)


def block_terms(query_rows, grad_rows, log_rows, delta_rows, key_block, value_block, allowed):
    return grad_terms(query_rows, grad_rows, log_rows, delta_rows, key_block, value_block, allowed)


def tiled_terms(
    query_rows,
    grad_rows,
    log_rows,
    delta_rows,
    query_pos,
    query_begin,
    key_block,
    value_block,
    key_pos,
):
    query_count = query_rows.shape[0]
    key_count = key_block.shape[0]
    feature_count = query_rows.shape[1]
    head_count = log_rows.shape[0]
    head_width = key_block.shape[1]
    row_step = math.gcd(query_count, 512)
    key_step = math.gcd(key_count, 512)
    row_tiles = query_count // row_step
    key_tiles = key_count // key_step
    query_pieces = (
        query_rows.reshape(row_tiles, row_step, feature_count),
        grad_rows.reshape(row_tiles, row_step, feature_count),
        log_rows.reshape(head_count, row_tiles, row_step).transpose(1, 0, 2),
        delta_rows.reshape(head_count, row_tiles, row_step).transpose(1, 0, 2),
        query_pos.reshape(row_tiles, row_step),
        query_begin.reshape(row_tiles, row_step),
    )
    key_pieces = (
        key_block.reshape(key_tiles, key_step, head_width),
        value_block.reshape(key_tiles, key_step, head_width),
        key_pos.reshape(key_tiles, key_step),
    )

    def outer(carried, query_piece):
        key_acc, value_acc = carried
        rows_now, grads_now, logs_now, deltas_now, pos_now, begin_now = query_piece

        def inner(query_acc, key_piece):
            keys_now, values_now, kpos_now = key_piece
            allowed = visible_pairs(pos_now, begin_now, kpos_now)
            query_term, key_term, value_term = block_terms(
                rows_now, grads_now, logs_now, deltas_now, keys_now, values_now, allowed
            )
            return (query_acc + query_term, (key_term, value_term))

        query_acc, (key_terms, value_terms) = lax.scan(
            inner, jnp.zeros((row_step, feature_count), jnp.float32), key_pieces
        )
        return ((key_acc + key_terms, value_acc + value_terms), query_acc)

    zero_keys = jnp.zeros((key_tiles, key_step, head_width), jnp.float32)
    (key_acc, value_acc), query_grad = lax.scan(outer, (zero_keys, zero_keys), query_pieces)
    return (
        query_grad.reshape(query_count, feature_count),
        key_acc.reshape(key_count, head_width),
        value_acc.reshape(key_count, head_width),
    )


def per_device(queries, keys, values, attn_out, out_grad, log_norm, doc_start):
    tok_rows = queries.shape[0]
    head_count = log_norm.shape[0]
    head_width = keys.shape[1]
    team_count = lax.axis_size("team")
    cycle_count = lax.axis_size("blk")
    team_index = lax.axis_index("team")
    cycle_index = lax.axis_index("blk")
    block_rows = tok_rows * team_count
    offsets = jnp.arange(tok_rows, dtype=jnp.int32)
    delta = jnp.einsum(
        "rhd,rhd->hr",
        out_grad.reshape(tok_rows, head_count, head_width),
        attn_out.reshape(tok_rows, head_count, head_width),
        preferred_element_type=jnp.float32,
    )
    begins = doc_start.astype(jnp.float32)
    block_pos = cycle_index * block_rows + jnp.arange(block_rows, dtype=jnp.int32)

    def slot_pos(block_number):
        return (block_number % cycle_count * team_count + team_index) * tok_rows + offsets

    query_block, grad_block = (
        lax.all_gather(queries, "team", axis=0, tiled=True),
        lax.all_gather(out_grad, "team", axis=0, tiled=True),
    )
    log_block, delta_block, begin_block = (
        lax.all_gather(log_norm, "team", axis=1, tiled=True),
        lax.all_gather(delta, "team", axis=1, tiled=True),
        lax.all_gather(begins, "team", axis=0, tiled=True),
    )
    near_keys, near_values = passed_along((keys, values), "blk", 1)
    key_pair = jnp.concatenate([keys, near_keys], 0)
    value_pair = jnp.concatenate([values, near_values], 0)
    key_pos = jnp.concatenate([slot_pos(cycle_index), slot_pos(cycle_index - 1 + cycle_count)])
    query_acc, key_acc, value_acc = tiled_terms(
        query_block,
        grad_block,
        log_block,
        delta_block,
        block_pos,
        begin_block.astype(jnp.int32),
        key_pair,
        value_pair,
        key_pos,
    )
    key_back, value_back = passed_along((key_acc[tok_rows:], value_acc[tok_rows:]), "blk", -1)
    key_grad = key_acc[:tok_rows] + key_back
    value_grad = value_acc[:tok_rows] + value_back
    query_grad = lax.psum_scatter(query_acc, "team", scatter_dimension=0, tiled=True)
    return (
        query_grad.astype(jnp.bfloat16),
        key_grad.astype(jnp.bfloat16),
        value_grad.astype(jnp.bfloat16),
    )


def solution(mesh):
    placed = (
        P(("blk", "team"), None),
        P(("blk", "team"), None),
        P(("blk", "team"), None),
        P(("blk", "team"), None),
        P(("blk", "team"), None),
        P(None, ("blk", "team")),
        P(("blk", "team")),
    )
    return jax.shard_map(
        per_device,
        mesh=mesh,
        in_specs=placed,
        out_specs=(P(("blk", "team"), None), P(("blk", "team"), None), P(("blk", "team"), None)),
        check_vma=False,
    )
```

profile of v0, /device:TPU:0, one launch (start us, length us, event | category | flops | bytes accessed | tf_op | source)
XLA Modules:
  0.0 88.8 jit_solution(15808860481382731863)
XLA Ops:
  7.2 0.0 copy-start.1
  7.2 0.0 copy-start.2
  7.2 0.0 reduce-scatter.2.cloned.1.call-start
  7.2 4.9 %collective-permute-start = (bf16[128,64]{0,1:T(8,128)(2,1)}, bf16[128,64]{0,1:T(8,128)(2,1)S(1)}, u32[]{:S(2)}, u32[]{:S(2)}) collective-permute-start(bf16[128,64]{0,1:T(8,128)(2,1)} %param.8), channel_id=1, source_target_pairs={{0,1},{1,2},{2,3},{3,4},{4,5},{5,6},{6,7},{8,9},{9,10},{10,11},{11... | collective-permute-start | bytes 49160 | tf_op jit(solution)/shard_map/ppermute | solution.py:12
  12.1 3.4 %collective-permute-start.1 = (bf16[128,64]{0,1:T(8,128)(2,1)}, bf16[128,64]{0,1:T(8,128)(2,1)S(1)}, u32[]{:S(2)}, u32[]{:S(2)}) collective-permute-start(bf16[128,64]{0,1:T(8,128)(2,1)} %param.9), channel_id=1, source_target_pairs={{0,1},{1,2},{2,3},{3,4},{4,5},{5,6},{6,7},{8,9},{9,10},{10,11},{11... | collective-permute-start | bytes 49160 | tf_op jit(solution)/shard_map/ppermute | solution.py:12
  15.6 7.4 %all_gather.18 = bf16[512,512]{1,0:T(8,128)(2,1)S(1)} all-gather(bf16[128,512]{1,0:T(8,128)(2,1)} %param.11), channel_id=1, replica_groups=mesh['team'=4,'blk'=8] {'team'}, dimensions={0}, use_global_device_ids=true | all-gather | bytes 655360 | tf_op jit(solution)/shard_map/all_gather | solution.py:137
  23.0 1.0 %copy.44 = bf16[128,512]{0,1:T(8,128)(2,1)S(1)} copy(bf16[128,512]{1,0:T(8,128)(2,1)} %param.11) | data formatting | bytes 262144
  24.0 0.0 copy-start.3
  24.1 0.7 convert_bitcast_fusion
  24.7 5.0 %all-gather = f32[4,1,128]{2,1,0:T(1,128)S(1)} all-gather(f32[1,1,128]{2,1,0:T(1,128)S(1)} %convert_bitcast_fusion), channel_id=1, replica_groups=mesh['team'=4,'blk'=8] {'team'}, dimensions={0}, use_global_device_ids=true | all-gather | bytes 2560 | tf_op jit(solution)/shard_map/all_gather | solution.py:142
  29.8 7.5 %all_gather.16 = bf16[512,512]{1,0:T(8,128)(2,1)S(1)} all-gather(bf16[128,512]{1,0:T(8,128)(2,1)} %param.7), channel_id=1, replica_groups=mesh['team'=4,'blk'=8] {'team'}, dimensions={0}, use_global_device_ids=true | all-gather | bytes 655360 | tf_op jit(solution)/shard_map/all_gather | solution.py:136
  37.2 1.0 %copy.43 = bf16[128,512]{0,1:T(8,128)(2,1)S(1)} copy(bf16[128,512]{1,0:T(8,128)(2,1)} %param.10) | data formatting | bytes 262144
  38.3 0.2 compare_and_fusion
  38.5 0.2 copy.24
  38.7 0.2 copy.25
  39.0 0.0 copy-done.2
  39.0 5.2 %all_gather.17 = f32[8,512]{1,0:T(8,128)S(1)} all-gather(f32[8,128]{1,0:T(8,128)S(1)} %copy-done.2), channel_id=1, replica_groups=mesh['team'=4,'blk'=8] {'team'}, dimensions={1}, use_global_device_ids=true | all-gather | bytes 20480 | tf_op jit(solution)/shard_map/all_gather | solution.py:140
  44.2 5.2 %all_gather.19 = f32[8,512]{1,0:T(8,128)S(1)} all-gather(f32[8,128]{1,0:T(8,128)S(1)} %fusion.12), channel_id=1, replica_groups=mesh['team'=4,'blk'=8] {'team'}, dimensions={1}, use_global_device_ids=true | all-gather | bytes 20480 | tf_op jit(solution)/shard_map/all_gather | solution.py:141
  49.4 0.0 collective-permute-done
  49.4 0.0 copy-done.1
  49.4 0.7 fusion.17
  50.1 0.0 copy-start
  50.1 0.0 collective-permute-done.1
  50.1 0.0 copy-done.3
  50.1 1.5 %fusion.1 = bf16[8,512,256]{1,2,0:T(8,128)(2,1)S(1)} fusion(f32[256,512,8]{1,0,2:T(8,128)S(1)} %fusion.17, bf16[512,8,64]{0,2,1:T(8,128)(2,1)S(1)} %bitcast.60, f32[8,512]{1,0:T(8,128)S(1)} %all_gather.19, f32[8,512]{1,0:T(8,128)S(1)} %all_gather.17, pred[512,256]{0,1:T(8,128)(4,1)S(1)} %compare_and_fusion, bf16[128,64]{0,1:T(8,128)(2,1)S(1)} %collective-permute-done.1, ...), kind=kOutput, calls=%fused_computation.2 | convolution fusion | flops 140574720 | bytes 7012352 | tf_op jit(solution)/shard_map/while/body/eval_jaxpr/while/body/eval_jaxpr/rhd,cd->hrc/dot_general | solution.py:34
  51.7 1.5 %convolution_multiply_fusion = f32[64,8,512]{2,0,1:T(8,128)} fusion(bf16[8,512,256]{1,2,0:T(8,128)(2,1)S(1)} %fusion.1, bf16[128,64]{0,1:T(8,128)(2,1)S(1)} %collective-permute-done, bf16[128,64]{0,1:T(8,128)(2,1)S(1)} %copy-done.1), kind=kOutput, calls=%fused_computation.9 | convolution fusion | flops 134545408 | bytes 3178496 | tf_op jit(solution)/shard_map/while/body/eval_jaxpr/while/body/eval_jaxpr/hrc,cd->rhd/dot_general | solution.py:38
  53.1 0.0 copy-done
  53.1 2.5 %copy.29 = f32[512,512]{1,0:T(8,128)} copy(f32[512,512]{0,1:T(8,128)} %bitcast.59) | data formatting | bytes 2097152 | tf_op jit(solution)/shard_map/while/body/eval_jaxpr/while/body/eval_jaxpr/mul | solution.py:41
  55.7 0.0 reduce-scatter.2.cloned.1.call-update
  55.7 3.1 %fusion.8 = f32[256,64]{0,1:T(8,128)S(1)} fusion(bf16[512,8,64]{0,2,1:T(8,128)(2,1)S(1)} %bitcast.61, f32[256,512,8]{1,0,2:T(8,128)} %copy-done, f32[8,512]{1,0:T(8,128)S(1)} %all_gather.17, pred[512,256]{0,1:T(8,128)(4,1)S(1)} %compare_and_fusion), kind=kOutput, calls=%fused_computation.10 | convolution fusion | flops 138412032 | bytes 4931584 | tf_op jit(solution)/shard_map/while/body/eval_jaxpr/while/body/eval_jaxpr/hrc,rhd->cd/dot_general | solution.py:31
  58.8 1.3 %collective-permute-start.3 = (f32[128,64]{0,1:T(8,128)S(1)}, f32[128,64]{0,1:T(8,128)S(1)}, u32[]{:S(2)}, u32[]{:S(2)}) collective-permute-start(f32[128,64]{0,1:T(8,128)S(1)} %slice.21), channel_id=1, source_target_pairs={{1,0},{2,1},{3,2},{4,3},{5,4},{6,5},{7,6},{9,8},{10,9},{11,10},{12... | collective-permute-start | bytes 98312 | tf_op jit(solution)/shard_map/ppermute | solution.py:12
  60.1 0.8 fusion.11
  60.9 1.3 %collective-permute-start.2 = (f32[128,64]{0,1:T(8,128)S(1)}, f32[128,64]{0,1:T(8,128)S(1)}, u32[]{:S(2)}, u32[]{:S(2)}) collective-permute-start(f32[128,64]{0,1:T(8,128)S(1)} %slice.19), channel_id=1, source_target_pairs={{1,0},{2,1},{3,2},{4,3},{5,4},{6,5},{7,6},{9,8},{10,9},{11,10},{12... | collective-permute-start | bytes 98312 | tf_op jit(solution)/shard_map/ppermute | solution.py:12
  62.2 2.4 %collective-permute-done.3 = f32[128,64]{0,1:T(8,128)S(1)} collective-permute-done((f32[128,64]{0,1:T(8,128)S(1)}, f32[128,64]{0,1:T(8,128)S(1)}, u32[]{:S(2)}, u32[]{:S(2)}) %collective-permute-start.3) | collective-permute-done | bytes 32800 | tf_op jit(solution)/shard_map/ppermute | solution.py:12
  64.6 0.6 fusion.13
  65.2 2.1 %collective-permute-done.2 = f32[128,64]{0,1:T(8,128)S(1)} collective-permute-done((f32[128,64]{0,1:T(8,128)S(1)}, f32[128,64]{0,1:T(8,128)S(1)}, u32[]{:S(2)}, u32[]{:S(2)}) %collective-permute-start.2) | collective-permute-done | bytes 32800 | tf_op jit(solution)/shard_map/ppermute | solution.py:12
  67.3 0.6 fusion.14
  67.9 12.4 %reduce-scatter.2.cloned.1.call-done = f32[128,512]{1,0:T(8,128)} async-done(((f32[512,512]{1,0:T(8,128)}), f32[128,512]{1,0:T(8,128)}) %reduce-scatter.2.cloned.1.call-update) | async-done | bytes 262160 | tf_op jit(solution)/shard_map/reduce_scatter | solution.py:162
  80.3 1.6 %convert_element_type.28 = bf16[128,512]{1,0:T(8,128)(2,1)} convert(f32[128,512]{1,0:T(8,128)} %reduce-scatter.2.cloned.1.call-done) | non-fusion elementwise | flops 65536 | bytes 393216 | tf_op jit(solution)/shard_map/convert_element_type | solution.py:164
  (7 shorter events, 0.1 us)
Async XLA Ops:
  7.2 42.2 %copy-start.1 = (bf16[128,64]{0,1:T(8,128)(2,1)S(1)}, bf16[128,64]{0,1:T(8,128)(2,1)}, u32[]{:S(2)}) copy-start(bf16[128,64]{0,1:T(8,128)(2,1)} %param.8) | copy-start | bytes 49156
  7.2 31.8 %copy-start.2 = (f32[8,128]{1,0:T(8,128)S(1)}, f32[8,128]{1,0:T(8,128)}, u32[]{:S(2)}) copy-start(f32[8,128]{1,0:T(8,128)} %param.12) | copy-start | bytes 12292
  7.2 73.1 %reduce-scatter.2.cloned.1.call-start = ((), (), s32[]{:S(2)}) async-start(), calls=%async_computation.1 | async-start | bytes 1310720 | tf_op jit(solution)/shard_map/reduce_scatter | solution.py:162
  7.2 42.1 %collective-permute-start = (bf16[128,64]{0,1:T(8,128)(2,1)}, bf16[128,64]{0,1:T(8,128)(2,1)S(1)}, u32[]{:S(2)}, u32[]{:S(2)}) collective-permute-start(bf16[128,64]{0,1:T(8,128)(2,1)} %param.8), channel_id=1, source_target_pairs={{0,1},{1,2},{2,3},{3,4},{4,5},{5,6},{6,7},{8,9},{9,10},{10,11},{11... | collective-permute-start | bytes 49160 | tf_op jit(solution)/shard_map/ppermute | solution.py:12
  12.1 38.0 %collective-permute-start.1 = (bf16[128,64]{0,1:T(8,128)(2,1)}, bf16[128,64]{0,1:T(8,128)(2,1)S(1)}, u32[]{:S(2)}, u32[]{:S(2)}) collective-permute-start(bf16[128,64]{0,1:T(8,128)(2,1)} %param.9), channel_id=1, source_target_pairs={{0,1},{1,2},{2,3},{3,4},{4,5},{5,6},{6,7},{8,9},{9,10},{10,11},{11... | collective-permute-start | bytes 49160 | tf_op jit(solution)/shard_map/ppermute | solution.py:12
  24.0 26.1 %copy-start.3 = (bf16[128,64]{0,1:T(8,128)(2,1)S(1)}, bf16[128,64]{0,1:T(8,128)(2,1)}, u32[]{:S(2)}) copy-start(bf16[128,64]{0,1:T(8,128)(2,1)} %param.9) | copy-start | bytes 49156
  50.1 3.0 %copy-start = (f32[256,512,8]{1,0,2:T(8,128)}, f32[256,512,8]{1,0,2:T(8,128)S(1)}, u32[]{:S(2)}) copy-start(f32[256,512,8]{1,0,2:T(8,128)S(1)} %fusion.17) | copy-start | bytes 12582916
  58.8 5.8 %collective-permute-start.3 = (f32[128,64]{0,1:T(8,128)S(1)}, f32[128,64]{0,1:T(8,128)S(1)}, u32[]{:S(2)}, u32[]{:S(2)}) collective-permute-start(f32[128,64]{0,1:T(8,128)S(1)} %slice.21), channel_id=1, source_target_pairs={{1,0},{2,1},{3,2},{4,3},{5,4},{6,5},{7,6},{9,8},{10,9},{11,10},{12... | collective-permute-start | bytes 98312 | tf_op jit(solution)/shard_map/ppermute | solution.py:12
  60.9 6.4 %collective-permute-start.2 = (f32[128,64]{0,1:T(8,128)S(1)}, f32[128,64]{0,1:T(8,128)S(1)}, u32[]{:S(2)}, u32[]{:S(2)}) collective-permute-start(f32[128,64]{0,1:T(8,128)S(1)} %slice.19), channel_id=1, source_target_pairs={{1,0},{2,1},{3,2},{4,3},{5,4},{6,5},{7,6},{9,8},{10,9},{11,10},{12... | collective-permute-start | bytes 98312 | tf_op jit(solution)/shard_map/ppermute | solution.py:12
Sparse Core Ops, SparseCore 0:
  55.8 24.4 reduce-scatter.1
where the time goes:
time: 89.2 us; the launch traced here: 88.8 us
  blocking collectives  30.3 us (34%)
  waiting for transfers between devices  16.9 us (19%)
  between operations  14.2 us (16%)
  starting transfers between devices  11 us (12%)
  matrix products  7.57 us (8%)
  local copies, waits for them, and re-layouts  5.03 us (6%)
  other arithmetic  3.75 us (4%)
    reduce_scatter x1, waiting for transfers between devices, per_device(): lax.psum_scatter(query_acc, 'team', scatter_dimension=0, tiled=True)  12.4 us
    ppermute x4, starting transfers between devices, passed_along(): return lax.ppermute(x, axis, pairs)  10.9 us
    all_gather x1, blocking collectives, per_device(): lax.all_gather(queries, 'team', axis=0, tiled=True)  7.47 us
    all_gather x1, blocking collectives, per_device(): lax.all_gather(out_grad, 'team', axis=0, tiled=True)  7.38 us
    all_gather x1, blocking collectives, per_device(): lax.all_gather(log_norm, 'team', axis=1, tiled=True)  5.21 us
    all_gather x1, blocking collectives, per_device(): lax.all_gather(delta, 'team', axis=1, tiled=True)  5.19 us
    all_gather x1, blocking collectives, per_device(): lax.all_gather(begins, 'team', axis=0, tiled=True)  5.05 us
    ppermute x4, waiting for transfers between devices, passed_along(): return lax.ppermute(x, axis, pairs)  4.53 us
  transfers between devices with their start and end apart: 5, of which 3 were waited for; matrix products, arithmetic and copies ran while one was open for 10% of the time, Pallas kernels for 0%

commit v1 on v0

v1 whole, which is shorter than its diff:
```python
import math

import jax
import jax.numpy as jnp
from jax import lax
from jax.experimental import pallas as pl
from jax.experimental.pallas import tpu as pltpu
from jax.sharding import PartitionSpec as P

NT = (((1,), (1,)), ((), ()))
NN = (((1,), (0,)), ((), ()))


def passed_along(x, axis, by):
    count = lax.axis_size(axis)
    pairs = [(i, i + by) for i in range(count) if 0 <= i + by < count]
    return lax.ppermute(x, axis, pairs)


def dot(a, b, dims):
    return lax.dot_general(a, b, dims, preferred_element_type=jnp.float32)


def grad_kernel(rows, team, heads, width):
    lanes = 2 * width
    window = (team + 1) * rows
    factor = 1.0 / math.sqrt(width)

    def body(q_ref, g_ref, o_ref, log_ref, begin_ref, own_ref, near_ref, *rest):
        dq_ref, own_out, near_out = rest[:3]
        piece_refs = rest[3 : 3 + team - 1]
        kv_ref, acc_ref = rest[3 + team - 1 :]
        spot = lax.axis_index("team")
        place = lax.axis_index("blk") * team + spot
        kv_ref[: team * rows] = near_ref[...]
        kv_ref[team * rows :] = own_ref[...]
        kv = kv_ref[pl.ds(pl.multiple_of(spot * rows, rows), window), :]
        low_lane = lax.broadcasted_iota(jnp.int32, (window, lanes), 1) < width
        none = jnp.zeros_like(kv)
        k_low = jnp.where(low_lane, kv * jnp.asarray(factor, kv.dtype), none)
        v_high = jnp.where(low_lane, none, kv)
        turned_k = jnp.concatenate([k_low[:, width:], k_low[:, :width]], 1)
        turned_v = jnp.concatenate([v_high[:, width:], v_high[:, :width]], 1)
        key_halves = (k_low, turned_k)
        value_halves = (turned_v, v_high)
        key_flip = k_low.astype(jnp.float32).T[:width].astype(kv.dtype)
        key_pos = lax.broadcasted_iota(jnp.int32, (window, rows), 0)
        row_pos = lax.broadcasted_iota(jnp.int32, (window, rows), 1) + team * rows
        begin = begin_ref[...] - (place - team) * rows
        allowed = (key_pos <= row_pos) & (key_pos >= begin)
        prod = g_ref[...].astype(jnp.float32) * o_ref[...].astype(jnp.float32)
        feature = lax.broadcasted_iota(jnp.int32, (heads, heads * width), 1)
        head_of = lax.broadcasted_iota(jnp.int32, (heads, heads * width), 0)
        pick = (feature // width == head_of).astype(jnp.float32)
        delta = lax.dot_general(
            pick,
            prod,
            NT,
            precision=lax.Precision.HIGHEST,
            preferred_element_type=jnp.float32,
        )
        row_low = lax.broadcasted_iota(jnp.int32, (rows, lanes), 1) < width
        for pair in range(heads // 2):
            span = slice(pair * lanes, (pair + 1) * lanes)
            q_pair = q_ref[:, span]
            g_pair = g_ref[:, span]
            q_turn = jnp.concatenate([q_pair[:, width:], q_pair[:, :width]], 1)
            g_turn = jnp.concatenate([g_pair[:, width:], g_pair[:, :width]], 1)
            blank = jnp.zeros_like(q_pair)
            stack = jnp.concatenate(
                [
                    jnp.where(row_low, q_pair, blank),
                    jnp.where(row_low, q_turn, blank),
                    jnp.where(row_low, blank, g_turn),
                    jnp.where(row_low, blank, g_pair),
                ],
                0,
            )
            probs, grads, flips = [], [], []
            for half in range(2):
                head = 2 * pair + half
                scores = dot(key_halves[half], q_pair, NT)
                shifted = scores - log_ref[head : head + 1, :]
                weights = jnp.exp(jnp.where(allowed, shifted, -jnp.inf))
                prob_grad = dot(value_halves[half], g_pair, NT)
                score_grad = weights * (prob_grad - delta[head : head + 1, :])
                low = score_grad.astype(jnp.bfloat16)
                probs.append(weights.astype(jnp.bfloat16))
                grads.append(low)
                flips.append(dot(key_flip, low, NN))
            term = dot(jnp.concatenate(grads + probs, 1), stack, NN)
            if pair == 0:
                acc_ref[...] = term
            else:
                acc_ref[...] += term
            dq_ref[:, span] = jnp.concatenate(flips, 0).T.astype(dq_ref.dtype)
        scale = jnp.where(row_low, jnp.float32(factor), jnp.float32(1.0))
        near_out[...] = acc_ref[:rows] * scale
        own_out[...] = acc_ref[team * rows :] * scale
        for step in range(1, team):
            ahead = ((spot ^ step) - spot + team) % team
            part = acc_ref[pl.ds(pl.multiple_of(ahead * rows, rows), rows), :]
            piece_refs[step - 1][...] = (part * scale).astype(jnp.bfloat16)

    self_shape = jax.ShapeDtypeStruct((rows, lanes), jnp.float32)
    piece_shape = jax.ShapeDtypeStruct((rows, lanes), jnp.bfloat16)
    return pl.pallas_call(
        body,
        out_shape=[
            jax.ShapeDtypeStruct((rows, heads * width), jnp.bfloat16),
            self_shape,
            self_shape,
        ]
        + [piece_shape] * (team - 1),
        scratch_shapes=[
            pltpu.VMEM((2 * team * rows, lanes), jnp.bfloat16),
            pltpu.VMEM((window, lanes), jnp.float32),
        ],
    )


def per_device(queries, keys, values, attn_out, out_grad, log_norm, doc_start):
    rows = queries.shape[0]
    heads = log_norm.shape[0]
    width = keys.shape[1]
    team = lax.axis_size("team")
    spot = lax.axis_index("team")
    packed = jnp.concatenate([keys, values], 1)
    own = lax.all_gather(packed, "team", axis=0, tiled=False)
    near = passed_along(own, "blk", 1)
    outs = grad_kernel(rows, team, heads, width)(
        queries,
        out_grad,
        attn_out,
        log_norm,
        doc_start.reshape(1, rows),
        own.reshape(team * rows, 2 * width),
        near.reshape(team * rows, 2 * width),
    )
    query_grad, own_sum, near_sum = outs[:3]
    nothing = jnp.float32(0.0)
    for step in range(1, team):
        got = lax.ppermute(outs[2 + step], "team", [(i, i ^ step) for i in range(team)])
        got = got.astype(jnp.float32)
        later = (spot ^ step) > spot
        own_sum = own_sum + jnp.where(later, got, nothing)
        near_sum = near_sum + jnp.where(later, nothing, got)
    back = passed_along(near_sum.astype(jnp.bfloat16), "blk", -1)
    total = (own_sum + back.astype(jnp.float32)).astype(jnp.bfloat16)
    return (query_grad, total[:, :width], total[:, width:])


def solution(mesh):
    row = P(("blk", "team"), None)
    return jax.shard_map(
        per_device,
        mesh=mesh,
        in_specs=(row, row, row, row, row, P(None, ("blk", "team")), P(("blk", "team"))),
        out_specs=(row, row, row),
        check_vma=False,
    )
```

time: 89.2 us -> 35.3 us (0.40)
  blocking collectives: 30.3 us -> 6.51 us
  between operations: 14.2 us -> 0.69 us
  matrix products: 7.57 us -> 0 us
  waiting for transfers between devices: 16.9 us -> 11.5 us
  Pallas kernels: 0 us -> 5.26 us
  starting transfers between devices: 11 us -> 6.96 us
  other arithmetic: 3.75 us -> 1.02 us
  local copies, waits for them, and re-layouts: 5.03 us -> 3.09 us
    all_gather x5 -> x1, blocking collectives: 30.3 us -> 6.51 us  [per_device(): own = lax.all_gather(packed, 'team', axis=0, tiled=False)]
    reduce_scatter x1 -> x0, waiting for transfers between devices: 12.4 us -> none  [per_device(): lax.psum_scatter(query_acc, 'team', scatter_dimension=0, tiled=True)]
    dot_general x5 -> x0, matrix products: 7.57 us -> none  [the longest x1 3.08 us: grad_terms(): jnp.einsum('hrc,rhd->cd', weights.astype(jnp.bfloat16), grad_heads, prefe...]
    ppermute x4 -> x2, starting transfers between devices: 10.9 us -> 5.09 us  [passed_along(): return lax.ppermute(x, axis, pairs)]
    pallas_call x0 -> x1, Pallas kernels: none -> 5.26 us  [per_device(): grad_kernel(rows, team, heads, width)]
    ppermute x4 -> x2, waiting for transfers between devices: 4.53 us -> 8.22 us  [passed_along(): return lax.ppermute(x, axis, pairs)]
    ppermute x0 -> x3, waiting for transfers between devices: none -> 3.24 us  [per_device(): lax.ppermute(outs[2 + step], 'team', [(i, i ^ step) for i in range(team)])]
    mul x1 -> x0, local copies, waits for them, and re-layouts: 2.53 us -> none  [grad_terms(): query_grad = query_grad.reshape(row_count, head_count * head_width) * factor]
  transfers between devices with their start and end apart: 5 -> 5, of which waited for: 3 -> 4; matrix products, arithmetic and copies ran while one was open for 10% -> 0% of each run, Pallas kernels for 0% -> 0%
where the time goes in v1:
time: 35.3 us; the launch traced here: 35 us
  waiting for transfers between devices  11.5 us (33%)
  starting transfers between devices  6.96 us (20%)
  blocking collectives  6.51 us (18%)
  Pallas kernels  5.26 us (15%)
  local copies, waits for them, and re-layouts  3.09 us (9%)
  other arithmetic  1.02 us (3%)
  between operations  0.69 us (2%)
    ppermute x2, waiting for transfers between devices, passed_along(): return lax.ppermute(x, axis, pairs)  8.22 us
    all_gather x1, blocking collectives, per_device(): own = lax.all_gather(packed, 'team', axis=0, tiled=False)  6.51 us
    pallas_call x1, Pallas kernels, per_device(): grad_kernel(rows, team, heads, width)  5.26 us
    ppermute x2, starting transfers between devices, passed_along(): return lax.ppermute(x, axis, pairs)  5.09 us
    ppermute x3, waiting for transfers between devices, per_device(): lax.ppermute(outs[2 + step], 'team', [(i, i ^ step) for i in range(team)])  3.24 us
    unnamed x12, local copies, waits for them, and re-layouts  3.01 us
    ppermute x3, starting transfers between devices, per_device(): lax.ppermute(outs[2 + step], 'team', [(i, i ^ step) for i in range(team)])  1.86 us
    convert_element_type x1, other arithmetic, per_device(): back = passed_along(near_sum.astype(jnp.bfloat16), 'blk', -1)  0.9 us
  transfers between devices with their start and end apart: 5, of which 4 were waited for; matrix products, arithmetic and copies ran while one was open for 0% of the time, Pallas kernels for 0%

profile of v1, /device:TPU:0, one launch (start us, length us, event | category | flops | bytes accessed | tf_op | source)
XLA Modules:
  0.0 35.0 jit_solution(2609733241551021814)
XLA Ops:
  0.6 0.0 copy-start.3
  0.6 0.8 %copy.11 = bf16[128,64]{1,0:T(8,128)(2,1)S(1)} copy(bf16[128,64]{0,1:T(8,128)(2,1)} %param.9) | data formatting | bytes 32768 | tf_op args[2]
  1.5 0.0 copy-done.3
  1.5 0.1 copy.10
  1.6 0.1 pad_maximum_fusion
  1.7 6.5 %all-gather.own_ref = bf16[512,128]{1,0:T(8,128)(2,1)S(1)} all-gather(bf16[128,128]{1,0:T(8,128)(2,1)S(1)} %pad_maximum_fusion), channel_id=2, replica_groups=mesh['team'=4,'blk'=8] {'team'}, dimensions={0}, use_global_device_ids=true | all-gather | bytes 163840 | tf_op jit(solution)/shard_map/all_gather | solution.py:129
  8.2 0.0 copy-start
  8.2 3.8 %collective-permute-start = (bf16[4,128,128]{2,1,0:T(8,128)(2,1)S(1)}, bf16[4,128,128]{2,1,0:T(8,128)(2,1)S(1)}, u32[]{:S(2)}, u32[]{:S(2)}) collective-permute-start(bf16[4,128,128]{2,1,0:T(8,128)(2,1)S(1)} %bitcast.3), channel_id=1, source_target_pairs={{0,1},{1,2},{2,3},{3,4},{4,5},{5,6},{6,7},{8,9},{9,10},{10,11},{11... | collective-permute-start | bytes 393224 | tf_op jit(solution)/shard_map/ppermute | solution.py:17
  12.0 3.2 %collective-permute-done = bf16[4,128,128]{2,1,0:T(8,128)(2,1)S(1)} collective-permute-done((bf16[4,128,128]{2,1,0:T(8,128)(2,1)S(1)}, bf16[4,128,128]{2,1,0:T(8,128)(2,1)S(1)}, u32[]{:S(2)}, u32[]{:S(2)}) %collective-permute-start) | collective-permute-done | bytes 131104 | tf_op jit(solution)/shard_map/ppermute | solution.py:17
  15.3 0.0 copy-start.1
  15.3 0.0 copy-done
  15.3 0.7 %copy-done.1 = bf16[4,128,128]{2,1,0:T(8,128)(2,1)} copy-done((bf16[4,128,128]{2,1,0:T(8,128)(2,1)}, bf16[4,128,128]{2,1,0:T(8,128)(2,1)S(1)}, u32[]{:S(2)}) %copy-start.1) | copy-done | bytes 131096
  15.9 5.3 %shard_map.94 = (bf16[128,512]{1,0:T(8,128)(2,1)}, f32[128,128]{1,0:T(8,128)}, f32[128,128]{1,0:T(8,128)}, bf16[128,128]{1,0:T(8,128)(2,1)}, bf16[128,128]{1,0:T(8,128)(2,1)}, /*index=5*/bf16[128,128]{1,0:T(8,128)(2,1)}) custom-call(bf16[128,512]{1,0:T(8,128)(2,1)} %q_ref.1, bf16[128,512]{1,0:T(8,128)(2,1)} %g_ref.1, bf16[128,512]{1,0:T(8,128)(2,1)} %o_ref.1, ...), custom_call_target="tpu_custom_call" | custom-call | tf_op jit(solution)/shard_map/pallas_call | solution.py:131
  21.2 0.0 collective-permute-start.1
  21.2 1.5 %collective-permute-start.2 = (bf16[128,128]{1,0:T(8,128)(2,1)}, bf16[128,128]{1,0:T(8,128)(2,1)S(1)}, u32[]{:S(2)}, u32[]{:S(2)}) collective-permute-start(bf16[128,128]{1,0:T(8,128)(2,1)} %get-tuple-element.12), channel_id=1, source_target_pairs={{0,16},{8,24},{16,0},{24,8},{1,17},{9,25},{17,1},{25,9},{2,18},{10... | collective-permute-start | bytes 98312 | tf_op jit(solution)/shard_map/ppermute | solution.py:143
  22.7 0.3 collective-permute-start.3
  23.1 0.0 collective-permute-done.1
  23.1 2.3 %collective-permute-done.2 = bf16[128,128]{1,0:T(8,128)(2,1)S(1)} collective-permute-done((bf16[128,128]{1,0:T(8,128)(2,1)}, bf16[128,128]{1,0:T(8,128)(2,1)S(1)}, u32[]{:S(2)}, u32[]{:S(2)}) %collective-permute-start.2) | collective-permute-done | bytes 32800 | tf_op jit(solution)/shard_map/ppermute | solution.py:143
  25.4 0.9 %collective-permute-done.3 = bf16[128,128]{1,0:T(8,128)(2,1)S(1)} collective-permute-done((bf16[128,128]{1,0:T(8,128)(2,1)}, bf16[128,128]{1,0:T(8,128)(2,1)S(1)}, u32[]{:S(2)}, u32[]{:S(2)}) %collective-permute-start.3) | collective-permute-done | bytes 32800 | tf_op jit(solution)/shard_map/ppermute | solution.py:143
  26.3 0.0 copy-start.2
  26.3 0.9 %fusion.8 = bf16[128,128]{1,0:T(8,128)(2,1)S(1)} fusion(f32[128,128]{1,0:T(8,128)} %get-tuple-element.14, bf16[128,128]{1,0:T(8,128)(2,1)S(1)} %collective-permute-done.1, bf16[128,128]{1,0:T(8,128)(2,1)S(1)} %collective-permute-done.2, bf16[128,128]{1,0:T(8,128)(2,1)S(1)} %collective-permute-done.3, pred[]{:T(512)S(6)} %gt.11, pred[]{:T(512)S(6)} %gt.10, ...), kind=kLoop, calls=%fused_computation.14 | loop fusion | flops 163840 | bytes 196611 | tf_op jit(solution)/shard_map/convert_element_type | solution.py:148
  27.2 1.3 %collective-permute-start.4 = (bf16[128,128]{1,0:T(8,128)(2,1)S(1)}, bf16[128,128]{1,0:T(8,128)(2,1)S(1)}, u32[]{:S(2)}, u32[]{:S(2)}) collective-permute-start(bf16[128,128]{1,0:T(8,128)(2,1)S(1)} %fusion.8), channel_id=1, source_target_pairs={{1,0},{2,1},{3,2},{4,3},{5,4},{6,5},{7,6},{9,8},{10,9},{11,10},{12... | collective-permute-start | bytes 98312 | tf_op jit(solution)/shard_map/ppermute | solution.py:17
  28.5 5.0 %collective-permute-done.4 = bf16[128,128]{1,0:T(8,128)(2,1)S(1)} collective-permute-done((bf16[128,128]{1,0:T(8,128)(2,1)S(1)}, bf16[128,128]{1,0:T(8,128)(2,1)S(1)}, u32[]{:S(2)}, u32[]{:S(2)}) %collective-permute-start.4) | collective-permute-done | bytes 32800 | tf_op jit(solution)/shard_map/ppermute | solution.py:17
  33.5 0.0 copy-done.2
  33.5 0.1 fusion.9
  33.6 0.7 %copy.12 = bf16[128,64]{0,1:T(8,128)(2,1)} copy(bf16[128,64]{1,0:T(8,128)(2,1)S(1)} %get-tuple-element.19) | data formatting | bytes 32768
  34.3 0.7 %copy.13 = bf16[128,64]{0,1:T(8,128)(2,1)} copy(bf16[128,64]{1,0:T(8,128)(2,1)S(1)} %get-tuple-element.18) | data formatting | bytes 32768
  (1 shorter events, 0.0 us)
Async XLA Ops:
  0.6 0.8 %copy-start.3 = (bf16[128,64]{0,1:T(8,128)(2,1)S(1)}, bf16[128,64]{0,1:T(8,128)(2,1)}, u32[]{:S(2)}) copy-start(bf16[128,64]{0,1:T(8,128)(2,1)} %param.8) | copy-start | bytes 49156
  8.2 7.1 %copy-start = (bf16[512,128]{1,0:T(8,128)(2,1)}, bf16[512,128]{1,0:T(8,128)(2,1)S(1)}, u32[]{:S(2)}) copy-start(bf16[512,128]{1,0:T(8,128)(2,1)S(1)} %all-gather.own_ref) | copy-start | bytes 393220
  8.2 7.1 %collective-permute-start = (bf16[4,128,128]{2,1,0:T(8,128)(2,1)S(1)}, bf16[4,128,128]{2,1,0:T(8,128)(2,1)S(1)}, u32[]{:S(2)}, u32[]{:S(2)}) collective-permute-start(bf16[4,128,128]{2,1,0:T(8,128)(2,1)S(1)} %bitcast.3), channel_id=1, source_target_pairs={{0,1},{1,2},{2,3},{3,4},{4,5},{5,6},{6,7},{8,9},{9,10},{10,11},{11... | collective-permute-start | bytes 393224 | tf_op jit(solution)/shard_map/ppermute | solution.py:17
  15.3 0.7 %copy-start.1 = (bf16[4,128,128]{2,1,0:T(8,128)(2,1)}, bf16[4,128,128]{2,1,0:T(8,128)(2,1)S(1)}, u32[]{:S(2)}) copy-start(bf16[4,128,128]{2,1,0:T(8,128)(2,1)S(1)} %collective-permute-done) | copy-start | bytes 393220
  21.2 1.9 %collective-permute-start.1 = (bf16[128,128]{1,0:T(8,128)(2,1)}, bf16[128,128]{1,0:T(8,128)(2,1)S(1)}, u32[]{:S(2)}, u32[]{:S(2)}) collective-permute-start(bf16[128,128]{1,0:T(8,128)(2,1)} %get-tuple-element.11), channel_id=1, source_target_pairs={{0,8},{8,0},{16,24},{24,16},{1,9},{9,1},{17,25},{25,17},{2,10},{10... | collective-permute-start | bytes 98312 | tf_op jit(solution)/shard_map/ppermute | solution.py:143
  21.2 4.2 %collective-permute-start.2 = (bf16[128,128]{1,0:T(8,128)(2,1)}, bf16[128,128]{1,0:T(8,128)(2,1)S(1)}, u32[]{:S(2)}, u32[]{:S(2)}) collective-permute-start(bf16[128,128]{1,0:T(8,128)(2,1)} %get-tuple-element.12), channel_id=1, source_target_pairs={{0,16},{8,24},{16,0},{24,8},{1,17},{9,25},{17,1},{25,9},{2,18},{10... | collective-permute-start | bytes 98312 | tf_op jit(solution)/shard_map/ppermute | solution.py:143
  22.7 3.6 %collective-permute-start.3 = (bf16[128,128]{1,0:T(8,128)(2,1)}, bf16[128,128]{1,0:T(8,128)(2,1)S(1)}, u32[]{:S(2)}, u32[]{:S(2)}) collective-permute-start(bf16[128,128]{1,0:T(8,128)(2,1)} %get-tuple-element.13), channel_id=1, source_target_pairs={{0,24},{8,16},{16,8},{24,0},{1,25},{9,17},{17,9},{25,1},{2,26},{10... | collective-permute-start | bytes 98312 | tf_op jit(solution)/shard_map/ppermute | solution.py:143
  26.3 7.2 %copy-start.2 = (f32[128,128]{1,0:T(8,128)S(1)}, f32[128,128]{1,0:T(8,128)}, u32[]{:S(2)}) copy-start(f32[128,128]{1,0:T(8,128)} %get-tuple-element.10) | copy-start | bytes 196612
  27.2 6.3 %collective-permute-start.4 = (bf16[128,128]{1,0:T(8,128)(2,1)S(1)}, bf16[128,128]{1,0:T(8,128)(2,1)S(1)}, u32[]{:S(2)}, u32[]{:S(2)}) collective-permute-start(bf16[128,128]{1,0:T(8,128)(2,1)S(1)} %fusion.8), channel_id=1, source_target_pairs={{1,0},{2,1},{3,2},{4,3},{5,4},{6,5},{7,6},{9,8},{10,9},{11,10},{12... | collective-permute-start | bytes 98312 | tf_op jit(solution)/shard_map/ppermute | solution.py:17

commit v2 on v1

v2 whole, which is shorter than its diff:
```python
import math

import jax
import jax.numpy as jnp
from jax import lax
from jax.experimental import pallas as pl
from jax.experimental.pallas import tpu as pltpu
from jax.sharding import PartitionSpec as P

NT = (((1,), (1,)), ((), ()))
NN = (((1,), (0,)), ((), ()))


def around(x, axis, by):
    count = lax.axis_size(axis)
    return lax.ppermute(x, axis, [(i, (i + by) % count) for i in range(count)])


def exchanged(x, axis, step):
    count = lax.axis_size(axis)
    return lax.ppermute(x, axis, [(i, i ^ step) for i in range(count)])


def dot(a, b, dims):
    return lax.dot_general(a, b, dims, preferred_element_type=jnp.float32)


def half_turn(x, width):
    return jnp.concatenate([x[:, width:], x[:, :width]], 1)


def tile_terms(kv_cols, q_ref, g_ref, log_ref, begin_ref, delta, first, causal, acc_ref, emit):
    lanes, total = kv_cols.shape
    width = lanes // 2
    rows = q_ref.shape[0]
    team = total // rows
    heads = log_ref.shape[0]
    factor = 1.0 / math.sqrt(width)
    spot = lax.axis_index("team")
    kv = kv_cols.T
    low_key = lax.broadcasted_iota(jnp.int32, (total, lanes), 1) < width
    none = jnp.zeros_like(kv)
    small = jnp.asarray(factor, kv.dtype)
    k_low = jnp.where(low_key, kv * small, none)
    v_high = jnp.where(low_key, none, kv)
    key_halves = (k_low, half_turn(k_low, width))
    value_halves = (half_turn(v_high, width), v_high)
    key_flip = kv_cols[:width] * small
    slabs = []
    for step in range(team):
        inside = lax.broadcasted_iota(jnp.int32, (rows, rows), 0)
        slabs.append(inside + (first + (spot ^ step) * rows))
    key_pos = jnp.concatenate(slabs, 0)
    allowed = key_pos >= begin_ref[...]
    if causal:
        allowed &= key_pos <= lax.broadcasted_iota(jnp.int32, (total, rows), 1)
    row_low = lax.broadcasted_iota(jnp.int32, (rows, lanes), 1) < width
    for pair in range(heads // 2):
        span = slice(pair * lanes, (pair + 1) * lanes)
        q_pair = q_ref[:, span]
        g_pair = g_ref[:, span]
        blank = jnp.zeros_like(q_pair)
        stack = jnp.concatenate(
            [
                jnp.where(row_low, q_pair, blank),
                jnp.where(row_low, half_turn(q_pair, width), blank),
                jnp.where(row_low, blank, half_turn(g_pair, width)),
                jnp.where(row_low, blank, g_pair),
            ],
            0,
        )
        probs, grads, flips = [], [], []
        for half in range(2):
            head = 2 * pair + half
            scores = dot(key_halves[half], q_pair, NT)
            shifted = scores - log_ref[head : head + 1, :]
            weights = jnp.exp(jnp.where(allowed, shifted, -jnp.inf))
            prob_grad = dot(value_halves[half], g_pair, NT)
            score_grad = weights * (prob_grad - delta[head : head + 1, :])
            low = score_grad.astype(jnp.bfloat16)
            probs.append(weights.astype(jnp.bfloat16))
            grads.append(low)
            flips.append(dot(key_flip, low, NN))
        term = dot(jnp.concatenate(grads + probs, 1), stack, NN)
        if pair == 0:
            acc_ref[...] = term
        else:
            acc_ref[...] += term
        emit(pair, jnp.concatenate(flips, 0))


def slab_of(acc_ref, step, rows, width):
    part = acc_ref[step * rows : (step + 1) * rows, :].T
    upper = lax.broadcasted_iota(jnp.int32, part.shape, 0) < width
    return part * jnp.where(upper, jnp.float32(1.0 / math.sqrt(width)), jnp.float32(1.0))


def own_body(q_ref, g_ref, o_ref, log_ref, begin_ref, kv_ref, *rest):
    dq_ref, delta_ref, self_ref, *more = rest
    piece_refs, acc_ref = more[:-1], more[-1]
    rows, features = q_ref.shape
    heads = log_ref.shape[0]
    width = features // heads
    prod = g_ref[...].astype(jnp.float32) * o_ref[...].astype(jnp.float32)
    feature = lax.broadcasted_iota(jnp.int32, (heads, features), 1)
    head_of = lax.broadcasted_iota(jnp.int32, (heads, features), 0)
    pick = (feature // width == head_of).astype(jnp.float32)
    delta = lax.dot_general(
        pick, prod, NT, precision=lax.Precision.HIGHEST, preferred_element_type=jnp.float32
    )
    delta_ref[...] = delta

    def emit(pair, flips):
        dq_ref[pair * 2 * width : (pair + 1) * 2 * width, :] = flips

    first = -lax.axis_index("team") * rows
    tile_terms(kv_ref[...], q_ref, g_ref, log_ref, begin_ref, delta, first, True, acc_ref, emit)
    self_ref[...] = slab_of(acc_ref, 0, rows, width)
    for step in range(1, len(piece_refs) + 1):
        piece_refs[step - 1][...] = slab_of(acc_ref, step, rows, width).astype(jnp.bfloat16)


def near_body(team, q_ref, g_ref, log_ref, begin_ref, kv_ref, part_ref, delta_ref, *rest):
    own_refs, more = rest[: team - 1], rest[team - 1 :]
    dq_ref, self_ref = more[:2]
    piece_refs, acc_ref = more[2:-1], more[-1]
    rows, features = q_ref.shape
    width = features // log_ref.shape[0]
    spot = lax.axis_index("team")

    def emit(pair, flips):
        span = slice(pair * 2 * width, (pair + 1) * 2 * width)
        dq_ref[:, span] = (part_ref[span, :] + flips).T.astype(dq_ref.dtype)

    first = -(spot + team) * rows
    tile_terms(
        kv_ref[...], q_ref, g_ref, log_ref, begin_ref, delta_ref[...], first, False, acc_ref, emit
    )
    self_ref[...] = slab_of(acc_ref, 0, rows, width)
    for step in range(1, team):
        mine = slab_of(acc_ref, step, rows, width).astype(jnp.bfloat16)
        later = jnp.full(mine.shape, (spot ^ step) > spot)
        piece_refs[step - 1][...] = jnp.where(later, mine, own_refs[step - 1][...])


def in_vmem(count):
    return [pl.BlockSpec(memory_space=pltpu.VMEM) for _ in range(count)]


def held(*arrays):
    return [pltpu.with_memory_space_constraint(x, pltpu.VMEM) for x in arrays]


def per_device(queries, keys, values, attn_out, out_grad, log_norm, doc_start):
    rows, features = queries.shape
    heads = log_norm.shape[0]
    width = keys.shape[1]
    team = lax.axis_size("team")
    spot = lax.axis_index("team")
    place = lax.axis_index("blk") * team + spot
    begin = (doc_start - place * rows).reshape(1, rows)
    mine = jnp.concatenate([keys.T, values.T], 0)
    own = jnp.concatenate([mine] + [exchanged(mine, "team", k) for k in range(1, team)], 1)
    near = around(own, "blk", 1)

    def shape(*dims, dtype=jnp.float32):
        return pltpu.VMEM(dims, dtype)

    slab = shape(2 * width, rows)
    pieces = [shape(2 * width, rows, dtype=jnp.bfloat16)] * (team - 1)
    acc = pltpu.VMEM((team * rows, 2 * width), jnp.float32)
    part, delta, own_self, *own_pieces = pl.pallas_call(
        own_body,
        out_shape=[shape(features, rows), shape(heads, rows), slab] + pieces,
        in_specs=in_vmem(6),
        out_specs=in_vmem(2 + team),
        scratch_shapes=[acc],
    )(*held(queries, out_grad, attn_out, log_norm, begin, own))

    def body(*refs):
        near_body(team, *refs)

    query_grad, near_self, *sent = pl.pallas_call(
        body,
        out_shape=[shape(rows, features, dtype=jnp.bfloat16), slab] + pieces,
        in_specs=in_vmem(6 + team),
        out_specs=in_vmem(1 + team),
        scratch_shapes=[acc],
    )(*held(queries, out_grad, log_norm, begin, near, part, delta, *own_pieces))
    got = [exchanged(sent[k - 1], "team", k).astype(jnp.float32) for k in range(1, team)]
    nothing = jnp.float32(0.0)
    near_sum, own_sum = near_self, own_self
    for step in range(1, team):
        later = (spot ^ step) > spot
        near_sum = near_sum + jnp.where(later, nothing, got[step - 1])
        own_sum = own_sum + jnp.where(later, got[step - 1], nothing)
    back = around(near_sum.astype(jnp.bfloat16), "blk", -1)
    total = (own_sum + back.astype(jnp.float32)).astype(jnp.bfloat16)
    return (query_grad, total[:width].T, total[width:].T)


def solution(mesh):
    row = P(("blk", "team"), None)
    return jax.shard_map(
        per_device,
        mesh=mesh,
        in_specs=(row, row, row, row, row, P(None, ("blk", "team")), P(("blk", "team"))),
        out_specs=(row, row, row),
        check_vma=False,
    )
```

time: 35.3 us -> 28.4 us (0.80)
  blocking collectives: 6.51 us -> 0 us
  starting transfers between devices: 6.96 us -> 8.4 us
  waiting for transfers between devices: 11.5 us -> 10.3 us
  local copies, waits for them, and re-layouts: 3.09 us -> 2.19 us
  Pallas kernels: 5.26 us -> 5.76 us
    all_gather x1 -> x0, blocking collectives: 6.51 us -> none  [per_device(): own = lax.all_gather(packed, 'team', axis=0, tiled=False)]
    ppermute x5 -> x8, starting transfers between devices: 6.96 us -> 8.4 us  [the longest x6 5 us: exchanged(): return lax.ppermute(x, axis, [(i, i ^ step) for i in range(count)])]
    unnamed x12 -> x15, local copies, waits for them, and re-layouts: 3.01 us -> 1.58 us
    ppermute x5 -> x8, waiting for transfers between devices: 11.5 us -> 10.3 us  [the longest x6 5.79 us: exchanged(): return lax.ppermute(x, axis, [(i, i ^ step) for i in range(count)])]
    convert_element_type x1, other arithmetic: 0.9 us -> 0.03 us  [per_device(): back = around(near_sum.astype(jnp.bfloat16), 'blk', -1)]
    concatenate x1 -> x2, other arithmetic: 0.09 us -> 0.8 us  [the longest x1 0.79 us: per_device(): mine = jnp.concatenate([keys.T, values.T], 0)]
    transpose x0 -> x1, local copies, waits for them, and re-layouts: none -> 0.61 us  [per_device(): return (query_grad, total[:width].T, total[width:].T)]
    pallas_call x1 -> x2, Pallas kernels: 5.26 us -> 5.76 us  [the longest x1 3 us: per_device(): pl.pallas_call(own_body, out_shape=[shape(features, rows), shape(heads, r...]
  transfers between devices with their start and end apart: 5 -> 8, of which waited for: 4 -> 6; matrix products, arithmetic and copies ran while one was open for 0% -> 2% of each run, Pallas kernels for 0% -> 11%
where the time goes in v2:
time: 28.4 us; the launch traced here: 28.2 us
  waiting for transfers between devices  10.3 us (36%)
  starting transfers between devices  8.4 us (30%)
  Pallas kernels  5.76 us (20%)
  local copies, waits for them, and re-layouts  2.19 us (8%)
  other arithmetic  0.87 us (3%)
  between operations  0.72 us (3%)
    ppermute x6, waiting for transfers between devices, exchanged(): return lax.ppermute(x, axis, [(i, i ^ step) for i in range(count)])  5.79 us
    ppermute x6, starting transfers between devices, exchanged(): return lax.ppermute(x, axis, [(i, i ^ step) for i in range(count)])  5 us
    ppermute x2, waiting for transfers between devices, around(): return lax.ppermute(x, axis, [(i, (i + by) % count) for i in range(count)])  4.47 us
    ppermute x2, starting transfers between devices, around(): return lax.ppermute(x, axis, [(i, (i + by) % count) for i in range(count)])  3.4 us
    pallas_call x1, Pallas kernels, per_device(): pl.pallas_call(own_body, out_shape=[shape(features, rows), shape(heads, r...  3 us
    pallas_call x1, Pallas kernels, per_device(): pl.pallas_call(body, out_shape=[shape(rows, features, dtype=jnp.bfloat16)...  2.75 us
    unnamed x15, local copies, waits for them, and re-layouts  1.58 us
    concatenate x1, other arithmetic, per_device(): mine = jnp.concatenate([keys.T, values.T], 0)  0.79 us
  transfers between devices with their start and end apart: 8, of which 6 were waited for; matrix products, arithmetic and copies ran while one was open for 2% of the time, Pallas kernels for 11%

profile of v2, /device:TPU:0, one launch (start us, length us, event | category | flops | bytes accessed | tf_op | source)
XLA Modules:
  0.0 28.2 jit_solution(5376458525348483473)
XLA Ops:
  0.6 0.0 copy-start.4
  0.6 0.0 copy-start.5
  0.7 0.8 %pad_maximum_fusion.1 = bf16[128,128]{1,0:T(8,128)(2,1)S(1)} fusion(bf16[64,128]{1,0:T(8,128)(2,1)} %bitcast.8, bf16[64,128]{1,0:T(8,128)(2,1)} %bitcast.10), kind=kLoop, calls=%fused_computation.16 | loop fusion | flops 65536 | bytes 65536 | tf_op jit(solution)/shard_map/concatenate | solution.py:162
  1.4 0.5 %collective-permute-start = (bf16[128,128]{1,0:T(8,128)(2,1)S(1)}, bf16[128,128]{1,0:T(8,128)(2,1)S(1)}, u32[]{:S(2)}, u32[]{:S(2)}) collective-permute-start(bf16[128,128]{1,0:T(8,128)(2,1)S(1)} %pad_maximum_fusion.1), channel_id=1, source_target_pairs={{0,8},{8,0},{16,24},{24,16},{1,9},{9,1},{17,25},{25,17},{2,10},{10... | collective-permute-start | bytes 98312 | tf_op jit(solution)/shard_map/ppermute | solution.py:21
  1.9 2.5 %collective-permute-start.1 = (bf16[128,128]{1,0:T(8,128)(2,1)S(1)}, bf16[128,128]{1,0:T(8,128)(2,1)S(1)}, u32[]{:S(2)}, u32[]{:S(2)}) collective-permute-start(bf16[128,128]{1,0:T(8,128)(2,1)S(1)} %pad_maximum_fusion.1), channel_id=1, source_target_pairs={{0,16},{8,24},{16,0},{24,8},{1,17},{9,25},{17,1},{25,9},{2,18},{10... | collective-permute-start | bytes 98312 | tf_op jit(solution)/shard_map/ppermute | solution.py:21
  4.4 0.1 collective-permute-start.2
  4.5 0.0 copy-start.3
  4.5 0.0 copy-start.6
  4.5 0.0 copy-start
  4.5 0.0 copy-start.1
  4.5 0.0 collective-permute-done
  4.5 1.9 %collective-permute-done.1 = bf16[128,128]{1,0:T(8,128)(2,1)S(1)} collective-permute-done((bf16[128,128]{1,0:T(8,128)(2,1)S(1)}, bf16[128,128]{1,0:T(8,128)(2,1)S(1)}, u32[]{:S(2)}, u32[]{:S(2)}) %collective-permute-start.1) | collective-permute-done | bytes 32800 | tf_op jit(solution)/shard_map/ppermute | solution.py:21
  6.5 1.3 %collective-permute-done.2 = bf16[128,128]{1,0:T(8,128)(2,1)S(1)} collective-permute-done((bf16[128,128]{1,0:T(8,128)(2,1)S(1)}, bf16[128,128]{1,0:T(8,128)(2,1)S(1)}, u32[]{:S(2)}, u32[]{:S(2)}) %collective-permute-start.2) | collective-permute-done | bytes 32800 | tf_op jit(solution)/shard_map/ppermute | solution.py:21
  7.7 0.0 copy-done.4
  7.7 0.0 copy-done.5
  7.8 1.6 %collective-permute-start.3 = (bf16[128,512]{1,0:T(8,128)(2,1)S(1)}, bf16[128,512]{1,0:T(8,128)(2,1)S(1)}, u32[]{:S(2)}, u32[]{:S(2)}) collective-permute-start(bf16[128,512]{1,0:T(8,128)(2,1)S(1)} %pad_maximum_fusion.kv_ref), channel_id=1, source_target_pairs={{0,1},{1,2},{2,3},{3,4},{4,5},{5,6},{6,7},{7,0},{8,9},{9,10},{10,1... | collective-permute-start | bytes 393224 | tf_op jit(solution)/shard_map/ppermute | solution.py:16
  9.3 0.0 copy-done.6
  9.4 0.0 copy-done.3
  9.4 0.0 copy-done
  9.4 0.0 copy-done.1
  9.4 0.0 copy-start.2
  9.4 0.9 %copy-done.2 = bf16[128,512]{1,0:T(8,128)(2,1)S(1)} copy-done((bf16[128,512]{1,0:T(8,128)(2,1)S(1)}, bf16[128,512]{1,0:T(8,128)(2,1)}, u32[]{:S(2)}) %copy-start.2) | copy-done | bytes 131096
  10.3 3.0 %shard_map.94 = (f32[512,128]{1,0:T(8,128)S(1)}, f32[8,128]{1,0:T(8,128)S(1)}, f32[128,128]{1,0:T(8,128)S(1)}, bf16[128,128]{1,0:T(8,128)(2,1)S(1)}, bf16[128,12...) custom-call(bf16[128,512]{1,0:T(8,128)(2,1)S(1)} %copy-done, bf16[128,512]{1,0:T(8,128)(2,1)S(1)} %copy-done.1, ...), custom_call_target="tpu_custom_call" | custom-call | tf_op jit(solution)/shard_map/pallas_call | solution.py:172
  13.3 3.0 %collective-permute-done.3.refs_4_ = bf16[128,512]{1,0:T(8,128)(2,1)S(1)} collective-permute-done((bf16[128,512]{1,0:T(8,128)(2,1)S(1)}, bf16[128,512]{1,0:T(8,128)(2,1)S(1)}, u32[]{:S(2)}, u32[]{:S(2)}) %collective-permute-start.3) | collective-permute-done | bytes 131104 | tf_op jit(solution)/shard_map/ppermute | solution.py:16
  16.3 2.8 %shard_map.95 = (bf16[128,512]{1,0:T(8,128)(2,1)S(1)}, f32[128,128]{1,0:T(8,128)S(1)}, bf16[128,128]{1,0:T(8,128)(2,1)S(1)}, bf16[128,128]{1,0:T(8,128)(2,1)S(1)}, bf16[128,128]{1,0:T(8,128)(2,1)S(1)}) custom-call(bf16[128,512]{1,0:T(8,128)(2,1)S(1)} %copy-done, bf16[128,512]{1,0:T(8,128)(2,1)S(1)} %copy-done.1, f32[8,128]{1,0:T(8,128)S(1)} %copy-done.3, ...), custom_call_target="tpu_custom_call" | custom-call | tf_op jit(solution)/shard_map/pallas_call | solution.py:183
  19.0 0.1 collective-permute-start.4
  19.1 0.9 %collective-permute-start.5 = (bf16[128,128]{1,0:T(8,128)(2,1)S(1)}, bf16[128,128]{1,0:T(8,128)(2,1)S(1)}, u32[]{:S(2)}, u32[]{:S(2)}) collective-permute-start(bf16[128,128]{1,0:T(8,128)(2,1)S(1)} %get-tuple-element.22), channel_id=1, source_target_pairs={{0,16},{8,24},{16,0},{24,8},{1,17},{9,25},{17,1},{25,9},{2,18},{10... | collective-permute-start | bytes 98312 | tf_op jit(solution)/shard_map/ppermute | solution.py:21
  20.0 0.9 %collective-permute-start.6 = (bf16[128,128]{1,0:T(8,128)(2,1)S(1)}, bf16[128,128]{1,0:T(8,128)(2,1)S(1)}, u32[]{:S(2)}, u32[]{:S(2)}) collective-permute-start(bf16[128,128]{1,0:T(8,128)(2,1)S(1)} %get-tuple-element.23), channel_id=1, source_target_pairs={{0,24},{8,16},{16,8},{24,0},{1,25},{9,17},{17,9},{25,1},{2,26},{10... | collective-permute-start | bytes 98312 | tf_op jit(solution)/shard_map/ppermute | solution.py:21
  21.0 0.0 collective-permute-done.4
  21.0 2.2 %collective-permute-done.5 = bf16[128,128]{1,0:T(8,128)(2,1)S(1)} collective-permute-done((bf16[128,128]{1,0:T(8,128)(2,1)S(1)}, bf16[128,128]{1,0:T(8,128)(2,1)S(1)}, u32[]{:S(2)}, u32[]{:S(2)}) %collective-permute-start.5) | collective-permute-done | bytes 32800 | tf_op jit(solution)/shard_map/ppermute | solution.py:21
  23.2 0.4 %collective-permute-done.6 = bf16[128,128]{1,0:T(8,128)(2,1)S(1)} collective-permute-done((bf16[128,128]{1,0:T(8,128)(2,1)S(1)}, bf16[128,128]{1,0:T(8,128)(2,1)S(1)}, u32[]{:S(2)}, u32[]{:S(2)}) %collective-permute-start.6) | collective-permute-done | bytes 32800 | tf_op jit(solution)/shard_map/ppermute | solution.py:21
  23.6 1.8 %collective-permute-start.7 = (bf16[128,128]{1,0:T(8,128)(2,1)S(1)}, bf16[128,128]{1,0:T(8,128)(2,1)S(1)}, u32[]{:S(2)}, u32[]{:S(2)}) collective-permute-start(bf16[128,128]{1,0:T(8,128)(2,1)S(1)} %fusion.8), channel_id=1, source_target_pairs={{0,7},{1,0},{2,1},{3,2},{4,3},{5,4},{6,5},{7,6},{8,15},{9,8},{10,9... | collective-permute-start | bytes 98312 | tf_op jit(solution)/shard_map/ppermute | solution.py:16
  25.4 0.7 %copy.10 = bf16[128,512]{1,0:T(8,128)(2,1)} copy(bf16[128,512]{1,0:T(8,128)(2,1)S(1)} %get-tuple-element.27) | data formatting | bytes 262144
  26.1 1.5 %collective-permute-done.7 = bf16[128,128]{1,0:T(8,128)(2,1)S(1)} collective-permute-done((bf16[128,128]{1,0:T(8,128)(2,1)S(1)}, bf16[128,128]{1,0:T(8,128)(2,1)S(1)}, u32[]{:S(2)}, u32[]{:S(2)}) %collective-permute-start.7) | collective-permute-done | bytes 32800 | tf_op jit(solution)/shard_map/ppermute | solution.py:16
  27.6 0.6 %slice_bitcast_fusion = (bf16[128,64]{0,1:T(8,128)(2,1)}, bf16[128,64]{0,1:T(8,128)(2,1)}) fusion(bf16[128,128]{1,0:T(8,128)(2,1)S(1)} %fusion.4), kind=kLoop, calls=%fused_computation.17 | loop fusion | bytes 65536 | tf_op jit(solution)/shard_map/transpose | solution.py:199
  (4 shorter events, 0.1 us)
Async XLA Ops:
  0.6 7.1 %copy-start.4 = (bf16[128,64]{0,1:T(8,128)(2,1)S(1)}, bf16[128,64]{0,1:T(8,128)(2,1)}, u32[]{:S(2)}) copy-start(bf16[128,64]{0,1:T(8,128)(2,1)} %param.9) | copy-start | bytes 49156
  0.6 7.1 %copy-start.5 = (bf16[128,64]{0,1:T(8,128)(2,1)S(1)}, bf16[128,64]{0,1:T(8,128)(2,1)}, u32[]{:S(2)}) copy-start(bf16[128,64]{0,1:T(8,128)(2,1)} %param.8) | copy-start | bytes 49156
  1.4 3.1 %collective-permute-start = (bf16[128,128]{1,0:T(8,128)(2,1)S(1)}, bf16[128,128]{1,0:T(8,128)(2,1)S(1)}, u32[]{:S(2)}, u32[]{:S(2)}) collective-permute-start(bf16[128,128]{1,0:T(8,128)(2,1)S(1)} %pad_maximum_fusion.1), channel_id=1, source_target_pairs={{0,8},{8,0},{16,24},{24,16},{1,9},{9,1},{17,25},{25,17},{2,10},{10... | collective-permute-start | bytes 98312 | tf_op jit(solution)/shard_map/ppermute | solution.py:21
  1.9 4.5 %collective-permute-start.1 = (bf16[128,128]{1,0:T(8,128)(2,1)S(1)}, bf16[128,128]{1,0:T(8,128)(2,1)S(1)}, u32[]{:S(2)}, u32[]{:S(2)}) collective-permute-start(bf16[128,128]{1,0:T(8,128)(2,1)S(1)} %pad_maximum_fusion.1), channel_id=1, source_target_pairs={{0,16},{8,24},{16,0},{24,8},{1,17},{9,25},{17,1},{25,9},{2,18},{10... | collective-permute-start | bytes 98312 | tf_op jit(solution)/shard_map/ppermute | solution.py:21
  4.4 3.3 %collective-permute-start.2 = (bf16[128,128]{1,0:T(8,128)(2,1)S(1)}, bf16[128,128]{1,0:T(8,128)(2,1)S(1)}, u32[]{:S(2)}, u32[]{:S(2)}) collective-permute-start(bf16[128,128]{1,0:T(8,128)(2,1)S(1)} %pad_maximum_fusion.1), channel_id=1, source_target_pairs={{0,24},{8,16},{16,8},{24,0},{1,25},{9,17},{17,9},{25,1},{2,26},{10... | collective-permute-start | bytes 98312 | tf_op jit(solution)/shard_map/ppermute | solution.py:21
  4.5 4.8 %copy-start.3 = (f32[8,128]{1,0:T(8,128)S(1)}, f32[8,128]{1,0:T(8,128)}, u32[]{:S(2)}) copy-start(f32[8,128]{1,0:T(8,128)} %refs_2_.1) | copy-start | bytes 12292
  4.5 4.8 %copy-start.6 = (s32[128]{0:T(128)S(1)}, s32[128]{0:T(128)}, u32[]{:S(2)}) copy-start(s32[128]{0:T(128)} %param.13) | copy-start | bytes 1540
  4.5 4.8 %copy-start = (bf16[128,512]{1,0:T(8,128)(2,1)S(1)}, bf16[128,512]{1,0:T(8,128)(2,1)}, u32[]{:S(2)}) copy-start(bf16[128,512]{1,0:T(8,128)(2,1)} %refs_0_.1) | copy-start | bytes 393220
  4.5 4.8 %copy-start.1 = (bf16[128,512]{1,0:T(8,128)(2,1)S(1)}, bf16[128,512]{1,0:T(8,128)(2,1)}, u32[]{:S(2)}) copy-start(bf16[128,512]{1,0:T(8,128)(2,1)} %refs_1_.1) | copy-start | bytes 393220
  7.8 8.5 %collective-permute-start.3 = (bf16[128,512]{1,0:T(8,128)(2,1)S(1)}, bf16[128,512]{1,0:T(8,128)(2,1)S(1)}, u32[]{:S(2)}, u32[]{:S(2)}) collective-permute-start(bf16[128,512]{1,0:T(8,128)(2,1)S(1)} %pad_maximum_fusion.kv_ref), channel_id=1, source_target_pairs={{0,1},{1,2},{2,3},{3,4},{4,5},{5,6},{6,7},{7,0},{8,9},{9,10},{10,1... | collective-permute-start | bytes 393224 | tf_op jit(solution)/shard_map/ppermute | solution.py:16
  9.4 0.9 %copy-start.2 = (bf16[128,512]{1,0:T(8,128)(2,1)S(1)}, bf16[128,512]{1,0:T(8,128)(2,1)}, u32[]{:S(2)}) copy-start(bf16[128,512]{1,0:T(8,128)(2,1)} %o_ref.1) | copy-start | bytes 393220
  19.0 1.9 %collective-permute-start.4 = (bf16[128,128]{1,0:T(8,128)(2,1)S(1)}, bf16[128,128]{1,0:T(8,128)(2,1)S(1)}, u32[]{:S(2)}, u32[]{:S(2)}) collective-permute-start(bf16[128,128]{1,0:T(8,128)(2,1)S(1)} %get-tuple-element.21), channel_id=1, source_target_pairs={{0,8},{8,0},{16,24},{24,16},{1,9},{9,1},{17,25},{25,17},{2,10},{10... | collective-permute-start | bytes 98312 | tf_op jit(solution)/shard_map/ppermute | solution.py:21
  19.1 4.1 %collective-permute-start.5 = (bf16[128,128]{1,0:T(8,128)(2,1)S(1)}, bf16[128,128]{1,0:T(8,128)(2,1)S(1)}, u32[]{:S(2)}, u32[]{:S(2)}) collective-permute-start(bf16[128,128]{1,0:T(8,128)(2,1)S(1)} %get-tuple-element.22), channel_id=1, source_target_pairs={{0,16},{8,24},{16,0},{24,8},{1,17},{9,25},{17,1},{25,9},{2,18},{10... | collective-permute-start | bytes 98312 | tf_op jit(solution)/shard_map/ppermute | solution.py:21
  20.0 3.5 %collective-permute-start.6 = (bf16[128,128]{1,0:T(8,128)(2,1)S(1)}, bf16[128,128]{1,0:T(8,128)(2,1)S(1)}, u32[]{:S(2)}, u32[]{:S(2)}) collective-permute-start(bf16[128,128]{1,0:T(8,128)(2,1)S(1)} %get-tuple-element.23), channel_id=1, source_target_pairs={{0,24},{8,16},{16,8},{24,0},{1,25},{9,17},{17,9},{25,1},{2,26},{10... | collective-permute-start | bytes 98312 | tf_op jit(solution)/shard_map/ppermute | solution.py:21
  23.6 4.0 %collective-permute-start.7 = (bf16[128,128]{1,0:T(8,128)(2,1)S(1)}, bf16[128,128]{1,0:T(8,128)(2,1)S(1)}, u32[]{:S(2)}, u32[]{:S(2)}) collective-permute-start(bf16[128,128]{1,0:T(8,128)(2,1)S(1)} %fusion.8), channel_id=1, source_target_pairs={{0,7},{1,0},{2,1},{3,2},{4,3},{5,4},{6,5},{7,6},{8,15},{9,8},{10,9... | collective-permute-start | bytes 98312 | tf_op jit(solution)/shard_map/ppermute | solution.py:16

commit v3 on v2

v3 whole, which is shorter than its diff:
```python
import functools
import math

import jax
import jax.numpy as jnp
from jax import lax
from jax.experimental import pallas as pl
from jax.experimental.pallas import tpu as pltpu
from jax.sharding import PartitionSpec as P


NT = (((1,), (1,)), ((), ()))
NN = (((1,), (0,)), ((), ()))
FRONT = 6


def around(x, axis, by):
    count = lax.axis_size(axis)
    return lax.ppermute(x, axis, [(i, (i + by) % count) for i in range(count)])


def exchanged(x, axis, step):
    count = lax.axis_size(axis)
    return lax.ppermute(x, axis, [(i, i ^ step) for i in range(count)])


def dot(a, b, dims):
    return lax.dot_general(a, b, dims, preferred_element_type=jnp.float32)


def half_turn(x, width):
    return jnp.concatenate([x[:, width:], x[:, :width]], 1)


def front_body(
    q_in, g_in, o_ref, log_in, begin_in, q_ref, g_ref, stack_ref, delta_ref, log_ref, begin_ref
):
    rows, features = q_in.shape
    heads = log_in.shape[0]
    width = features // heads
    lanes = 2 * width
    q_ref[...] = q_in[...]
    g_ref[...] = g_in[...]
    log_ref[...] = log_in[...]
    place = lax.axis_index("blk") * lax.axis_size("team") + lax.axis_index("team")
    begin_ref[...] = begin_in[...] - place * rows
    prod = g_in[...].astype(jnp.float32) * o_ref[...].astype(jnp.float32)
    feature = lax.broadcasted_iota(jnp.int32, (heads, features), 1)
    head_of = lax.broadcasted_iota(jnp.int32, (heads, features), 0)
    pick = (feature // width == head_of).astype(jnp.float32)
    delta_ref[...] = lax.dot_general(
        pick, prod, NT, precision=lax.Precision.HIGHEST, preferred_element_type=jnp.float32
    )
    row_low = lax.broadcasted_iota(jnp.int32, (rows, lanes), 1) < width
    for pair in range(heads // 2):
        span = slice(pair * lanes, (pair + 1) * lanes)
        q_pair = q_in[:, span]
        g_pair = g_in[:, span]
        blank = jnp.zeros_like(q_pair)
        parts = (
            jnp.where(row_low, q_pair, blank),
            jnp.where(row_low, half_turn(q_pair, width), blank),
            jnp.where(row_low, blank, half_turn(g_pair, width)),
            jnp.where(row_low, blank, g_pair),
        )
        for n, part in enumerate(parts):
            at = (4 * pair + n) * rows
            stack_ref[at : at + rows, :] = part


def tile_terms(slab_refs, bases, front, grad_ref, acc_ref):
    q_ref, g_ref, stack_ref, delta_ref, log_ref, begin_ref = front
    lanes = slab_refs[0].shape[0]
    width = lanes // 2
    rows = q_ref.shape[0]
    total = len(slab_refs) * rows
    heads = log_ref.shape[0]
    kv = jnp.concatenate([ref[...] for ref in slab_refs], 1).T
    low_key = lax.broadcasted_iota(jnp.int32, (total, lanes), 1) < width
    none = jnp.zeros_like(kv)
    k_low = jnp.where(low_key, kv * jnp.asarray(1.0 / math.sqrt(width), kv.dtype), none)
    v_high = jnp.where(low_key, none, kv)
    key_halves = (k_low, half_turn(k_low, width))
    value_halves = (half_turn(v_high, width), v_high)
    inside = lax.broadcasted_iota(jnp.int32, (rows, rows), 0)
    key_pos = jnp.concatenate([inside + base for base in bases], 0)
    row_pos = lax.broadcasted_iota(jnp.int32, (total, rows), 1)
    allowed = (key_pos >= begin_ref[...]) & (key_pos <= row_pos)
    for pair in range(heads // 2):
        span = slice(pair * lanes, (pair + 1) * lanes)
        q_pair = q_ref[:, span]
        g_pair = g_ref[:, span]
        stack = stack_ref[4 * pair * rows : 4 * (pair + 1) * rows, :]
        probs, grads = [], []
        for half in range(2):
            head = 2 * pair + half
            scores = dot(key_halves[half], q_pair, NT)
            shifted = scores - log_ref[head : head + 1, :]
            weights = jnp.exp(jnp.where(allowed, shifted, -jnp.inf))
            prob_grad = dot(value_halves[half], g_pair, NT)
            score_grad = weights * (prob_grad - delta_ref[head : head + 1, :])
            low = score_grad.astype(jnp.bfloat16)
            grad_ref[head * total : (head + 1) * total, :] = low
            probs.append(weights.astype(jnp.bfloat16))
            grads.append(low)
        term = dot(jnp.concatenate(grads + probs, 1), stack, NN)
        if pair == 0:
            acc_ref[...] = term
        else:
            acc_ref[...] += term


def slab_of(acc_ref, step, rows, width):
    part = acc_ref[step * rows : (step + 1) * rows, :].T
    upper = lax.broadcasted_iota(jnp.int32, part.shape, 0) < width
    return part * jnp.where(upper, jnp.float32(1.0 / math.sqrt(width)), jnp.float32(1.0))


def own_body(team, *refs):
    front, slab_refs = refs[:FRONT], refs[FRONT : FRONT + team + 1]
    grad_ref, own_ref, near_ref, *piece_refs, acc_ref = refs[FRONT + team + 1 :]
    rows, features = front[0].shape
    width = features // front[4].shape[0]
    spot = lax.axis_index("team")
    bases = [((spot ^ step) - spot) * rows for step in range(team)] + [-team * rows]
    tile_terms(slab_refs, bases, front, grad_ref, acc_ref)
    own_ref[...] = slab_of(acc_ref, 0, rows, width)
    near_ref[...] = slab_of(acc_ref, team, rows, width)
    for step in range(1, team):
        piece_refs[step - 1][...] = slab_of(acc_ref, step, rows, width).astype(jnp.bfloat16)


def near_body(team, *refs):
    front, slab_refs = refs[:FRONT], refs[FRONT : FRONT + team - 1]
    own_refs = refs[FRONT + team - 1 : FRONT + 2 * team - 2]
    grad_ref, *piece_refs, acc_ref = refs[FRONT + 2 * team - 2 :]
    rows, features = front[0].shape
    width = features // front[4].shape[0]
    spot = lax.axis_index("team")
    has_past = lax.axis_index("blk") > 0

    @pl.when(has_past)
    def _():
        bases = [((spot ^ step) - spot - team) * rows for step in range(1, team)]
        tile_terms(slab_refs, bases, front, grad_ref, acc_ref)
        for step in range(1, team):
            mine = slab_of(acc_ref, step - 1, rows, width).astype(jnp.bfloat16)
            later = jnp.full(mine.shape, (spot ^ step) > spot)
            piece_refs[step - 1][...] = jnp.where(later, mine, own_refs[step - 1][...])

    @pl.when(jnp.logical_not(has_past))
    def _():
        grad_ref[...] = jnp.zeros_like(grad_ref)
        for step in range(1, team):
            kept = own_refs[step - 1][...]
            later = jnp.full(kept.shape, (spot ^ step) > spot)
            piece_refs[step - 1][...] = jnp.where(later, jnp.zeros_like(kept), kept)


def query_body(team, own_grad_ref, near_grad_ref, *refs):
    slab_refs, out_ref = refs[:-1], refs[-1]
    lanes, _ = slab_refs[0].shape
    width = lanes // 2
    heads = out_ref.shape[1] // width
    small = jnp.asarray(1.0 / math.sqrt(width), slab_refs[0].dtype)
    own_keys = jnp.concatenate([ref[:width, :] for ref in slab_refs[: team + 1]], 1) * small
    near_keys = jnp.concatenate([ref[:width, :] for ref in slab_refs[team + 1 :]], 1) * small

    def flipped(head):
        terms = 0.0
        for keys, grads in ((own_keys, own_grad_ref), (near_keys, near_grad_ref)):
            total = keys.shape[1]
            terms += dot(keys, grads[head * total : (head + 1) * total, :], NN)
        return terms

    for pair in range(heads // 2):
        both = jnp.concatenate([flipped(2 * pair), flipped(2 * pair + 1)], 0)
        out_ref[:, pair * lanes : (pair + 1) * lanes] = both.T.astype(out_ref.dtype)


def in_vmem(count):
    return [pl.BlockSpec(memory_space=pltpu.VMEM) for _ in range(count)]


def held(*arrays, space=pltpu.VMEM):
    return [pltpu.with_memory_space_constraint(x, space) for x in arrays]


def grant(slabs, rows, lanes):
    return pltpu.CompilerParams(vmem_limit_bytes=(8 << 20) + 96 * slabs * rows * lanes)


def per_device(queries, keys, values, attn_out, out_grad, log_norm, doc_start):
    rows, features = queries.shape
    heads = log_norm.shape[0]
    width = keys.shape[1]
    team = lax.axis_size("team")
    spot = lax.axis_index("team")
    mine = jnp.concatenate([keys.T, values.T], 0)
    past = around(mine, "blk", 1)
    own = [exchanged(mine, "team", k) for k in range(1, team)]
    near = [exchanged(past, "team", k) for k in range(1, team)]

    def low(*dims):
        return pltpu.VMEM(dims, jnp.bfloat16)

    def full(*dims):
        return pltpu.VMEM(dims, jnp.float32)

    pieces = [low(2 * width, rows)] * (team - 1)
    slab = full(2 * width, rows)
    params = grant(team + 1, rows, 2 * width)
    front = pl.pallas_call(
        front_body,
        out_shape=[
            low(rows, features),
            low(rows, features),
            low(2 * heads * rows, 2 * width),
            full(heads, rows),
            full(heads, rows),
            pltpu.VMEM((1, rows), jnp.int32),
        ],
        in_specs=in_vmem(5),
        out_specs=in_vmem(FRONT),
        compiler_params=params,
    )(*held(queries, out_grad, attn_out, log_norm, doc_start.reshape(1, rows), space=pltpu.HBM))
    own_grads, own_sum, near_sum, *own_pieces = pl.pallas_call(
        functools.partial(own_body, team),
        out_shape=[low(heads * (team + 1) * rows, rows), slab, slab] + pieces,
        in_specs=in_vmem(FRONT + team + 1),
        out_specs=in_vmem(2 + team),
        compiler_params=params,
        scratch_shapes=[full((team + 1) * rows, 2 * width)],
    )(*held(*front, mine, *own, past))
    near_grads, *sent = pl.pallas_call(
        functools.partial(near_body, team),
        out_shape=[low(heads * (team - 1) * rows, rows)] + pieces,
        in_specs=in_vmem(FRONT + 2 * team - 2),
        out_specs=in_vmem(team),
        compiler_params=params,
        scratch_shapes=[full((team - 1) * rows, 2 * width)],
    )(*held(*front, *near, *own_pieces))
    query_grad = pl.pallas_call(
        functools.partial(query_body, team),
        out_shape=jax.ShapeDtypeStruct((rows, features), jnp.bfloat16),
        in_specs=in_vmem(2 + 2 * team),
        out_specs=in_vmem(1)[0],
        compiler_params=params,
    )(*held(own_grads, near_grads, mine, *own, past, *near))
    got = [exchanged(sent[k - 1], "team", k).astype(jnp.float32) for k in range(1, team)]
    nothing = jnp.float32(0.0)
    for step in range(1, team):
        later = (spot ^ step) > spot
        near_sum = near_sum + jnp.where(later, nothing, got[step - 1])
        own_sum = own_sum + jnp.where(later, got[step - 1], nothing)
    back = around(near_sum.astype(jnp.bfloat16), "blk", -1)
    total = (own_sum + back.astype(jnp.float32)).astype(jnp.bfloat16)
    return (query_grad, total[:width].T, total[width:].T)


def solution(mesh):
    row = P(("blk", "team"), None)

    return jax.shard_map(
        per_device,
        mesh=mesh,
        in_specs=(row, row, row, row, row, P(None, ("blk", "team")), P(("blk", "team"))),
        out_specs=(row, row, row),
        check_vma=False,
    )
```

time: 28.4 us -> 26.5 us (0.933)
  starting transfers between devices: 8.4 us -> 12.1 us
  waiting for transfers between devices: 10.3 us -> 7.02 us
  local copies, waits for them, and re-layouts: 2.19 us -> 0.61 us
  Pallas kernels: 5.76 us -> 5.01 us
    ppermute x2, starting transfers between devices: 3.4 us -> 6.35 us  [around(): return lax.ppermute(x, axis, [(i, (i + by) % count) for i in range(count)])]
    ppermute x6 -> x9, waiting for transfers between devices: 5.79 us -> 3.58 us  [exchanged(): return lax.ppermute(x, axis, [(i, i ^ step) for i in range(count)])]
    unnamed x15 -> x0, local copies, waits for them, and re-layouts: 1.58 us -> none
    ppermute x2, waiting for transfers between devices: 4.47 us -> 3.45 us  [around(): return lax.ppermute(x, axis, [(i, (i + by) % count) for i in range(count)])]
    pallas_call x2 -> x4, Pallas kernels: 5.76 us -> 5.01 us  [the longest x1 2.24 us: per_device(): pl.pallas_call(functools.partial(own_body, team), out_shape=[low(heads *...]
    ppermute x6 -> x9, starting transfers between devices: 5 us -> 5.73 us  [exchanged(): return lax.ppermute(x, axis, [(i, i ^ step) for i in range(count)])]
  transfers between devices with their start and end apart: 8 -> 11, of which waited for: 6 -> 4; matrix products, arithmetic and copies ran while one was open for 2% -> 0% of each run, Pallas kernels for 11% -> 19%
where the time goes in v3:
time: 26.5 us; the launch traced here: 26.2 us
  starting transfers between devices  12.1 us (46%)
  waiting for transfers between devices  7.02 us (26%)
  Pallas kernels  5.01 us (19%)
  other arithmetic  0.8 us (3%)
  between operations  0.69 us (3%)
  local copies, waits for them, and re-layouts  0.61 us (2%)
    ppermute x2, starting transfers between devices, around(): return lax.ppermute(x, axis, [(i, (i + by) % count) for i in range(count)])  6.35 us
    ppermute x9, starting transfers between devices, exchanged(): return lax.ppermute(x, axis, [(i, i ^ step) for i in range(count)])  5.73 us
    ppermute x9, waiting for transfers between devices, exchanged(): return lax.ppermute(x, axis, [(i, i ^ step) for i in range(count)])  3.58 us
    ppermute x2, waiting for transfers between devices, around(): return lax.ppermute(x, axis, [(i, (i + by) % count) for i in range(count)])  3.45 us
    pallas_call x1, Pallas kernels, per_device(): pl.pallas_call(functools.partial(own_body, team), out_shape=[low(heads *...  2.24 us
    pallas_call x1, Pallas kernels, per_device(): pl.pallas_call(front_body, out_shape=[low(rows, features), low(rows, feat...  1.41 us
    pallas_call x1, Pallas kernels, per_device(): pl.pallas_call(functools.partial(query_body, team), out_shape=jax.ShapeDt...  1.22 us
    concatenate x1, other arithmetic, per_device(): mine = jnp.concatenate([keys.T, values.T], 0)  0.74 us
  transfers between devices with their start and end apart: 11, of which 4 were waited for; matrix products, arithmetic and copies ran while one was open for 0% of the time, Pallas kernels for 19%

profile of v3, /device:TPU:0, one launch (start us, length us, event | category | flops | bytes accessed | tf_op | source)
XLA Modules:
  0.0 26.2 jit_solution(15353833154609634556)
XLA Ops:
  0.6 0.7 %pad_maximum_fusion.refs_6_.refs_0_ = bf16[128,128]{1,0:T(8,128)(2,1)S(1)} fusion(bf16[64,128]{1,0:T(8,128)(2,1)} %bitcast.7, bf16[64,128]{1,0:T(8,128)(2,1)} %bitcast.8), kind=kLoop, calls=%fused_computation.15 | loop fusion | flops 65536 | bytes 65536 | tf_op jit(solution)/shard_map/concatenate | solution.py:199
  1.4 3.0 %collective-permute-start.3 = (bf16[128,128]{1,0:T(8,128)(2,1)S(1)}, bf16[128,128]{1,0:T(8,128)(2,1)S(1)}, u32[]{:S(2)}, u32[]{:S(2)}) collective-permute-start(bf16[128,128]{1,0:T(8,128)(2,1)S(1)} %pad_maximum_fusion.refs_6_.refs_0_), channel_id=1, source_target_pairs={{0,1},{1,2},{2,3},{3,4},{4,5},{5,6},{6,7},{7,0},{8,9},{9,10},{10,1... | collective-permute-start | bytes 98312 | tf_op jit(solution)/shard_map/ppermute | solution.py:19
  4.4 0.0 collective-permute-start
  4.4 1.5 %collective-permute-start.1 = (bf16[128,128]{1,0:T(8,128)(2,1)S(1)}, bf16[128,128]{1,0:T(8,128)(2,1)S(1)}, u32[]{:S(2)}, u32[]{:S(2)}) collective-permute-start(bf16[128,128]{1,0:T(8,128)(2,1)S(1)} %pad_maximum_fusion.refs_6_.refs_0_), channel_id=1, source_target_pairs={{0,16},{8,24},{16,0},{24,8},{1,17},{9,25},{17,1},{25,9},{2,18},{10... | collective-permute-start | bytes 98312 | tf_op jit(solution)/shard_map/ppermute | solution.py:24
  5.9 0.4 %collective-permute-start.2 = (bf16[128,128]{1,0:T(8,128)(2,1)S(1)}, bf16[128,128]{1,0:T(8,128)(2,1)S(1)}, u32[]{:S(2)}, u32[]{:S(2)}) collective-permute-start(bf16[128,128]{1,0:T(8,128)(2,1)S(1)} %pad_maximum_fusion.refs_6_.refs_0_), channel_id=1, source_target_pairs={{0,24},{8,16},{16,8},{24,0},{1,25},{9,17},{17,9},{25,1},{2,26},{10... | collective-permute-start | bytes 98312 | tf_op jit(solution)/shard_map/ppermute | solution.py:24
  6.2 3.1 %collective-permute-done.3.refs_10_.refs_4_ = bf16[128,128]{1,0:T(8,128)(2,1)S(1)} collective-permute-done((bf16[128,128]{1,0:T(8,128)(2,1)S(1)}, bf16[128,128]{1,0:T(8,128)(2,1)S(1)}, u32[]{:S(2)}, u32[]{:S(2)}) %collective-permute-start.3) | collective-permute-done | bytes 32800 | tf_op jit(solution)/shard_map/ppermute | solution.py:19
  9.3 0.0 collective-permute-start.4
  9.3 1.7 %collective-permute-start.5 = (bf16[128,128]{1,0:T(8,128)(2,1)S(1)}, bf16[128,128]{1,0:T(8,128)(2,1)S(1)}, u32[]{:S(2)}, u32[]{:S(2)}) collective-permute-start(bf16[128,128]{1,0:T(8,128)(2,1)S(1)} %collective-permute-done.3.refs_10_.refs_4_), channel_id=1, source_target_pairs={{0,16},{8,24},{16,0},{24,8},{1,17},{9,25},{17,1},{25,9},{2,18},{10... | collective-permute-start | bytes 98312 | tf_op jit(solution)/shard_map/ppermute | solution.py:24
  11.0 0.0 collective-permute-done.refs_7_.refs_1_
  11.0 0.2 collective-permute-start.6
  11.2 1.4 %shard_map.94 = (bf16[128,512]{1,0:T(8,128)(2,1)S(1)}, bf16[128,512]{1,0:T(8,128)(2,1)S(1)}, bf16[2048,128]{1,0:T(8,128)(2,1)S(1)}, f32[8,128]{1,0:T(8,128)S(1)}...) custom-call(bf16[128,512]{1,0:T(8,128)(2,1)} %q_in.1, bf16[128,512]{1,0:T(8,128)(2,1)} %g_in.1, bf16[128,512]{1,0:T(8,128)(2,1)} %o_ref.1, ...), custom_call_target="tpu_custom_call" | custom-call | tf_op jit(solution)/shard_map/pallas_call | solution.py:213
  12.6 0.0 collective-permute-done.1.refs_8_.refs_2_
  12.6 0.0 collective-permute-done.2.refs_9_.refs_3_
  12.6 2.2 %shard_map.95 = (bf16[5120,128]{1,0:T(8,128)(2,1)S(1)}, f32[128,128]{1,0:T(8,128)S(1)}, f32[128,128]{1,0:T(8,128)S(1)}, bf16[128,128]{1,0:T(8,128)(2,1)S(1)}, bf...) custom-call(bf16[128,512]{1,0:T(8,128)(2,1)S(1)} %get-tuple-element.19.refs_0_, ...), custom_call_target="tpu_custom_call" | custom-call | tf_op jit(solution)/shard_map/pallas_call | solution.py:227
  14.8 0.0 collective-permute-done.4.refs_6_.refs_5_
  14.8 0.0 collective-permute-done.5.refs_7_.refs_6_
  14.8 0.0 collective-permute-done.6.refs_8_.refs_7_
  14.9 0.1 shard_map.96
  15.0 0.3 %collective-permute-start.7 = (bf16[128,128]{1,0:T(8,128)(2,1)S(1)}, bf16[128,128]{1,0:T(8,128)(2,1)S(1)}, u32[]{:S(2)}, u32[]{:S(2)}) collective-permute-start(bf16[128,128]{1,0:T(8,128)(2,1)S(1)} %get-tuple-element.31), channel_id=1, source_target_pairs={{0,8},{8,0},{16,24},{24,16},{1,9},{9,1},{17,25},{25,17},{2,10},{10... | collective-permute-start | bytes 98312 | tf_op jit(solution)/shard_map/ppermute | solution.py:24
  15.4 1.7 %collective-permute-start.8 = (bf16[128,128]{1,0:T(8,128)(2,1)S(1)}, bf16[128,128]{1,0:T(8,128)(2,1)S(1)}, u32[]{:S(2)}, u32[]{:S(2)}) collective-permute-start(bf16[128,128]{1,0:T(8,128)(2,1)S(1)} %get-tuple-element.32), channel_id=1, source_target_pairs={{0,16},{8,24},{16,0},{24,8},{1,17},{9,25},{17,1},{25,9},{2,18},{10... | collective-permute-start | bytes 98312 | tf_op jit(solution)/shard_map/ppermute | solution.py:24
  17.0 0.0 collective-permute-start.9
  17.0 0.0 collective-permute-done.7
  17.0 2.3 %collective-permute-done.8 = bf16[128,128]{1,0:T(8,128)(2,1)S(1)} collective-permute-done((bf16[128,128]{1,0:T(8,128)(2,1)S(1)}, bf16[128,128]{1,0:T(8,128)(2,1)S(1)}, u32[]{:S(2)}, u32[]{:S(2)}) %collective-permute-start.8) | collective-permute-done | bytes 32800 | tf_op jit(solution)/shard_map/ppermute | solution.py:24
  19.3 1.3 %collective-permute-done.9 = bf16[128,128]{1,0:T(8,128)(2,1)S(1)} collective-permute-done((bf16[128,128]{1,0:T(8,128)(2,1)S(1)}, bf16[128,128]{1,0:T(8,128)(2,1)S(1)}, u32[]{:S(2)}, u32[]{:S(2)}) %collective-permute-start.9) | collective-permute-done | bytes 32800 | tf_op jit(solution)/shard_map/ppermute | solution.py:24
  20.6 3.4 %collective-permute-start.10 = (bf16[128,128]{1,0:T(8,128)(2,1)S(1)}, bf16[128,128]{1,0:T(8,128)(2,1)S(1)}, u32[]{:S(2)}, u32[]{:S(2)}) collective-permute-start(bf16[128,128]{1,0:T(8,128)(2,1)S(1)} %fusion.8), channel_id=1, source_target_pairs={{0,7},{1,0},{2,1},{3,2},{4,3},{5,4},{6,5},{7,6},{8,15},{9,8},{10,9... | collective-permute-start | bytes 98312 | tf_op jit(solution)/shard_map/ppermute | solution.py:19
  24.0 1.2 %shard_map.97 = bf16[128,512]{1,0:T(8,128)(2,1)} custom-call(bf16[5120,128]{1,0:T(8,128)(2,1)S(1)} %get-tuple-element.25.own_grad_ref, bf16[3072,128]{1,0:T(8,128)(2,1)S(1)} %get-tuple-element.29.near_grad_ref, bf16[128,128]{1,0:T(8,128)(2,1)S(1)} %pad_maximum_fusion.refs_6_.refs_0_, bf16[128,128]{1,0:T(8,128)(2,1)S(1)} %collective-permute-done.refs_7_.refs_1_, ...), custom_call_target="tpu_custom_call" | custom-call | tf_op jit(solution)/shard_map/pallas_call | solution.py:243
  25.2 0.4 %collective-permute-done.10 = bf16[128,128]{1,0:T(8,128)(2,1)S(1)} collective-permute-done((bf16[128,128]{1,0:T(8,128)(2,1)S(1)}, bf16[128,128]{1,0:T(8,128)(2,1)S(1)}, u32[]{:S(2)}, u32[]{:S(2)}) %collective-permute-start.10) | collective-permute-done | bytes 32800 | tf_op jit(solution)/shard_map/ppermute | solution.py:19
  25.6 0.6 %slice_bitcast_fusion = (bf16[128,64]{0,1:T(8,128)(2,1)}, bf16[128,64]{0,1:T(8,128)(2,1)}) fusion(bf16[128,128]{1,0:T(8,128)(2,1)S(1)} %fusion.4), kind=kLoop, calls=%fused_computation.16 | loop fusion | bytes 65536 | tf_op jit(solution)/shard_map/transpose | solution.py:258
  (2 shorter events, 0.1 us)
Async XLA Ops:
  1.4 7.9 %collective-permute-start.3 = (bf16[128,128]{1,0:T(8,128)(2,1)S(1)}, bf16[128,128]{1,0:T(8,128)(2,1)S(1)}, u32[]{:S(2)}, u32[]{:S(2)}) collective-permute-start(bf16[128,128]{1,0:T(8,128)(2,1)S(1)} %pad_maximum_fusion.refs_6_.refs_0_), channel_id=1, source_target_pairs={{0,1},{1,2},{2,3},{3,4},{4,5},{5,6},{6,7},{7,0},{8,9},{9,10},{10,1... | collective-permute-start | bytes 98312 | tf_op jit(solution)/shard_map/ppermute | solution.py:19
  4.4 6.6 %collective-permute-start = (bf16[128,128]{1,0:T(8,128)(2,1)S(1)}, bf16[128,128]{1,0:T(8,128)(2,1)S(1)}, u32[]{:S(2)}, u32[]{:S(2)}) collective-permute-start(bf16[128,128]{1,0:T(8,128)(2,1)S(1)} %pad_maximum_fusion.refs_6_.refs_0_), channel_id=1, source_target_pairs={{0,8},{8,0},{16,24},{24,16},{1,9},{9,1},{17,25},{25,17},{2,10},{10... | collective-permute-start | bytes 98312 | tf_op jit(solution)/shard_map/ppermute | solution.py:24
  4.4 8.2 %collective-permute-start.1 = (bf16[128,128]{1,0:T(8,128)(2,1)S(1)}, bf16[128,128]{1,0:T(8,128)(2,1)S(1)}, u32[]{:S(2)}, u32[]{:S(2)}) collective-permute-start(bf16[128,128]{1,0:T(8,128)(2,1)S(1)} %pad_maximum_fusion.refs_6_.refs_0_), channel_id=1, source_target_pairs={{0,16},{8,24},{16,0},{24,8},{1,17},{9,25},{17,1},{25,9},{2,18},{10... | collective-permute-start | bytes 98312 | tf_op jit(solution)/shard_map/ppermute | solution.py:24
  5.9 6.7 %collective-permute-start.2 = (bf16[128,128]{1,0:T(8,128)(2,1)S(1)}, bf16[128,128]{1,0:T(8,128)(2,1)S(1)}, u32[]{:S(2)}, u32[]{:S(2)}) collective-permute-start(bf16[128,128]{1,0:T(8,128)(2,1)S(1)} %pad_maximum_fusion.refs_6_.refs_0_), channel_id=1, source_target_pairs={{0,24},{8,16},{16,8},{24,0},{1,25},{9,17},{17,9},{25,1},{2,26},{10... | collective-permute-start | bytes 98312 | tf_op jit(solution)/shard_map/ppermute | solution.py:24
  9.3 5.5 %collective-permute-start.4 = (bf16[128,128]{1,0:T(8,128)(2,1)S(1)}, bf16[128,128]{1,0:T(8,128)(2,1)S(1)}, u32[]{:S(2)}, u32[]{:S(2)}) collective-permute-start(bf16[128,128]{1,0:T(8,128)(2,1)S(1)} %collective-permute-done.3.refs_10_.refs_4_), channel_id=1, source_target_pairs={{0,8},{8,0},{16,24},{24,16},{1,9},{9,1},{17,25},{25,17},{2,10},{10... | collective-permute-start | bytes 98312 | tf_op jit(solution)/shard_map/ppermute | solution.py:24
  9.3 5.5 %collective-permute-start.5 = (bf16[128,128]{1,0:T(8,128)(2,1)S(1)}, bf16[128,128]{1,0:T(8,128)(2,1)S(1)}, u32[]{:S(2)}, u32[]{:S(2)}) collective-permute-start(bf16[128,128]{1,0:T(8,128)(2,1)S(1)} %collective-permute-done.3.refs_10_.refs_4_), channel_id=1, source_target_pairs={{0,16},{8,24},{16,0},{24,8},{1,17},{9,25},{17,1},{25,9},{2,18},{10... | collective-permute-start | bytes 98312 | tf_op jit(solution)/shard_map/ppermute | solution.py:24
  11.0 3.9 %collective-permute-start.6 = (bf16[128,128]{1,0:T(8,128)(2,1)S(1)}, bf16[128,128]{1,0:T(8,128)(2,1)S(1)}, u32[]{:S(2)}, u32[]{:S(2)}) collective-permute-start(bf16[128,128]{1,0:T(8,128)(2,1)S(1)} %collective-permute-done.3.refs_10_.refs_4_), channel_id=1, source_target_pairs={{0,24},{8,16},{16,8},{24,0},{1,25},{9,17},{17,9},{25,1},{2,26},{10... | collective-permute-start | bytes 98312 | tf_op jit(solution)/shard_map/ppermute | solution.py:24
  15.0 2.0 %collective-permute-start.7 = (bf16[128,128]{1,0:T(8,128)(2,1)S(1)}, bf16[128,128]{1,0:T(8,128)(2,1)S(1)}, u32[]{:S(2)}, u32[]{:S(2)}) collective-permute-start(bf16[128,128]{1,0:T(8,128)(2,1)S(1)} %get-tuple-element.31), channel_id=1, source_target_pairs={{0,8},{8,0},{16,24},{24,16},{1,9},{9,1},{17,25},{25,17},{2,10},{10... | collective-permute-start | bytes 98312 | tf_op jit(solution)/shard_map/ppermute | solution.py:24
  15.4 3.9 %collective-permute-start.8 = (bf16[128,128]{1,0:T(8,128)(2,1)S(1)}, bf16[128,128]{1,0:T(8,128)(2,1)S(1)}, u32[]{:S(2)}, u32[]{:S(2)}) collective-permute-start(bf16[128,128]{1,0:T(8,128)(2,1)S(1)} %get-tuple-element.32), channel_id=1, source_target_pairs={{0,16},{8,24},{16,0},{24,8},{1,17},{9,25},{17,1},{25,9},{2,18},{10... | collective-permute-start | bytes 98312 | tf_op jit(solution)/shard_map/ppermute | solution.py:24
  17.0 3.6 %collective-permute-start.9 = (bf16[128,128]{1,0:T(8,128)(2,1)S(1)}, bf16[128,128]{1,0:T(8,128)(2,1)S(1)}, u32[]{:S(2)}, u32[]{:S(2)}) collective-permute-start(bf16[128,128]{1,0:T(8,128)(2,1)S(1)} %get-tuple-element.33), channel_id=1, source_target_pairs={{0,24},{8,16},{16,8},{24,0},{1,25},{9,17},{17,9},{25,1},{2,26},{10... | collective-permute-start | bytes 98312 | tf_op jit(solution)/shard_map/ppermute | solution.py:24
  20.6 5.0 %collective-permute-start.10 = (bf16[128,128]{1,0:T(8,128)(2,1)S(1)}, bf16[128,128]{1,0:T(8,128)(2,1)S(1)}, u32[]{:S(2)}, u32[]{:S(2)}) collective-permute-start(bf16[128,128]{1,0:T(8,128)(2,1)S(1)} %fusion.8), channel_id=1, source_target_pairs={{0,7},{1,0},{2,1},{3,2},{4,3},{5,4},{6,5},{7,6},{8,15},{9,8},{10,9... | collective-permute-start | bytes 98312 | tf_op jit(solution)/shard_map/ppermute | solution.py:19

commit v4 on v3

v4 whole, which is shorter than its diff:
```python
import functools
import math

import jax
import jax.numpy as jnp
from jax import lax
from jax.experimental import pallas as pl
from jax.experimental.pallas import tpu as pltpu
from jax.sharding import PartitionSpec as P


NT = (((1,), (1,)), ((), ()))
NN = (((1,), (0,)), ((), ()))
FRONT = 4


def around(x, axis, by):
    count = lax.axis_size(axis)
    return lax.ppermute(x, axis, [(i, (i + by) % count) for i in range(count)])


def exchanged(x, axis, step):
    count = lax.axis_size(axis)
    return lax.ppermute(x, axis, [(i, i ^ step) for i in range(count)])


def dot(a, b, dims):
    return lax.dot_general(a, b, dims, preferred_element_type=jnp.float32)


def half_turn(x, width):
    return jnp.concatenate([x[:, width:], x[:, :width]], 1)


def front_body(q_in, g_in, o_ref, log_in, begin_in, rows_ref, aux_ref):
    rows, features = q_in.shape
    heads = log_in.shape[0]
    width = features // heads
    rows_ref[:, :features] = q_in[...]
    rows_ref[:, features:] = g_in[...]
    aux_ref[:heads, :] = log_in[...]
    prod = g_in[...].astype(jnp.float32) * o_ref[...].astype(jnp.float32)
    feature = lax.broadcasted_iota(jnp.int32, (heads, features), 1)
    head_of = lax.broadcasted_iota(jnp.int32, (heads, features), 0)
    pick = (feature // width == head_of).astype(jnp.float32)
    aux_ref[heads : 2 * heads, :] = lax.dot_general(
        pick, prod, NT, precision=lax.Precision.HIGHEST, preferred_element_type=jnp.float32
    )
    begin = begin_in[...].astype(jnp.float32)
    aux_ref[2 * heads :, :] = jnp.broadcast_to(begin, (heads, rows))


def tile_terms(slab_refs, bases, front, grad_ref, key_acc, value_acc):
    mine_ref, other_ref, aux_ref, aux_other_ref = front
    lanes, rows = slab_refs[0].shape
    width = lanes // 2
    heads = aux_ref.shape[0] // 3
    features = heads * width
    total = len(slab_refs) * rows
    spot = lax.axis_index("team")
    first_row = (lax.axis_index("blk") * lax.axis_size("team") + spot) * rows

    def of_rows(index):
        at = slice(index, index + 1)
        return jnp.concatenate([aux_ref[at, :], aux_other_ref[at, :]], 1)

    def pair_rows(start):
        span = slice(start, start + lanes)
        return jnp.concatenate([mine_ref[:, span], other_ref[:, span]], 0)

    kv = jnp.concatenate([ref[...] for ref in slab_refs], 1).T
    low_key = lax.broadcasted_iota(jnp.int32, (total, lanes), 1) < width
    none = jnp.zeros_like(kv)
    k_low = jnp.where(low_key, kv * jnp.asarray(1.0 / math.sqrt(width), kv.dtype), none)
    v_high = jnp.where(low_key, none, kv)
    key_halves = (k_low, half_turn(k_low, width))
    value_halves = (half_turn(v_high, width), v_high)
    inside = lax.broadcasted_iota(jnp.int32, (rows, 2 * rows), 0)
    key_pos = jnp.concatenate([inside + base for base in bases], 0)
    lane = lax.broadcasted_iota(jnp.int32, (1, 2 * rows), 1)
    row_pos = jnp.where(lane < rows, lane, lane + ((spot ^ 1) - spot - 1) * rows)
    begin = of_rows(2 * heads).astype(jnp.int32) - first_row
    allowed = (key_pos >= begin) & (key_pos <= row_pos)
    low_row = lax.broadcasted_iota(jnp.int32, (2 * rows, lanes), 1) < width
    for pair in range(heads // 2):
        q_pair = pair_rows(pair * lanes)
        g_pair = pair_rows(features + pair * lanes)
        blank = jnp.zeros_like(q_pair)
        probs, grads = [], []
        for half in range(2):
            head = 2 * pair + half
            scores = dot(key_halves[half], q_pair, NT)
            shifted = scores - of_rows(head)
            weights = jnp.exp(jnp.where(allowed, shifted, -jnp.inf))
            prob_grad = dot(value_halves[half], g_pair, NT)
            score_grad = weights * (prob_grad - of_rows(heads + head))
            low = score_grad.astype(jnp.bfloat16)
            grad_ref[head * total : (head + 1) * total, :] = low
            probs.append(weights.astype(jnp.bfloat16))
            grads.append(low)
        for acc, left, right in ((key_acc, grads, q_pair), (value_acc, probs, g_pair)):
            parts = [jnp.where(low_row, right, blank), jnp.where(low_row, blank, right)]
            term = dot(jnp.concatenate(left, 1), jnp.concatenate(parts, 0), NN)
            if pair == 0:
                acc[...] = term
            else:
                acc[...] += term


def slab_of(key_acc, value_acc, number, rows, width):
    keys = key_acc[number * rows : (number + 1) * rows, :]
    values = value_acc[number * rows : (number + 1) * rows, :]
    keys = (keys + half_turn(keys, width)) * jnp.float32(1.0 / math.sqrt(width))
    values = values + half_turn(values, width)
    low = lax.broadcasted_iota(jnp.int32, keys.shape, 1) < width
    return jnp.where(low, keys, values).T


def own_body(*refs):
    front, slab_refs = refs[:FRONT], refs[FRONT : FRONT + 2]
    grad_ref, own_ref, near_ref, key_acc, value_acc = refs[FRONT + 2 :]
    lanes, rows = slab_refs[0].shape
    bases = [0, -lax.axis_size("team") * rows]
    tile_terms(slab_refs, bases, front, grad_ref, key_acc, value_acc)
    own_ref[...] = slab_of(key_acc, value_acc, 0, rows, lanes // 2)
    near_ref[...] = slab_of(key_acc, value_acc, 1, rows, lanes // 2)


def rest_body(steps, *refs):
    count = len(steps)
    front, slab_refs = refs[:FRONT], refs[FRONT : FRONT + count]
    grad_ref, *piece_refs, key_acc, value_acc = refs[FRONT + count :]
    lanes, rows = slab_refs[0].shape
    spot = lax.axis_index("team")
    block = lax.axis_size("team")
    bases = []
    for step in steps:
        slot = spot ^ step
        bases.append((slot - spot - jnp.where(slot > spot, block, 0)) * rows)
    tile_terms(slab_refs, bases, front, grad_ref, key_acc, value_acc)
    for n, piece_ref in enumerate(piece_refs):
        part = slab_of(key_acc, value_acc, n, rows, lanes // 2)
        piece_ref[...] = part.astype(jnp.bfloat16)


def query_body(own_grad_ref, near_grad_ref, *refs):
    slab_refs, (mine_ref, other_ref) = refs[:-2], refs[-2:]
    lanes, rows = slab_refs[0].shape
    width = lanes // 2
    heads = mine_ref.shape[1] // width
    small = jnp.asarray(1.0 / math.sqrt(width), slab_refs[0].dtype)
    own_keys = jnp.concatenate([ref[:width, :] for ref in slab_refs[:2]], 1) * small
    near_keys = jnp.concatenate([ref[:width, :] for ref in slab_refs[2:]], 1) * small

    def flipped(head):
        terms = 0.0
        for keys, grads in ((own_keys, own_grad_ref), (near_keys, near_grad_ref)):
            total = keys.shape[1]
            terms += dot(keys, grads[head * total : (head + 1) * total, :], NN)
        return terms

    for pair in range(heads // 2):
        both = jnp.concatenate([flipped(2 * pair), flipped(2 * pair + 1)], 0)
        span = slice(pair * lanes, (pair + 1) * lanes)
        mine_ref[:, span] = both[:, :rows].T
        other_ref[:, span] = both[:, rows:].T.astype(jnp.bfloat16)


def in_vmem(count):
    return [pl.BlockSpec(memory_space=pltpu.VMEM) for _ in range(count)]


def held(*arrays, space=pltpu.VMEM):
    return [pltpu.with_memory_space_constraint(x, space) for x in arrays]


def grant(slabs, rows, lanes):
    return pltpu.CompilerParams(vmem_limit_bytes=(8 << 20) + 192 * slabs * rows * lanes)


def per_device(queries, keys, values, attn_out, out_grad, log_norm, doc_start):
    rows, features = queries.shape
    heads = log_norm.shape[0]
    width = keys.shape[1]
    lanes = 2 * width
    half = lax.axis_size("team") // 2
    spot = lax.axis_index("team")
    steps = [2 * n for n in range(1, half)]

    def low(*dims):
        return pltpu.VMEM(dims, jnp.bfloat16)

    def full(*dims):
        return pltpu.VMEM(dims, jnp.float32)

    slab = full(lanes, rows)
    params = grant(max(2, half), rows, lanes)
    mine = jnp.concatenate([keys.T, values.T], 0)
    past = around(mine, "blk", 1)
    own_rows, aux = pl.pallas_call(
        front_body,
        out_shape=[low(rows, 2 * features), full(3 * heads, rows)],
        in_specs=in_vmem(5),
        out_specs=in_vmem(2),
        compiler_params=params,
    )(
        *held(
            queries,
            out_grad,
            attn_out,
            log_norm,
            doc_start.reshape(1, rows),
            space=pltpu.HBM,
        )
    )
    other_rows = exchanged(own_rows, "team", 1)
    other_aux = exchanged(aux, "team", 1)
    front = (own_rows, other_rows, aux, other_aux)
    seen = []
    for k in steps:
        chosen = jnp.where((spot ^ k) < spot, past, mine)
        seen.append(exchanged(chosen, "team", k))
    own_grads, own_sum, near_sum = pl.pallas_call(
        own_body,
        out_shape=[low(2 * heads * rows, 2 * rows), slab, slab],
        in_specs=in_vmem(FRONT + 2),
        out_specs=in_vmem(3),
        scratch_shapes=[full(2 * rows, lanes)] * 2,
        compiler_params=params,
    )(*held(*front, mine, past))
    rest_grads, *sent = pl.pallas_call(
        functools.partial(rest_body, steps),
        out_shape=[low(heads * (half - 1) * rows, 2 * rows)] + [low(lanes, rows)] * (half - 1),
        in_specs=in_vmem(FRONT + half - 1),
        out_specs=in_vmem(half),
        scratch_shapes=[full((half - 1) * rows, lanes)] * 2,
        compiler_params=params,
    )(*held(*front, *seen))
    query_mine, query_other = pl.pallas_call(
        query_body,
        out_shape=[full(rows, features), low(rows, features)],
        in_specs=in_vmem(3 + half),
        out_specs=in_vmem(2),
        compiler_params=params,
    )(*held(own_grads, rest_grads, mine, past, *seen))
    query_back = exchanged(query_other, "team", 1)
    query_grad = (query_mine + query_back.astype(jnp.float32)).astype(jnp.bfloat16)
    nothing = jnp.float32(0.0)
    for k, piece in zip(steps, sent):
        got = exchanged(piece, "team", k).astype(jnp.float32)
        later = (spot ^ k) > spot
        near_sum = near_sum + jnp.where(later, nothing, got)
        own_sum = own_sum + jnp.where(later, got, nothing)
    back = around(near_sum.astype(jnp.bfloat16), "blk", -1)
    total = (own_sum + back.astype(jnp.float32)).astype(jnp.bfloat16)
    return (query_grad, total[:width].T, total[width:].T)


def solution(mesh):
    row = P(("blk", "team"), None)

    return jax.shard_map(
        per_device,
        mesh=mesh,
        in_specs=(row, row, row, row, row, P(None, ("blk", "team")), P(("blk", "team"))),
        out_specs=(row, row, row),
        check_vma=False,
    )
```

time: 26.5 us -> 24.2 us (0.913)
  starting transfers between devices: 12.1 us -> 8.58 us
  other arithmetic: 0.8 us -> 1.47 us
  waiting for transfers between devices: 7.02 us -> 7.58 us
    ppermute x9 -> x5, starting transfers between devices: 5.73 us -> 3.51 us  [exchanged(): return lax.ppermute(x, axis, [(i, i ^ step) for i in range(count)])]
    ppermute x2, waiting for transfers between devices: 3.45 us -> 4.83 us  [around(): return lax.ppermute(x, axis, [(i, (i + by) % count) for i in range(count)])]
    ppermute x2, starting transfers between devices: 6.35 us -> 5.07 us  [around(): return lax.ppermute(x, axis, [(i, (i + by) % count) for i in range(count)])]
    ppermute x9 -> x5, waiting for transfers between devices: 3.58 us -> 2.75 us  [exchanged(): return lax.ppermute(x, axis, [(i, i ^ step) for i in range(count)])]
    convert_element_type x0 -> x1, other arithmetic: none -> 0.68 us  [per_device(): (query_mine + query_back.astype(jnp.float32)).astype(jnp.bfloat16)]
  transfers between devices with their start and end apart: 11 -> 7, of which waited for: 4 -> 5; matrix products, arithmetic and copies ran while one was open for 0% -> 3% of each run, Pallas kernels for 19% -> 15%
where the time goes in v4:
time: 24.2 us; the launch traced here: 23.9 us
  starting transfers between devices  8.58 us (35%)
  waiting for transfers between devices  7.58 us (31%)
  Pallas kernels  4.98 us (21%)
  other arithmetic  1.47 us (6%)
  between operations  0.67 us (3%)
  local copies, waits for them, and re-layouts  0.62 us (3%)
    ppermute x2, starting transfers between devices, around(): return lax.ppermute(x, axis, [(i, (i + by) % count) for i in range(count)])  5.07 us
    ppermute x2, waiting for transfers between devices, around(): return lax.ppermute(x, axis, [(i, (i + by) % count) for i in range(count)])  4.83 us
    ppermute x5, starting transfers between devices, exchanged(): return lax.ppermute(x, axis, [(i, i ^ step) for i in range(count)])  3.51 us
    ppermute x5, waiting for transfers between devices, exchanged(): return lax.ppermute(x, axis, [(i, i ^ step) for i in range(count)])  2.75 us
    pallas_call x1, Pallas kernels, per_device(): pl.pallas_call(own_body, out_shape=[low(2 * heads * rows, 2 * rows), slab...  1.77 us
    pallas_call x1, Pallas kernels, per_device(): pl.pallas_call(front_body, out_shape=[low(rows, 2 * features), full(3 * h...  1.4 us
    pallas_call x1, Pallas kernels, per_device(): pl.pallas_call(functools.partial(rest_body, steps), out_shape=[low(heads...  1.31 us
    concatenate x1, other arithmetic, per_device(): mine = jnp.concatenate([keys.T, values.T], 0)  0.74 us
  transfers between devices with their start and end apart: 7, of which 5 were waited for; matrix products, arithmetic and copies ran while one was open for 3% of the time, Pallas kernels for 15%

profile of v4, /device:TPU:0, one launch (start us, length us, event | category | flops | bytes accessed | tf_op | source)
XLA Modules:
  0.0 23.9 jit_solution(18274557074301600220)
XLA Ops:
  0.6 0.7 %pad_maximum_fusion.refs_4_.refs_0_ = bf16[128,128]{1,0:T(8,128)(2,1)S(1)} fusion(bf16[64,128]{1,0:T(8,128)(2,1)} %bitcast.7, bf16[64,128]{1,0:T(8,128)(2,1)} %bitcast.9), kind=kLoop, calls=%fused_computation.8 | loop fusion | flops 65536 | bytes 65536 | tf_op jit(solution)/shard_map/concatenate | solution.py:198
  1.4 3.0 %collective-permute-start.2 = (bf16[128,128]{1,0:T(8,128)(2,1)S(1)}, bf16[128,128]{1,0:T(8,128)(2,1)S(1)}, u32[]{:S(2)}, u32[]{:S(2)}) collective-permute-start(bf16[128,128]{1,0:T(8,128)(2,1)S(1)} %pad_maximum_fusion.refs_4_.refs_0_), channel_id=1, source_target_pairs={{0,1},{1,2},{2,3},{3,4},{4,5},{5,6},{6,7},{7,0},{8,9},{9,10},{10,1... | collective-permute-start | bytes 98312 | tf_op jit(solution)/shard_map/ppermute | solution.py:19
  4.4 0.0 copy-start
  4.4 0.0 copy-start.1
  4.4 1.4 %shard_map.94 = (bf16[128,1024]{1,0:T(8,128)(2,1)S(1)}, f32[24,128]{1,0:T(8,128)S(1)}) custom-call(bf16[128,512]{1,0:T(8,128)(2,1)} %q_in.1, bf16[128,512]{1,0:T(8,128)(2,1)} %g_in.1, bf16[128,512]{1,0:T(8,128)(2,1)} %o_ref.1, f32[8,128]{1,0:T(8,128)} %log_in.1, s32[1,128]{1,0:T(1,128)} %bitcast.11), custom_call_target="tpu_custom_call" | custom-call | tf_op jit(solution)/shard_map/pallas_call | solution.py:200
  5.8 0.0 collective-permute-start
  5.8 3.5 %collective-permute-done.2.refs_5_.refs_1_ = bf16[128,128]{1,0:T(8,128)(2,1)S(1)} collective-permute-done((bf16[128,128]{1,0:T(8,128)(2,1)S(1)}, bf16[128,128]{1,0:T(8,128)(2,1)S(1)}, u32[]{:S(2)}, u32[]{:S(2)}) %collective-permute-start.2) | collective-permute-done | bytes 32800 | tf_op jit(solution)/shard_map/ppermute | solution.py:19
  9.3 0.0 copy-done
  9.3 0.0 copy-done.1
  9.3 1.7 %collective-permute-start.3 = (bf16[128,128]{1,0:T(8,128)(2,1)S(1)}, bf16[128,128]{1,0:T(8,128)(2,1)S(1)}, u32[]{:S(2)}, u32[]{:S(2)}) collective-permute-start(bf16[128,128]{1,0:T(8,128)(2,1)S(1)} %broadcast_select_fusion), channel_id=1, source_target_pairs={{0,16},{8,24},{16,0},{24,8},{1,17},{9,25},{17,1},{25,9},{2,18},{10... | collective-permute-start | bytes 98312 | tf_op jit(solution)/shard_map/ppermute | solution.py:24
  11.0 0.0 collective-permute-start.1
  11.0 1.2 %collective-permute-done.1.refs_3_ = f32[24,128]{1,0:T(8,128)S(1)} collective-permute-done((f32[24,128]{1,0:T(8,128)S(1)}, f32[24,128]{1,0:T(8,128)S(1)}, u32[]{:S(2)}, u32[]{:S(2)}) %collective-permute-start.1) | collective-permute-done | bytes 12320 | tf_op jit(solution)/shard_map/ppermute | solution.py:24
  12.2 1.1 %collective-permute-done.3.refs_4_.refs_2_ = bf16[128,128]{1,0:T(8,128)(2,1)S(1)} collective-permute-done((bf16[128,128]{1,0:T(8,128)(2,1)S(1)}, bf16[128,128]{1,0:T(8,128)(2,1)S(1)}, u32[]{:S(2)}, u32[]{:S(2)}) %collective-permute-start.3) | collective-permute-done | bytes 32800 | tf_op jit(solution)/shard_map/ppermute | solution.py:24
  13.3 0.0 collective-permute-done.refs_1_
  13.3 1.3 %shard_map.96 = (bf16[1024,256]{1,0:T(8,128)(2,1)S(1)}, bf16[128,128]{1,0:T(8,128)(2,1)S(1)}) custom-call(bf16[128,1024]{1,0:T(8,128)(2,1)S(1)} %get-tuple-element.12.refs_0_, bf16[128,1024]{1,0:T(8,128)(2,1)S(1)} %collective-permute-done.refs_1_, f32[24,128]{1,0:T(8,128)S(1)} %get-tuple-element.13.refs_2_, f32[24,128]{1,0:T(8,128)S(1)} %collective-permute-done.1.refs_3_, ...), custom_call_target="tpu_custom_call" | custom-call | tf_op jit(solution)/shard_map/pallas_call | solution.py:231
  14.6 1.7 %collective-permute-start.5 = (bf16[128,128]{1,0:T(8,128)(2,1)S(1)}, bf16[128,128]{1,0:T(8,128)(2,1)S(1)}, u32[]{:S(2)}, u32[]{:S(2)}) collective-permute-start(bf16[128,128]{1,0:T(8,128)(2,1)S(1)} %get-tuple-element.19), channel_id=1, source_target_pairs={{0,16},{8,24},{16,0},{24,8},{1,17},{9,25},{17,1},{25,9},{2,18},{10... | collective-permute-start | bytes 98312 | tf_op jit(solution)/shard_map/ppermute | solution.py:24
  16.3 1.8 %shard_map.95 = (bf16[2048,256]{1,0:T(8,128)(2,1)S(1)}, f32[128,128]{1,0:T(8,128)S(1)}, f32[128,128]{1,0:T(8,128)S(1)}) custom-call(bf16[128,1024]{1,0:T(8,128)(2,1)S(1)} %get-tuple-element.12.refs_0_, bf16[128,1024]{1,0:T(8,128)(2,1)S(1)} %collective-permute-done.refs_1_, f32[24,128]{1,0:T(8,128)S(1)} %get-tuple-element.13.refs_2_, ...), custom_call_target="tpu_custom_call" | custom-call | tf_op jit(solution)/shard_map/pallas_call | solution.py:223
  18.1 0.5 %collective-permute-done.5 = bf16[128,128]{1,0:T(8,128)(2,1)S(1)} collective-permute-done((bf16[128,128]{1,0:T(8,128)(2,1)S(1)}, bf16[128,128]{1,0:T(8,128)(2,1)S(1)}, u32[]{:S(2)}, u32[]{:S(2)}) %collective-permute-start.5) | collective-permute-done | bytes 32800 | tf_op jit(solution)/shard_map/ppermute | solution.py:24
  18.6 2.1 %collective-permute-start.6 = (bf16[128,128]{1,0:T(8,128)(2,1)S(1)}, bf16[128,128]{1,0:T(8,128)(2,1)S(1)}, u32[]{:S(2)}, u32[]{:S(2)}) collective-permute-start(bf16[128,128]{1,0:T(8,128)(2,1)S(1)} %fusion.4), channel_id=1, source_target_pairs={{0,7},{1,0},{2,1},{3,2},{4,3},{5,4},{6,5},{7,6},{8,15},{9,8},{10,9... | collective-permute-start | bytes 98312 | tf_op jit(solution)/shard_map/ppermute | solution.py:19
  20.7 0.5 %shard_map.97 = (f32[128,512]{1,0:T(8,128)S(1)}, bf16[128,512]{1,0:T(8,128)(2,1)S(1)}) custom-call(bf16[2048,256]{1,0:T(8,128)(2,1)S(1)} %get-tuple-element.14.own_grad_ref, bf16[1024,256]{1,0:T(8,128)(2,1)S(1)} %get-tuple-element.15.near_grad_ref, bf16[128,128]{1,0:T(8,128)(2,1)S(1)} %pad_maximum_fusion.refs_4_.refs_0_, ...), custom_call_target="tpu_custom_call" | custom-call | tf_op jit(solution)/shard_map/pallas_call | solution.py:239
  21.2 0.1 collective-permute-start.4
  21.3 1.3 %collective-permute-done.6 = bf16[128,128]{1,0:T(8,128)(2,1)S(1)} collective-permute-done((bf16[128,128]{1,0:T(8,128)(2,1)S(1)}, bf16[128,128]{1,0:T(8,128)(2,1)S(1)}, u32[]{:S(2)}, u32[]{:S(2)}) %collective-permute-start.6) | collective-permute-done | bytes 32800 | tf_op jit(solution)/shard_map/ppermute | solution.py:19
  22.6 0.6 %slice_bitcast_fusion = (bf16[128,64]{0,1:T(8,128)(2,1)}, bf16[128,64]{0,1:T(8,128)(2,1)}) fusion(bf16[128,128]{1,0:T(8,128)(2,1)S(1)} %fusion.2), kind=kLoop, calls=%fused_computation.10 | loop fusion | bytes 65536 | tf_op jit(solution)/shard_map/transpose | solution.py:256
  23.2 0.0 collective-permute-done.4
  23.2 0.7 %add_convert_fusion = bf16[128,512]{1,0:T(8,128)(2,1)} fusion(f32[128,512]{1,0:T(8,128)S(1)} %get-tuple-element.16, bf16[128,512]{1,0:T(8,128)(2,1)S(1)} %collective-permute-done.4), kind=kLoop, calls=%fused_computation | loop fusion | flops 196608 | bytes 524288 | tf_op jit(solution)/shard_map/convert_element_type | solution.py:247
  (3 shorter events, 0.0 us)
Async XLA Ops:
  1.4 7.9 %collective-permute-start.2 = (bf16[128,128]{1,0:T(8,128)(2,1)S(1)}, bf16[128,128]{1,0:T(8,128)(2,1)S(1)}, u32[]{:S(2)}, u32[]{:S(2)}) collective-permute-start(bf16[128,128]{1,0:T(8,128)(2,1)S(1)} %pad_maximum_fusion.refs_4_.refs_0_), channel_id=1, source_target_pairs={{0,1},{1,2},{2,3},{3,4},{4,5},{5,6},{6,7},{7,0},{8,9},{9,10},{10,1... | collective-permute-start | bytes 98312 | tf_op jit(solution)/shard_map/ppermute | solution.py:19
  4.4 4.9 %copy-start = (bf16[128,64]{0,1:T(8,128)(2,1)S(1)}, bf16[128,64]{0,1:T(8,128)(2,1)}, u32[]{:S(2)}) copy-start(bf16[128,64]{0,1:T(8,128)(2,1)} %param.9) | copy-start | bytes 49156
  4.4 4.9 %copy-start.1 = (bf16[128,64]{0,1:T(8,128)(2,1)S(1)}, bf16[128,64]{0,1:T(8,128)(2,1)}, u32[]{:S(2)}) copy-start(bf16[128,64]{0,1:T(8,128)(2,1)} %param.8) | copy-start | bytes 49156
  5.8 7.5 %collective-permute-start = (bf16[128,1024]{1,0:T(8,128)(2,1)S(1)}, bf16[128,1024]{1,0:T(8,128)(2,1)S(1)}, u32[]{:S(2)}, u32[]{:S(2)}) collective-permute-start(bf16[128,1024]{1,0:T(8,128)(2,1)S(1)} %get-tuple-element.12.refs_0_), channel_id=1, source_target_pairs={{0,8},{8,0},{16,24},{24,16},{1,9},{9,1},{17,25},{25,17},{2,10},{10... | collective-permute-start | bytes 786440 | tf_op jit(solution)/shard_map/ppermute | solution.py:24
  9.3 4.0 %collective-permute-start.3 = (bf16[128,128]{1,0:T(8,128)(2,1)S(1)}, bf16[128,128]{1,0:T(8,128)(2,1)S(1)}, u32[]{:S(2)}, u32[]{:S(2)}) collective-permute-start(bf16[128,128]{1,0:T(8,128)(2,1)S(1)} %broadcast_select_fusion), channel_id=1, source_target_pairs={{0,16},{8,24},{16,0},{24,8},{1,17},{9,25},{17,1},{25,9},{2,18},{10... | collective-permute-start | bytes 98312 | tf_op jit(solution)/shard_map/ppermute | solution.py:24
  11.0 1.2 %collective-permute-start.1 = (f32[24,128]{1,0:T(8,128)S(1)}, f32[24,128]{1,0:T(8,128)S(1)}, u32[]{:S(2)}, u32[]{:S(2)}) collective-permute-start(f32[24,128]{1,0:T(8,128)S(1)} %get-tuple-element.13.refs_2_), channel_id=1, source_target_pairs={{0,8},{8,0},{16,24},{24,16},{1,9},{9,1},{17,25},{25,17},{2,10},{10... | collective-permute-start | bytes 36872 | tf_op jit(solution)/shard_map/ppermute | solution.py:24
  14.6 4.0 %collective-permute-start.5 = (bf16[128,128]{1,0:T(8,128)(2,1)S(1)}, bf16[128,128]{1,0:T(8,128)(2,1)S(1)}, u32[]{:S(2)}, u32[]{:S(2)}) collective-permute-start(bf16[128,128]{1,0:T(8,128)(2,1)S(1)} %get-tuple-element.19), channel_id=1, source_target_pairs={{0,16},{8,24},{16,0},{24,8},{1,17},{9,25},{17,1},{25,9},{2,18},{10... | collective-permute-start | bytes 98312 | tf_op jit(solution)/shard_map/ppermute | solution.py:24
  18.6 4.0 %collective-permute-start.6 = (bf16[128,128]{1,0:T(8,128)(2,1)S(1)}, bf16[128,128]{1,0:T(8,128)(2,1)S(1)}, u32[]{:S(2)}, u32[]{:S(2)}) collective-permute-start(bf16[128,128]{1,0:T(8,128)(2,1)S(1)} %fusion.4), channel_id=1, source_target_pairs={{0,7},{1,0},{2,1},{3,2},{4,3},{5,4},{6,5},{7,6},{8,15},{9,8},{10,9... | collective-permute-start | bytes 98312 | tf_op jit(solution)/shard_map/ppermute | solution.py:19
  21.2 2.0 %collective-permute-start.4 = (bf16[128,512]{1,0:T(8,128)(2,1)S(1)}, bf16[128,512]{1,0:T(8,128)(2,1)S(1)}, u32[]{:S(2)}, u32[]{:S(2)}) collective-permute-start(bf16[128,512]{1,0:T(8,128)(2,1)S(1)} %get-tuple-element.17), channel_id=1, source_target_pairs={{0,8},{8,0},{16,24},{24,16},{1,9},{9,1},{17,25},{25,17},{2,10},{10... | collective-permute-start | bytes 393224 | tf_op jit(solution)/shard_map/ppermute | solution.py:24

commit v5 on v4

--- a/solution.py
+++ b/solution.py
@@ -16,12 +16,25 @@
 
 def around(x, axis, by):
     count = lax.axis_size(axis)
-    return lax.ppermute(x, axis, [(i, (i + by) % count) for i in range(count)])
+    pairs = [(i, (i + by) % count) for i in range(count) if by > 0 or i + by >= 0]
+    return lax.ppermute(x, axis, pairs)
 
 
 def exchanged(x, axis, step):
     count = lax.axis_size(axis)
     return lax.ppermute(x, axis, [(i, i ^ step) for i in range(count)])
+
+
+def sent_home(x, step):
+    team, blk = lax.axis_size("team"), lax.axis_size("blk")
+    pairs = []
+    for t in range(team):
+        slot = t ^ step
+        for b in range(blk):
+            home = b - 1 if slot > t else b
+            if home >= 0:
+                pairs.append((t * blk + b, slot * blk + home))
+    return lax.ppermute(x, ("team", "blk"), pairs)
 
 
 def dot(a, b, dims):
@@ -57,6 +70,7 @@
     heads = aux_ref.shape[0] // 3
     features = heads * width
     total = len(slab_refs) * rows
+    stride = grad_ref.shape[0] // heads
     spot = lax.axis_index("team")
     first_row = (lax.axis_index("blk") * lax.axis_size("team") + spot) * rows
 
@@ -95,16 +109,16 @@
             prob_grad = dot(value_halves[half], g_pair, NT)
             score_grad = weights * (prob_grad - of_rows(heads + head))
             low = score_grad.astype(jnp.bfloat16)
-            grad_ref[head * total : (head + 1) * total, :] = low
+            grad_ref[head * stride : head * stride + total, :] = low
             probs.append(weights.astype(jnp.bfloat16))
             grads.append(low)
         for acc, left, right in ((key_acc, grads, q_pair), (value_acc, probs, g_pair)):
             parts = [jnp.where(low_row, right, blank), jnp.where(low_row, blank, right)]
             term = dot(jnp.concatenate(left, 1), jnp.concatenate(parts, 0), NN)
             if pair == 0:
-                acc[...] = term
+                acc[:total, :] = term
             else:
-                acc[...] += term
+                acc[:total, :] += term
 
 
 def slab_of(key_acc, value_acc, number, rows, width):
@@ -120,10 +134,25 @@
     front, slab_refs = refs[:FRONT], refs[FRONT : FRONT + 2]
     grad_ref, own_ref, near_ref, key_acc, value_acc = refs[FRONT + 2 :]
     lanes, rows = slab_refs[0].shape
-    bases = [0, -lax.axis_size("team") * rows]
-    tile_terms(slab_refs, bases, front, grad_ref, key_acc, value_acc)
+    heads = grad_ref.shape[0] // (2 * rows)
+    has_past = lax.axis_index("blk") > 0
+
+    @pl.when(has_past)
+    def _():
+        bases = [0, -lax.axis_size("team") * rows]
+        tile_terms(slab_refs, bases, front, grad_ref, key_acc, value_acc)
+        part = slab_of(key_acc, value_acc, 1, rows, lanes // 2)
+        near_ref[...] = part.astype(jnp.bfloat16)
+
+    @pl.when(jnp.logical_not(has_past))
+    def _():
+        tile_terms(slab_refs[:1], [0], front, grad_ref, key_acc, value_acc)
+        near_ref[...] = jnp.zeros_like(near_ref)
+        for head in range(heads):
+            at = (2 * head + 1) * rows
+            grad_ref[at : at + rows, :] = jnp.zeros((rows, 2 * rows), grad_ref.dtype)
+
     own_ref[...] = slab_of(key_acc, value_acc, 0, rows, lanes // 2)
-    near_ref[...] = slab_of(key_acc, value_acc, 1, rows, lanes // 2)
 
 
 def rest_body(steps, *refs):
@@ -220,9 +249,9 @@
     for k in steps:
         chosen = jnp.where((spot ^ k) < spot, past, mine)
         seen.append(exchanged(chosen, "team", k))
-    own_grads, own_sum, near_sum = pl.pallas_call(
+    own_grads, total, past_piece = pl.pallas_call(
         own_body,
-        out_shape=[low(2 * heads * rows, 2 * rows), slab, slab],
+        out_shape=[low(2 * heads * rows, 2 * rows), slab, low(lanes, rows)],
         in_specs=in_vmem(FRONT + 2),
         out_specs=in_vmem(3),
         scratch_shapes=[full(2 * rows, lanes)] * 2,
@@ -245,14 +274,11 @@
     )(*held(own_grads, rest_grads, mine, past, *seen))
     query_back = exchanged(query_other, "team", 1)
     query_grad = (query_mine + query_back.astype(jnp.float32)).astype(jnp.bfloat16)
-    nothing = jnp.float32(0.0)
-    for k, piece in zip(steps, sent):
-        got = exchanged(piece, "team", k).astype(jnp.float32)
-        later = (spot ^ k) > spot
-        near_sum = near_sum + jnp.where(later, nothing, got)
-        own_sum = own_sum + jnp.where(later, got, nothing)
-    back = around(near_sum.astype(jnp.bfloat16), "blk", -1)
-    total = (own_sum + back.astype(jnp.float32)).astype(jnp.bfloat16)
+    got = [around(past_piece, "blk", -1)]
+    got += [sent_home(piece, k) for k, piece in zip(steps, sent)]
+    for term in got:
+        total = total + term.astype(jnp.float32)
+    total = total.astype(jnp.bfloat16)
     return (query_grad, total[:width].T, total[width:].T)
 
 

time: 24.2 us -> 27.1 us (1.12)
  waiting for transfers between devices: 7.58 us -> 12 us
  starting transfers between devices: 8.58 us -> 7.37 us
  Pallas kernels: 4.98 us -> 4.57 us
    ppermute x2 -> x3, waiting for transfers between devices: 4.83 us -> 9.78 us  [the longest x2 8.51 us: around(): return lax.ppermute(x, axis, pairs)]
    ppermute x5 -> x4, starting transfers between devices: 3.51 us -> 1.8 us  [exchanged(): return lax.ppermute(x, axis, [(i, i ^ step) for i in range(count)])]
    ppermute x2 -> x3, starting transfers between devices: 5.07 us -> 5.58 us  [the longest x2 4.29 us: around(): return lax.ppermute(x, axis, pairs)]
    ppermute x5 -> x4, waiting for transfers between devices: 2.75 us -> 2.26 us  [exchanged(): return lax.ppermute(x, axis, [(i, i ^ step) for i in range(count)])]
    pallas_call x1, Pallas kernels: 1.77 us -> 1.35 us  [per_device(): pl.pallas_call(own_body, out_shape=[low(2 * heads * rows, 2 * rows), slab...]
  transfers between devices with their start and end apart: 7 -> 7, of which waited for: 5 -> 5; matrix products, arithmetic and copies ran while one was open for 3% -> 2% of each run, Pallas kernels for 15% -> 12%
where the time goes in v5:
time: 27.1 us; the launch traced here: 26.7 us
  waiting for transfers between devices  12 us (44%)
  starting transfers between devices  7.37 us (27%)
  Pallas kernels  4.57 us (17%)
  other arithmetic  1.45 us (5%)
  between operations  0.68 us (3%)
  local copies, waits for them, and re-layouts  0.62 us (2%)
    ppermute x2, waiting for transfers between devices, around(): return lax.ppermute(x, axis, pairs)  8.51 us
    ppermute x2, starting transfers between devices, around(): return lax.ppermute(x, axis, pairs)  4.29 us
    ppermute x4, waiting for transfers between devices, exchanged(): return lax.ppermute(x, axis, [(i, i ^ step) for i in range(count)])  2.26 us
    ppermute x4, starting transfers between devices, exchanged(): return lax.ppermute(x, axis, [(i, i ^ step) for i in range(count)])  1.8 us
    pallas_call x1, Pallas kernels, per_device(): pl.pallas_call(front_body, out_shape=[low(rows, 2 * features), full(3 * h...  1.4 us
    pallas_call x1, Pallas kernels, per_device(): pl.pallas_call(own_body, out_shape=[low(2 * heads * rows, 2 * rows), slab...  1.35 us
    pallas_call x1, Pallas kernels, per_device(): pl.pallas_call(functools.partial(rest_body, steps), out_shape=[low(heads...  1.31 us
    ppermute x1, starting transfers between devices, sent_home(): return lax.ppermute(x, ('team', 'blk'), pairs)  1.29 us
  transfers between devices with their start and end apart: 7, of which 5 were waited for; matrix products, arithmetic and copies ran while one was open for 2% of the time, Pallas kernels for 12%

profile of v5, /device:TPU:0, one launch (start us, length us, event | category | flops | bytes accessed | tf_op | source)
XLA Modules:
  0.0 26.7 jit_solution(18366856434245894948)
XLA Ops:
  0.6 0.7 %pad_maximum_fusion.refs_4_.refs_0_ = bf16[128,128]{1,0:T(8,128)(2,1)S(1)} fusion(bf16[64,128]{1,0:T(8,128)(2,1)} %bitcast.7, bf16[64,128]{1,0:T(8,128)(2,1)} %bitcast.9), kind=kLoop, calls=%fused_computation.2 | loop fusion | flops 65536 | bytes 65536 | tf_op jit(solution)/shard_map/concatenate | solution.py:227
  1.4 3.0 %collective-permute-start.2 = (bf16[128,128]{1,0:T(8,128)(2,1)S(1)}, bf16[128,128]{1,0:T(8,128)(2,1)S(1)}, u32[]{:S(2)}, u32[]{:S(2)}) collective-permute-start(bf16[128,128]{1,0:T(8,128)(2,1)S(1)} %pad_maximum_fusion.refs_4_.refs_0_), channel_id=1, source_target_pairs={{0,1},{1,2},{2,3},{3,4},{4,5},{5,6},{6,7},{7,0},{8,9},{9,10},{10,1... | collective-permute-start | bytes 98312 | tf_op jit(solution)/shard_map/ppermute | solution.py:20
  4.4 0.0 copy-start
  4.4 0.0 copy-start.1
  4.4 1.4 %shard_map.94 = (bf16[128,1024]{1,0:T(8,128)(2,1)S(1)}, f32[24,128]{1,0:T(8,128)S(1)}) custom-call(bf16[128,512]{1,0:T(8,128)(2,1)} %q_in.1, bf16[128,512]{1,0:T(8,128)(2,1)} %g_in.1, bf16[128,512]{1,0:T(8,128)(2,1)} %o_ref.1, f32[8,128]{1,0:T(8,128)} %log_in.1, s32[1,128]{1,0:T(1,128)} %bitcast.11), custom_call_target="tpu_custom_call" | custom-call | tf_op jit(solution)/shard_map/pallas_call | solution.py:229
  5.8 0.0 collective-permute-start
  5.8 3.5 %collective-permute-done.2.refs_5_.refs_1_ = bf16[128,128]{1,0:T(8,128)(2,1)S(1)} collective-permute-done((bf16[128,128]{1,0:T(8,128)(2,1)S(1)}, bf16[128,128]{1,0:T(8,128)(2,1)S(1)}, u32[]{:S(2)}, u32[]{:S(2)}) %collective-permute-start.2) | collective-permute-done | bytes 32800 | tf_op jit(solution)/shard_map/ppermute | solution.py:20
  9.3 0.0 copy-done
  9.3 0.0 copy-done.1
  9.3 1.7 %collective-permute-start.3 = (bf16[128,128]{1,0:T(8,128)(2,1)S(1)}, bf16[128,128]{1,0:T(8,128)(2,1)S(1)}, u32[]{:S(2)}, u32[]{:S(2)}) collective-permute-start(bf16[128,128]{1,0:T(8,128)(2,1)S(1)} %broadcast_select_fusion), channel_id=1, source_target_pairs={{0,16},{8,24},{16,0},{24,8},{1,17},{9,25},{17,1},{25,9},{2,18},{10... | collective-permute-start | bytes 98312 | tf_op jit(solution)/shard_map/ppermute | solution.py:25
  11.0 0.0 collective-permute-start.1
  11.0 1.2 %collective-permute-done.1.refs_3_ = f32[24,128]{1,0:T(8,128)S(1)} collective-permute-done((f32[24,128]{1,0:T(8,128)S(1)}, f32[24,128]{1,0:T(8,128)S(1)}, u32[]{:S(2)}, u32[]{:S(2)}) %collective-permute-start.1) | collective-permute-done | bytes 12320 | tf_op jit(solution)/shard_map/ppermute | solution.py:25
  12.2 1.1 %collective-permute-done.3.refs_4_.refs_2_ = bf16[128,128]{1,0:T(8,128)(2,1)S(1)} collective-permute-done((bf16[128,128]{1,0:T(8,128)(2,1)S(1)}, bf16[128,128]{1,0:T(8,128)(2,1)S(1)}, u32[]{:S(2)}, u32[]{:S(2)}) %collective-permute-start.3) | collective-permute-done | bytes 32800 | tf_op jit(solution)/shard_map/ppermute | solution.py:25
  13.3 0.0 collective-permute-done.refs_1_
  13.3 1.3 %shard_map.96 = (bf16[1024,256]{1,0:T(8,128)(2,1)S(1)}, bf16[128,128]{1,0:T(8,128)(2,1)S(1)}) custom-call(bf16[128,1024]{1,0:T(8,128)(2,1)S(1)} %get-tuple-element.12.refs_0_, bf16[128,1024]{1,0:T(8,128)(2,1)S(1)} %collective-permute-done.refs_1_, f32[24,128]{1,0:T(8,128)S(1)} %get-tuple-element.13.refs_2_, f32[24,128]{1,0:T(8,128)S(1)} %collective-permute-done.1.refs_3_, ...), custom_call_target="tpu_custom_call" | custom-call | tf_op jit(solution)/shard_map/pallas_call | solution.py:260
  14.6 1.3 %collective-permute-start.6 = (bf16[128,128]{1,0:T(8,128)(2,1)S(1)}, bf16[128,128]{1,0:T(8,128)(2,1)S(1)}, u32[]{:S(2)}, u32[]{:S(2)}) collective-permute-start(bf16[128,128]{1,0:T(8,128)(2,1)S(1)} %get-tuple-element.20), channel_id=1, source_target_pairs={{1,16},{2,17},{3,18},{4,19},{5,20},{6,21},{7,22},{9,24},{10,25},{1... | collective-permute-start | bytes 98312 | tf_op jit(solution)/shard_map/ppermute | solution.py:37
  15.9 1.4 %shard_map.95 = (bf16[2048,256]{1,0:T(8,128)(2,1)S(1)}, f32[128,128]{1,0:T(8,128)S(1)}, bf16[128,128]{1,0:T(8,128)(2,1)S(1)}) custom-call(bf16[128,1024]{1,0:T(8,128)(2,1)S(1)} %get-tuple-element.12.refs_0_, bf16[128,1024]{1,0:T(8,128)(2,1)S(1)} %collective-permute-done.refs_1_, f32[24,128]{1,0:T(8,128)S(1)} %get-tuple-element.13.refs_2_, ...), custom_call_target="tpu_custom_call" | custom-call | tf_op jit(solution)/shard_map/pallas_call | solution.py:252
  17.3 1.3 %collective-permute-start.5 = (bf16[128,128]{1,0:T(8,128)(2,1)S(1)}, bf16[128,128]{1,0:T(8,128)(2,1)S(1)}, u32[]{:S(2)}, u32[]{:S(2)}) collective-permute-start(bf16[128,128]{1,0:T(8,128)(2,1)S(1)} %get-tuple-element.19), channel_id=1, source_target_pairs={{1,0},{2,1},{3,2},{4,3},{5,4},{6,5},{7,6},{9,8},{10,9},{11,10},{12... | collective-permute-start | bytes 98312 | tf_op jit(solution)/shard_map/ppermute | solution.py:20
  18.6 0.5 %shard_map.97 = (f32[128,512]{1,0:T(8,128)S(1)}, bf16[128,512]{1,0:T(8,128)(2,1)S(1)}) custom-call(bf16[2048,256]{1,0:T(8,128)(2,1)S(1)} %get-tuple-element.14.own_grad_ref, bf16[1024,256]{1,0:T(8,128)(2,1)S(1)} %get-tuple-element.15.near_grad_ref, bf16[128,128]{1,0:T(8,128)(2,1)S(1)} %pad_maximum_fusion.refs_4_.refs_0_, ...), custom_call_target="tpu_custom_call" | custom-call | tf_op jit(solution)/shard_map/pallas_call | solution.py:268
  19.1 0.1 collective-permute-start.4
  19.2 1.3 %collective-permute-done.6 = bf16[128,128]{1,0:T(8,128)(2,1)S(1)} collective-permute-done((bf16[128,128]{1,0:T(8,128)(2,1)S(1)}, bf16[128,128]{1,0:T(8,128)(2,1)S(1)}, u32[]{:S(2)}, u32[]{:S(2)}) %collective-permute-start.6) | collective-permute-done | bytes 32800 | tf_op jit(solution)/shard_map/ppermute | solution.py:37
  20.4 5.0 %collective-permute-done.5 = bf16[128,128]{1,0:T(8,128)(2,1)S(1)} collective-permute-done((bf16[128,128]{1,0:T(8,128)(2,1)S(1)}, bf16[128,128]{1,0:T(8,128)(2,1)S(1)}, u32[]{:S(2)}, u32[]{:S(2)}) %collective-permute-start.5) | collective-permute-done | bytes 32800 | tf_op jit(solution)/shard_map/ppermute | solution.py:20
  25.4 0.6 %slice_bitcast_fusion = (bf16[128,64]{0,1:T(8,128)(2,1)}, bf16[128,64]{0,1:T(8,128)(2,1)}) fusion(bf16[128,128]{1,0:T(8,128)(2,1)S(1)} %add_convert_fusion.1), kind=kLoop, calls=%fused_computation.4 | loop fusion | bytes 65536 | tf_op jit(solution)/shard_map/transpose | solution.py:282
  26.1 0.0 collective-permute-done.4
  26.1 0.7 %add_convert_fusion = bf16[128,512]{1,0:T(8,128)(2,1)} fusion(f32[128,512]{1,0:T(8,128)S(1)} %get-tuple-element.16, bf16[128,512]{1,0:T(8,128)(2,1)S(1)} %collective-permute-done.4), kind=kLoop, calls=%fused_computation | loop fusion | flops 196608 | bytes 524288 | tf_op jit(solution)/shard_map/convert_element_type | solution.py:276
  (2 shorter events, 0.0 us)
Async XLA Ops:
  1.4 7.9 %collective-permute-start.2 = (bf16[128,128]{1,0:T(8,128)(2,1)S(1)}, bf16[128,128]{1,0:T(8,128)(2,1)S(1)}, u32[]{:S(2)}, u32[]{:S(2)}) collective-permute-start(bf16[128,128]{1,0:T(8,128)(2,1)S(1)} %pad_maximum_fusion.refs_4_.refs_0_), channel_id=1, source_target_pairs={{0,1},{1,2},{2,3},{3,4},{4,5},{5,6},{6,7},{7,0},{8,9},{9,10},{10,1... | collective-permute-start | bytes 98312 | tf_op jit(solution)/shard_map/ppermute | solution.py:20
  4.4 4.9 %copy-start = (bf16[128,64]{0,1:T(8,128)(2,1)S(1)}, bf16[128,64]{0,1:T(8,128)(2,1)}, u32[]{:S(2)}) copy-start(bf16[128,64]{0,1:T(8,128)(2,1)} %param.9) | copy-start | bytes 49156
  4.4 4.9 %copy-start.1 = (bf16[128,64]{0,1:T(8,128)(2,1)S(1)}, bf16[128,64]{0,1:T(8,128)(2,1)}, u32[]{:S(2)}) copy-start(bf16[128,64]{0,1:T(8,128)(2,1)} %param.8) | copy-start | bytes 49156
  5.8 7.5 %collective-permute-start = (bf16[128,1024]{1,0:T(8,128)(2,1)S(1)}, bf16[128,1024]{1,0:T(8,128)(2,1)S(1)}, u32[]{:S(2)}, u32[]{:S(2)}) collective-permute-start(bf16[128,1024]{1,0:T(8,128)(2,1)S(1)} %get-tuple-element.12.refs_0_), channel_id=1, source_target_pairs={{0,8},{8,0},{16,24},{24,16},{1,9},{9,1},{17,25},{25,17},{2,10},{10... | collective-permute-start | bytes 786440 | tf_op jit(solution)/shard_map/ppermute | solution.py:25
  9.3 4.0 %collective-permute-start.3 = (bf16[128,128]{1,0:T(8,128)(2,1)S(1)}, bf16[128,128]{1,0:T(8,128)(2,1)S(1)}, u32[]{:S(2)}, u32[]{:S(2)}) collective-permute-start(bf16[128,128]{1,0:T(8,128)(2,1)S(1)} %broadcast_select_fusion), channel_id=1, source_target_pairs={{0,16},{8,24},{16,0},{24,8},{1,17},{9,25},{17,1},{25,9},{2,18},{10... | collective-permute-start | bytes 98312 | tf_op jit(solution)/shard_map/ppermute | solution.py:25
  11.0 1.2 %collective-permute-start.1 = (f32[24,128]{1,0:T(8,128)S(1)}, f32[24,128]{1,0:T(8,128)S(1)}, u32[]{:S(2)}, u32[]{:S(2)}) collective-permute-start(f32[24,128]{1,0:T(8,128)S(1)} %get-tuple-element.13.refs_2_), channel_id=1, source_target_pairs={{0,8},{8,0},{16,24},{24,16},{1,9},{9,1},{17,25},{25,17},{2,10},{10... | collective-permute-start | bytes 36872 | tf_op jit(solution)/shard_map/ppermute | solution.py:25
  14.6 5.8 %collective-permute-start.6 = (bf16[128,128]{1,0:T(8,128)(2,1)S(1)}, bf16[128,128]{1,0:T(8,128)(2,1)S(1)}, u32[]{:S(2)}, u32[]{:S(2)}) collective-permute-start(bf16[128,128]{1,0:T(8,128)(2,1)S(1)} %get-tuple-element.20), channel_id=1, source_target_pairs={{1,16},{2,17},{3,18},{4,19},{5,20},{6,21},{7,22},{9,24},{10,25},{1... | collective-permute-start | bytes 98312 | tf_op jit(solution)/shard_map/ppermute | solution.py:37
  17.3 8.2 %collective-permute-start.5 = (bf16[128,128]{1,0:T(8,128)(2,1)S(1)}, bf16[128,128]{1,0:T(8,128)(2,1)S(1)}, u32[]{:S(2)}, u32[]{:S(2)}) collective-permute-start(bf16[128,128]{1,0:T(8,128)(2,1)S(1)} %get-tuple-element.19), channel_id=1, source_target_pairs={{1,0},{2,1},{3,2},{4,3},{5,4},{6,5},{7,6},{9,8},{10,9},{11,10},{12... | collective-permute-start | bytes 98312 | tf_op jit(solution)/shard_map/ppermute | solution.py:20
  19.1 7.0 %collective-permute-start.4 = (bf16[128,512]{1,0:T(8,128)(2,1)S(1)}, bf16[128,512]{1,0:T(8,128)(2,1)S(1)}, u32[]{:S(2)}, u32[]{:S(2)}) collective-permute-start(bf16[128,512]{1,0:T(8,128)(2,1)S(1)} %get-tuple-element.17), channel_id=1, source_target_pairs={{0,8},{8,0},{16,24},{24,16},{1,9},{9,1},{17,25},{25,17},{2,10},{10... | collective-permute-start | bytes 393224 | tf_op jit(solution)/shard_map/ppermute | solution.py:25

commit v6 on v5

v6 whole, which is shorter than its diff:
```python
import functools
import math

import jax
import jax.numpy as jnp
from jax import lax
from jax.experimental import pallas as pl
from jax.experimental.pallas import tpu as pltpu
from jax.sharding import PartitionSpec as P


NT = (((1,), (1,)), ((), ()))
NN = (((1,), (0,)), ((), ()))
FRONT = 2


def around(x, axis, by):
    count = lax.axis_size(axis)
    pairs = [(i, (i + by) % count) for i in range(count) if by > 0 or i + by >= 0]
    return lax.ppermute(x, axis, pairs)


def exchanged(x, axis, step):
    count = lax.axis_size(axis)
    return lax.ppermute(x, axis, [(i, i ^ step) for i in range(count)])


def skewed(x, step, out):
    team, blk = lax.axis_size("team"), lax.axis_size("blk")
    pairs = []
    for t in range(team):
        slot = t ^ step
        for b in range(blk):
            ahead = b + 1 if slot < t else b
            if ahead < blk:
                pairs.append((t * blk + b, slot * blk + ahead))
    if not out:
        pairs = [(there, here) for here, there in pairs]
    return lax.ppermute(x, ("team", "blk"), pairs)


def dot(a, b, dims):
    return lax.dot_general(a, b, dims, preferred_element_type=jnp.float32)


def half_turn(x, width):
    return jnp.concatenate([x[:, width:], x[:, :width]], 1)


def in_parts(x):
    high = x.astype(jnp.bfloat16).astype(jnp.float32)
    middle = (x - high).astype(jnp.bfloat16).astype(jnp.float32)
    return [high, middle, x - high - middle]


def front_body(q_in, g_in, o_ref, log_in, begin_in, k_in, v_in, mine_ref, rows_ref):
    rows, features = q_in.shape
    heads = log_in.shape[0]
    width = features // heads
    lanes = 2 * width
    mine_ref[:width, :] = k_in[...]
    mine_ref[width:, :] = v_in[...]
    for n, ref in enumerate((q_in, g_in)):
        for pair in range(heads // 2):
            at = (n * (heads // 2) + pair) * rows
            rows_ref[at : at + rows, :] = ref[:, pair * lanes : (pair + 1) * lanes]
    prod = g_in[...].astype(jnp.float32) * o_ref[...].astype(jnp.float32)
    feature = lax.broadcasted_iota(jnp.int32, (heads, features), 1)
    head_of = lax.broadcasted_iota(jnp.int32, (heads, features), 0)
    pick = (feature // width == head_of).astype(jnp.float32)
    delta = lax.dot_general(
        pick, prod, NT, precision=lax.Precision.HIGHEST, preferred_element_type=jnp.float32
    )
    begin = jnp.broadcast_to(begin_in[...], (heads, rows))
    begins = [(begin >> 8).astype(jnp.float32), (begin & 255).astype(jnp.float32)]
    parts = in_parts(log_in[...]) + in_parts(delta) + begins
    rows_ref[heads * rows :, :] = jnp.concatenate(parts, 0).astype(jnp.bfloat16)


def tile_terms(slab_refs, bases, front, grad_ref):
    lanes, rows = slab_refs[0].shape
    width = lanes // 2
    heads = front[0].shape[0] // (rows + 8)
    total = len(slab_refs) * rows
    spot = lax.axis_index("team")
    first_row = (lax.axis_index("blk") * lax.axis_size("team") + spot) * rows
    aux = [ref[heads * rows :, :].astype(jnp.float32) for ref in front]

    def of_rows(*parts):
        both = []
        for one in aux:
            both.append(sum(one[part * heads : (part + 1) * heads, :] for part in parts))
        return jnp.concatenate(both, 1)

    def pair_rows(number):
        return jnp.concatenate([ref[number * rows : (number + 1) * rows, :] for ref in front], 0)

    log_norm = of_rows(0, 1, 2)
    delta = of_rows(3, 4, 5)
    begin = of_rows(6)[:1].astype(jnp.int32) * 256 + of_rows(7)[:1].astype(jnp.int32) - first_row
    kv = jnp.concatenate([ref[...] for ref in slab_refs], 1).T
    low_key = lax.broadcasted_iota(jnp.int32, (total, lanes), 1) < width
    none = jnp.zeros_like(kv)
    k_low = jnp.where(low_key, kv * jnp.asarray(1.0 / math.sqrt(width), kv.dtype), none)
    v_high = jnp.where(low_key, none, kv)
    key_halves = (k_low, half_turn(k_low, width))
    value_halves = (half_turn(v_high, width), v_high)
    inside = lax.broadcasted_iota(jnp.int32, (rows, 2 * rows), 0)
    key_pos = jnp.concatenate([inside + base for base in bases], 0)
    lane = lax.broadcasted_iota(jnp.int32, (1, 2 * rows), 1)
    row_pos = jnp.where(lane < rows, lane, lane + ((spot ^ 1) - spot - 1) * rows)
    allowed = (key_pos >= begin) & (key_pos <= row_pos)
    queries, cotangents, probs, grads = [], [], ([], []), ([], [])
    for pair in range(heads // 2):
        q_pair = pair_rows(pair)
        g_pair = pair_rows(heads // 2 + pair)
        queries.append(q_pair)
        cotangents.append(g_pair)
        for half in range(2):
            head = 2 * pair + half
            scores = dot(key_halves[half], q_pair, NT)
            shifted = scores - log_norm[head : head + 1, :]
            weights = jnp.exp(jnp.where(allowed, shifted, -jnp.inf))
            prob_grad = dot(value_halves[half], g_pair, NT)
            score_grad = weights * (prob_grad - delta[head : head + 1, :])
            low = score_grad.astype(jnp.bfloat16)
            grad_ref[head * total : (head + 1) * total, :] = low
            probs[half].append(weights.astype(jnp.bfloat16))
            grads[half].append(low)

    def summed(terms, rights):
        both = jnp.concatenate([jnp.concatenate(terms[half], 1) for half in range(2)], 0)
        both = dot(both, jnp.concatenate(rights, 0), NN)
        return both[:total], both[total:]

    key_even, key_odd = summed(grads, queries)
    value_even, value_odd = summed(probs, cotangents)
    factor = jnp.float32(1.0 / math.sqrt(width))
    low_key = lax.broadcasted_iota(jnp.int32, (total, lanes), 1) < width
    straight = jnp.where(low_key, key_even * factor, value_odd)
    turned = half_turn(jnp.where(low_key, value_even, key_odd * factor), width)
    return straight + turned


def slab_of(terms, number, rows):
    return terms[number * rows : (number + 1) * rows, :].T


def own_body(*refs):
    front, slab_ref, grad_ref, own_ref = refs[:FRONT], refs[FRONT], refs[-2], refs[-1]
    terms = tile_terms([slab_ref], [0], front, grad_ref)
    own_ref[...] = slab_of(terms, 0, slab_ref.shape[1])


def past_body(*refs):
    front, slab_ref, grad_ref, piece_ref = refs[:FRONT], refs[FRONT], refs[-2], refs[-1]
    rows = slab_ref.shape[1]
    has_past = lax.axis_index("blk") > 0

    @pl.when(has_past)
    def _():
        terms = tile_terms([slab_ref], [-lax.axis_size("team") * rows], front, grad_ref)
        piece_ref[...] = slab_of(terms, 0, rows).astype(jnp.bfloat16)

    @pl.when(jnp.logical_not(has_past))
    def _():
        grad_ref[...] = jnp.zeros_like(grad_ref)
        piece_ref[...] = jnp.zeros_like(piece_ref)


def rest_body(steps, *refs):
    count = len(steps)
    front, slab_refs = refs[:FRONT], refs[FRONT : FRONT + count]
    grad_ref, *piece_refs = refs[FRONT + count :]
    _, rows = slab_refs[0].shape
    spot = lax.axis_index("team")
    block = lax.axis_size("team")
    bases = []
    for step in steps:
        slot = spot ^ step
        bases.append((slot - spot - jnp.where(slot > spot, block, 0)) * rows)
    terms = tile_terms(slab_refs, bases, front, grad_ref)
    for n, piece_ref in enumerate(piece_refs):
        part = slab_of(terms, n, rows)
        piece_ref[...] = part.astype(jnp.bfloat16)


def query_body(count, *refs):
    grad_refs, slab_refs, (mine_ref, other_ref) = refs[:3], refs[3 : 3 + count], refs[3 + count :]
    lanes, rows = slab_refs[0].shape
    width = lanes // 2
    heads = mine_ref.shape[1] // width
    small = jnp.asarray(1.0 / math.sqrt(width), slab_refs[0].dtype)
    groups = (slab_refs[:1], slab_refs[1:2], slab_refs[2:])
    keys = [jnp.concatenate([ref[:width, :] for ref in some], 1) * small for some in groups]

    def flipped(head):
        terms = 0.0
        for some, grads in zip(keys, grad_refs):
            total = some.shape[1]
            terms += dot(some, grads[head * total : (head + 1) * total, :], NN)
        return terms

    for pair in range(heads // 2):
        both = jnp.concatenate([flipped(2 * pair), flipped(2 * pair + 1)], 0)
        span = slice(pair * lanes, (pair + 1) * lanes)
        mine_ref[:, span] = both[:, :rows].T
        other_ref[:, span] = both[:, rows:].T.astype(jnp.bfloat16)


def in_vmem(count):
    return [pl.BlockSpec(memory_space=pltpu.VMEM) for _ in range(count)]


def held(*arrays, space=pltpu.VMEM):
    return [pltpu.with_memory_space_constraint(x, space) for x in arrays]


def grant(slabs, rows, lanes):
    return pltpu.CompilerParams(vmem_limit_bytes=(8 << 20) + 192 * slabs * rows * lanes)


def per_device(queries, keys, values, attn_out, out_grad, log_norm, doc_start):
    rows, features = queries.shape
    heads = log_norm.shape[0]
    width = keys.shape[1]
    lanes = 2 * width
    half = lax.axis_size("team") // 2
    steps = [2 * n for n in range(1, half)]

    def low(*dims):
        return pltpu.VMEM(dims, jnp.bfloat16)

    def full(*dims):
        return pltpu.VMEM(dims, jnp.float32)

    params = grant(max(2, half), rows, lanes)
    mine, own_rows = pl.pallas_call(
        front_body,
        out_shape=[low(lanes, rows), low(heads * (rows + 8), lanes)],
        in_specs=in_vmem(7),
        out_specs=in_vmem(2),
        compiler_params=params,
    )(
        *held(
            queries,
            out_grad,
            attn_out,
            log_norm,
            doc_start.reshape(1, rows),
            keys.T,
            values.T,
            space=pltpu.HBM,
        )
    )
    past = around(mine, "blk", 1)
    front = (own_rows, exchanged(own_rows, "team", 1))
    seen = [skewed(mine, k, True) for k in steps]
    own_grads, total = pl.pallas_call(
        own_body,
        out_shape=[low(heads * rows, 2 * rows), full(lanes, rows)],
        in_specs=in_vmem(FRONT + 1),
        out_specs=in_vmem(2),
        compiler_params=params,
    )(*held(*front, mine))
    past_grads, past_piece = pl.pallas_call(
        past_body,
        out_shape=[low(heads * rows, 2 * rows), low(lanes, rows)],
        in_specs=in_vmem(FRONT + 1),
        out_specs=in_vmem(2),
        compiler_params=params,
    )(*held(*front, past))
    rest_grads, *sent = pl.pallas_call(
        functools.partial(rest_body, steps),
        out_shape=[low(heads * (half - 1) * rows, 2 * rows)] + [low(lanes, rows)] * (half - 1),
        in_specs=in_vmem(FRONT + half - 1),
        out_specs=in_vmem(half),
        compiler_params=params,
    )(*held(*front, *seen))
    query_mine, query_other = pl.pallas_call(
        functools.partial(query_body, 1 + half),
        out_shape=[full(rows, features), low(rows, features)],
        in_specs=in_vmem(4 + half),
        out_specs=in_vmem(2),
        compiler_params=params,
    )(*held(own_grads, past_grads, rest_grads, mine, past, *seen))
    query_back = exchanged(query_other, "team", 1)
    query_grad = (query_mine + query_back.astype(jnp.float32)).astype(jnp.bfloat16)
    got = [around(past_piece, "blk", -1)]
    got += [skewed(piece, k, False) for k, piece in zip(steps, sent)]
    for term in got:
        total = total + term.astype(jnp.float32)
    total = total.astype(jnp.bfloat16)
    return (query_grad, total[:width].T, total[width:].T)


def solution(mesh):
    row = P(("blk", "team"), None)

    return jax.shard_map(
        per_device,
        mesh=mesh,
        in_specs=(row, row, row, row, row, P(None, ("blk", "team")), P(("blk", "team"))),
        out_specs=(row, row, row),
        check_vma=False,
    )
```

time: 27.1 us -> 21.6 us (0.80)
  waiting for transfers between devices: 12 us -> 6.32 us
  starting transfers between devices: 7.37 us -> 9.14 us
  Pallas kernels: 4.57 us -> 3.78 us
  other arithmetic: 1.45 us -> 0.7 us
    ppermute x1 -> x2, starting transfers between devices: 1.29 us -> 5.69 us  [skewed(): return lax.ppermute(x, ('team', 'blk'), pairs)]
    ppermute x4 -> x2, waiting for transfers between devices: 2.26 us -> 0.01 us  [exchanged(): return lax.ppermute(x, axis, [(i, i ^ step) for i in range(count)])]
    ppermute x2, waiting for transfers between devices: 8.51 us -> 6.3 us  [around(): return lax.ppermute(x, axis, pairs)]
    ppermute x2, starting transfers between devices: 4.29 us -> 2.87 us  [around(): return lax.ppermute(x, axis, pairs)]
    ppermute x1 -> x2, waiting for transfers between devices: 1.27 us -> 0.01 us  [skewed(): return lax.ppermute(x, ('team', 'blk'), pairs)]
    ppermute x4 -> x2, starting transfers between devices: 1.8 us -> 0.58 us  [exchanged(): return lax.ppermute(x, axis, [(i, i ^ step) for i in range(count)])]
    concatenate x1 -> x0, other arithmetic: 0.74 us -> none  [per_device(): mine = jnp.concatenate([keys.T, values.T], 0)]
    pallas_call x1, Pallas kernels: 1.31 us -> 0.91 us  [per_device(): pl.pallas_call(functools.partial(rest_body, steps), out_shape=[low(heads...]
  transfers between devices with their start and end apart: 7 -> 6, of which waited for: 5 -> 2; matrix products, arithmetic and copies ran while one was open for 2% -> 3% of each run, Pallas kernels for 12% -> 11%
where the time goes in v6:
time: 21.6 us; the launch traced here: 21.2 us
  starting transfers between devices  9.14 us (42%)
  waiting for transfers between devices  6.32 us (29%)
  Pallas kernels  3.78 us (18%)
  other arithmetic  0.7 us (3%)
  between operations  0.7 us (3%)
  local copies, waits for them, and re-layouts  0.61 us (3%)
    ppermute x2, waiting for transfers between devices, around(): return lax.ppermute(x, axis, pairs)  6.3 us
    ppermute x2, starting transfers between devices, skewed(): return lax.ppermute(x, ('team', 'blk'), pairs)  5.69 us
    ppermute x2, starting transfers between devices, around(): return lax.ppermute(x, axis, pairs)  2.87 us
    pallas_call x1, Pallas kernels, per_device(): pl.pallas_call(front_body, out_shape=[low(lanes, rows), low(heads * (rows...  1.45 us
    pallas_call x1, Pallas kernels, per_device(): pl.pallas_call(own_body, out_shape=[low(heads * rows, 2 * rows), full(lan...  0.93 us
    pallas_call x1, Pallas kernels, per_device(): pl.pallas_call(functools.partial(rest_body, steps), out_shape=[low(heads...  0.91 us
    convert_element_type x1, other arithmetic, per_device(): (query_mine + query_back.astype(jnp.float32)).astype(jnp.bfloat16)  0.68 us
    transpose x1, local copies, waits for them, and re-layouts, per_device(): return (query_grad, total[:width].T, total[width:].T)  0.61 us
  transfers between devices with their start and end apart: 6, of which 2 were waited for; matrix products, arithmetic and copies ran while one was open for 3% of the time, Pallas kernels for 11%

profile of v6, /device:TPU:0, one launch (start us, length us, event | category | flops | bytes accessed | tf_op | source)
XLA Modules:
  0.0 21.2 jit_solution(16276832893751651174)
XLA Ops:
  0.6 1.4 %shard_map.94 = (bf16[128,128]{1,0:T(8,128)(2,1)S(1)}, bf16[1088,128]{1,0:T(8,128)(2,1)S(1)}) custom-call(bf16[128,512]{1,0:T(8,128)(2,1)} %q_in.1, bf16[128,512]{1,0:T(8,128)(2,1)} %g_in.1, bf16[128,512]{1,0:T(8,128)(2,1)} %o_ref.1, f32[8,128]{1,0:T(8,128)} %log_in.1, s32[1,128]{1,0:T(1,128)} %bitcast.9, bf16[64,128]{1,0:T(8,128)(2,1)} %bitcast.7, ...), custom_call_target="tpu_custom_call" | custom-call | tf_op jit(solution)/shard_map/pallas_call | solution.py:238
  2.1 0.5 %collective-permute-start = (bf16[1088,128]{1,0:T(8,128)(2,1)S(1)}, bf16[1088,128]{1,0:T(8,128)(2,1)S(1)}, u32[]{:S(2)}, u32[]{:S(2)}) collective-permute-start(bf16[1088,128]{1,0:T(8,128)(2,1)S(1)} %get-tuple-element.13.refs_0_), channel_id=1, source_target_pairs={{0,8},{8,0},{16,24},{24,16},{1,9},{9,1},{17,25},{25,17},{2,10},{10... | collective-permute-start | bytes 835592 | tf_op jit(solution)/shard_map/ppermute | solution.py:25
  2.6 4.4 %collective-permute-start.2 = (bf16[128,128]{1,0:T(8,128)(2,1)S(1)}, bf16[128,128]{1,0:T(8,128)(2,1)S(1)}, u32[]{:S(2)}, u32[]{:S(2)}) collective-permute-start(bf16[128,128]{1,0:T(8,128)(2,1)S(1)} %get-tuple-element.14.refs_2_.refs_3_), channel_id=1, source_target_pairs={{0,16},{1,17},{2,18},{3,19},{4,20},{5,21},{6,22},{7,23},{8,24},{9,... | collective-permute-start | bytes 98312 | tf_op jit(solution)/shard_map/ppermute | solution.py:39
  7.0 1.6 %collective-permute-start.1 = (bf16[128,128]{1,0:T(8,128)(2,1)S(1)}, bf16[128,128]{1,0:T(8,128)(2,1)S(1)}, u32[]{:S(2)}, u32[]{:S(2)}) collective-permute-start(bf16[128,128]{1,0:T(8,128)(2,1)S(1)} %get-tuple-element.14.refs_2_.refs_3_), channel_id=1, source_target_pairs={{0,1},{1,2},{2,3},{3,4},{4,5},{5,6},{6,7},{7,0},{8,9},{9,10},{10,1... | collective-permute-start | bytes 98312 | tf_op jit(solution)/shard_map/ppermute | solution.py:20
  8.6 0.0 collective-permute-done.2.refs_2_.refs_5_
  8.6 0.0 collective-permute-done.refs_1_
  8.6 0.9 %shard_map.97 = (bf16[1024,256]{1,0:T(8,128)(2,1)S(1)}, bf16[128,128]{1,0:T(8,128)(2,1)S(1)}) custom-call(bf16[1088,128]{1,0:T(8,128)(2,1)S(1)} %get-tuple-element.13.refs_0_, bf16[1088,128]{1,0:T(8,128)(2,1)S(1)} %collective-permute-done.refs_1_, bf16[128,128]{1,0:T(8,128)(2,1)S(1)} %collective-permute-done.2.refs_2_.refs_5_), custom_call_target="tpu_custom_call" | custom-call | tf_op jit(solution)/shard_map/pallas_call | solution.py:273
  9.5 1.3 %collective-permute-start.5 = (bf16[128,128]{1,0:T(8,128)(2,1)S(1)}, bf16[128,128]{1,0:T(8,128)(2,1)S(1)}, u32[]{:S(2)}, u32[]{:S(2)}) collective-permute-start(bf16[128,128]{1,0:T(8,128)(2,1)S(1)} %get-tuple-element.22), channel_id=1, source_target_pairs={{16,0},{17,1},{18,2},{19,3},{20,4},{21,5},{22,6},{23,7},{24,8},{25... | collective-permute-start | bytes 98312 | tf_op jit(solution)/shard_map/ppermute | solution.py:39
  10.8 2.9 %collective-permute-done.1.refs_2_.refs_4_ = bf16[128,128]{1,0:T(8,128)(2,1)S(1)} collective-permute-done((bf16[128,128]{1,0:T(8,128)(2,1)S(1)}, bf16[128,128]{1,0:T(8,128)(2,1)S(1)}, u32[]{:S(2)}, u32[]{:S(2)}) %collective-permute-start.1) | collective-permute-done | bytes 32800 | tf_op jit(solution)/shard_map/ppermute | solution.py:20
  13.7 1.3 %collective-permute-start.4 = (bf16[128,128]{1,0:T(8,128)(2,1)S(1)}, bf16[128,128]{1,0:T(8,128)(2,1)S(1)}, u32[]{:S(2)}, u32[]{:S(2)}) collective-permute-start(bf16[128,128]{1,0:T(8,128)(2,1)S(1)} %get-tuple-element.21), channel_id=1, source_target_pairs={{1,0},{2,1},{3,2},{4,3},{5,4},{6,5},{7,6},{9,8},{10,9},{11,10},{12... | collective-permute-start | bytes 98312 | tf_op jit(solution)/shard_map/ppermute | solution.py:20
  15.0 0.9 %shard_map.95 = (bf16[1024,256]{1,0:T(8,128)(2,1)S(1)}, f32[128,128]{1,0:T(8,128)S(1)}) custom-call(bf16[1088,128]{1,0:T(8,128)(2,1)S(1)} %get-tuple-element.13.refs_0_, bf16[1088,128]{1,0:T(8,128)(2,1)S(1)} %collective-permute-done.refs_1_, bf16[128,128]{1,0:T(8,128)(2,1)S(1)} %get-tuple-element.14.refs_2_.refs_3_), custom_call_target="tpu_custom_call" | custom-call | tf_op jit(solution)/shard_map/pallas_call | solution.py:259
  15.9 0.5 %shard_map.98 = (f32[128,512]{1,0:T(8,128)S(1)}, bf16[128,512]{1,0:T(8,128)(2,1)S(1)}) custom-call(bf16[1024,256]{1,0:T(8,128)(2,1)S(1)} %get-tuple-element.15.refs_0_, bf16[1024,256]{1,0:T(8,128)(2,1)S(1)} %get-tuple-element.16.refs_1_, bf16[1024,256]{1,0:T(8,128)(2,1)S(1)} %get-tuple-element.17.refs_2_, ...), custom_call_target="tpu_custom_call" | custom-call | tf_op jit(solution)/shard_map/pallas_call | solution.py:280
  16.4 0.1 collective-permute-start.3
  16.5 0.0 collective-permute-done.5
  16.5 3.4 %collective-permute-done.4 = bf16[128,128]{1,0:T(8,128)(2,1)S(1)} collective-permute-done((bf16[128,128]{1,0:T(8,128)(2,1)S(1)}, bf16[128,128]{1,0:T(8,128)(2,1)S(1)}, u32[]{:S(2)}, u32[]{:S(2)}) %collective-permute-start.4) | collective-permute-done | bytes 32800 | tf_op jit(solution)/shard_map/ppermute | solution.py:20
  19.9 0.6 %slice_bitcast_fusion = (bf16[128,64]{0,1:T(8,128)(2,1)}, bf16[128,64]{0,1:T(8,128)(2,1)}) fusion(bf16[128,128]{1,0:T(8,128)(2,1)S(1)} %add_convert_fusion.1), kind=kLoop, calls=%fused_computation.2 | loop fusion | bytes 65536 | tf_op jit(solution)/shard_map/transpose | solution.py:294
  20.6 0.0 collective-permute-done.3
  20.6 0.7 %add_convert_fusion = bf16[128,512]{1,0:T(8,128)(2,1)} fusion(f32[128,512]{1,0:T(8,128)S(1)} %get-tuple-element.18, bf16[128,512]{1,0:T(8,128)(2,1)S(1)} %collective-permute-done.3), kind=kLoop, calls=%fused_computation | loop fusion | flops 196608 | bytes 524288 | tf_op jit(solution)/shard_map/convert_element_type | solution.py:288
  (2 shorter events, 0.1 us)
Async XLA Ops:
  2.1 6.5 %collective-permute-start = (bf16[1088,128]{1,0:T(8,128)(2,1)S(1)}, bf16[1088,128]{1,0:T(8,128)(2,1)S(1)}, u32[]{:S(2)}, u32[]{:S(2)}) collective-permute-start(bf16[1088,128]{1,0:T(8,128)(2,1)S(1)} %get-tuple-element.13.refs_0_), channel_id=1, source_target_pairs={{0,8},{8,0},{16,24},{24,16},{1,9},{9,1},{17,25},{25,17},{2,10},{10... | collective-permute-start | bytes 835592 | tf_op jit(solution)/shard_map/ppermute | solution.py:25
  2.6 6.0 %collective-permute-start.2 = (bf16[128,128]{1,0:T(8,128)(2,1)S(1)}, bf16[128,128]{1,0:T(8,128)(2,1)S(1)}, u32[]{:S(2)}, u32[]{:S(2)}) collective-permute-start(bf16[128,128]{1,0:T(8,128)(2,1)S(1)} %get-tuple-element.14.refs_2_.refs_3_), channel_id=1, source_target_pairs={{0,16},{1,17},{2,18},{3,19},{4,20},{5,21},{6,22},{7,23},{8,24},{9,... | collective-permute-start | bytes 98312 | tf_op jit(solution)/shard_map/ppermute | solution.py:39
  7.0 6.7 %collective-permute-start.1 = (bf16[128,128]{1,0:T(8,128)(2,1)S(1)}, bf16[128,128]{1,0:T(8,128)(2,1)S(1)}, u32[]{:S(2)}, u32[]{:S(2)}) collective-permute-start(bf16[128,128]{1,0:T(8,128)(2,1)S(1)} %get-tuple-element.14.refs_2_.refs_3_), channel_id=1, source_target_pairs={{0,1},{1,2},{2,3},{3,4},{4,5},{5,6},{6,7},{7,0},{8,9},{9,10},{10,1... | collective-permute-start | bytes 98312 | tf_op jit(solution)/shard_map/ppermute | solution.py:20
  9.5 7.0 %collective-permute-start.5 = (bf16[128,128]{1,0:T(8,128)(2,1)S(1)}, bf16[128,128]{1,0:T(8,128)(2,1)S(1)}, u32[]{:S(2)}, u32[]{:S(2)}) collective-permute-start(bf16[128,128]{1,0:T(8,128)(2,1)S(1)} %get-tuple-element.22), channel_id=1, source_target_pairs={{16,0},{17,1},{18,2},{19,3},{20,4},{21,5},{22,6},{23,7},{24,8},{25... | collective-permute-start | bytes 98312 | tf_op jit(solution)/shard_map/ppermute | solution.py:39
  13.7 6.2 %collective-permute-start.4 = (bf16[128,128]{1,0:T(8,128)(2,1)S(1)}, bf16[128,128]{1,0:T(8,128)(2,1)S(1)}, u32[]{:S(2)}, u32[]{:S(2)}) collective-permute-start(bf16[128,128]{1,0:T(8,128)(2,1)S(1)} %get-tuple-element.21), channel_id=1, source_target_pairs={{1,0},{2,1},{3,2},{4,3},{5,4},{6,5},{7,6},{9,8},{10,9},{11,10},{12... | collective-permute-start | bytes 98312 | tf_op jit(solution)/shard_map/ppermute | solution.py:20
  16.4 4.2 %collective-permute-start.3 = (bf16[128,512]{1,0:T(8,128)(2,1)S(1)}, bf16[128,512]{1,0:T(8,128)(2,1)S(1)}, u32[]{:S(2)}, u32[]{:S(2)}) collective-permute-start(bf16[128,512]{1,0:T(8,128)(2,1)S(1)} %get-tuple-element.19), channel_id=1, source_target_pairs={{0,8},{8,0},{16,24},{24,16},{1,9},{9,1},{17,25},{25,17},{2,10},{10... | collective-permute-start | bytes 393224 | tf_op jit(solution)/shard_map/ppermute | solution.py:25

commit v7 on v6

--- a/solution.py
+++ b/solution.py
@@ -53,27 +53,46 @@
     return [high, middle, x - high - middle]
 
 
-def front_body(q_in, g_in, o_ref, log_in, begin_in, k_in, v_in, mine_ref, rows_ref):
+def load_body(q_in, g_in, o_in, log_in, begin_in, k_in, v_in, *refs):
+    mine_ref, rows_ref, o_ref, log_ref, begin_ref, sems = refs
     rows, features = q_in.shape
-    heads = log_in.shape[0]
-    width = features // heads
-    lanes = 2 * width
-    mine_ref[:width, :] = k_in[...]
-    mine_ref[width:, :] = v_in[...]
-    for n, ref in enumerate((q_in, g_in)):
-        for pair in range(heads // 2):
-            at = (n * (heads // 2) + pair) * rows
-            rows_ref[at : at + rows, :] = ref[:, pair * lanes : (pair + 1) * lanes]
-    prod = g_in[...].astype(jnp.float32) * o_ref[...].astype(jnp.float32)
-    feature = lax.broadcasted_iota(jnp.int32, (heads, features), 1)
-    head_of = lax.broadcasted_iota(jnp.int32, (heads, features), 0)
+    width, lanes = k_in.shape[0], rows_ref.shape[1]
+    moves = [
+        (k_in, mine_ref.at[:width, :]),
+        (v_in, mine_ref.at[width:, :]),
+        (o_in, o_ref),
+        (log_in, log_ref),
+        (begin_in, begin_ref),
+    ]
+    for n, source in enumerate((q_in, g_in)):
+        for pair in range(features // lanes):
+            at = n * (features // lanes) + pair
+            target = rows_ref.at[at * rows : (at + 1) * rows, :]
+            moves.append((source.at[:, pair * lanes : (pair + 1) * lanes], target))
+    copies = [pltpu.make_async_copy(x, y, sems.at[n]) for n, (x, y) in enumerate(moves)]
+    for copy in copies:
+        copy.start()
+    for copy in copies:
+        copy.wait()
+
+
+def front_body(rows_in, o_ref, log_ref, begin_ref, rows_ref):
+    heads, rows = log_ref.shape
+    pairs, lanes = heads // 2, rows_in.shape[1]
+    width = lanes // 2
+    first = pairs * rows
+    cotangents = [rows_in[first + n * rows : first + (n + 1) * rows, :] for n in range(pairs)]
+    cotangents = jnp.concatenate(cotangents, 1).astype(jnp.float32)
+    prod = cotangents * o_ref[...].astype(jnp.float32)
+    feature = lax.broadcasted_iota(jnp.int32, (heads, heads * width), 1)
+    head_of = lax.broadcasted_iota(jnp.int32, (heads, heads * width), 0)
     pick = (feature // width == head_of).astype(jnp.float32)
     delta = lax.dot_general(
         pick, prod, NT, precision=lax.Precision.HIGHEST, preferred_element_type=jnp.float32
     )
-    begin = jnp.broadcast_to(begin_in[...], (heads, rows))
+    begin = jnp.broadcast_to(begin_ref[...], (heads, rows))
     begins = [(begin >> 8).astype(jnp.float32), (begin & 255).astype(jnp.float32)]
-    parts = in_parts(log_in[...]) + in_parts(delta) + begins
+    parts = in_parts(log_ref[...]) + in_parts(delta) + begins
     rows_ref[heads * rows :, :] = jnp.concatenate(parts, 0).astype(jnp.bfloat16)
 
 
@@ -235,11 +254,18 @@
         return pltpu.VMEM(dims, jnp.float32)
 
     params = grant(max(2, half), rows, lanes)
-    mine, own_rows = pl.pallas_call(
-        front_body,
-        out_shape=[low(lanes, rows), low(heads * (rows + 8), lanes)],
-        in_specs=in_vmem(7),
-        out_specs=in_vmem(2),
+    mine, loaded, loaded_out, loaded_log, loaded_begin = pl.pallas_call(
+        load_body,
+        out_shape=[
+            low(lanes, rows),
+            low(heads * (rows + 8), lanes),
+            low(rows, features),
+            full(heads, rows),
+            pltpu.VMEM((1, rows), jnp.int32),
+        ],
+        in_specs=[pl.BlockSpec(memory_space=pltpu.HBM)] * 7,
+        out_specs=in_vmem(5),
+        scratch_shapes=[pltpu.SemaphoreType.DMA((heads + 5,))],
         compiler_params=params,
     )(
         *held(
@@ -254,6 +280,14 @@
         )
     )
     past = around(mine, "blk", 1)
+    own_rows = pl.pallas_call(
+        front_body,
+        out_shape=low(heads * (rows + 8), lanes),
+        in_specs=in_vmem(4),
+        out_specs=in_vmem(1)[0],
+        input_output_aliases={0: 0},
+        compiler_params=params,
+    )(*held(loaded, loaded_out, loaded_log, loaded_begin))
     front = (own_rows, exchanged(own_rows, "team", 1))
     seen = [skewed(mine, k, True) for k in steps]
     own_grads, total = pl.pallas_call(

time: 21.6 us -> 21.7 us (level)
  the two profiles are of different devices: /device:TPU:0 before, /device:TPU:26 now
where the time goes in v7:
time: 21.7 us; the launch traced here: 21.4 us
  starting transfers between devices  10.3 us (47%)
  Pallas kernels  4.67 us (22%)
  waiting for transfers between devices  4.45 us (21%)
  between operations  0.73 us (3%)
  other arithmetic  0.7 us (3%)
  local copies, waits for them, and re-layouts  0.61 us (3%)
    ppermute x2, starting transfers between devices, skewed(): return lax.ppermute(x, ('team', 'blk'), pairs)  7.92 us
    ppermute x2, waiting for transfers between devices, skewed(): return lax.ppermute(x, ('team', 'blk'), pairs)  2.34 us
    ppermute x2, starting transfers between devices, around(): return lax.ppermute(x, axis, pairs)  2.28 us
    ppermute x2, waiting for transfers between devices, around(): return lax.ppermute(x, axis, pairs)  2.1 us
    pallas_call x1, Pallas kernels, per_device(): pl.pallas_call(load_body, out_shape=[low(lanes, rows), low(heads * (rows...  1.12 us
    pallas_call x1, Pallas kernels, per_device(): pl.pallas_call(past_body, out_shape=[low(heads * rows, 2 * rows), low(lan...  0.93 us
    pallas_call x1, Pallas kernels, per_device(): pl.pallas_call(own_body, out_shape=[low(heads * rows, 2 * rows), full(lan...  0.92 us
    pallas_call x1, Pallas kernels, per_device(): pl.pallas_call(functools.partial(rest_body, steps), out_shape=[low(heads...  0.92 us
  transfers between devices with their start and end apart: 6, of which 2 were waited for; matrix products, arithmetic and copies ran while one was open for 3% of the time, Pallas kernels for 15%

profile of v7, /device:TPU:26, one launch (start us, length us, event | category | flops | bytes accessed | tf_op | source)
XLA Modules:
  0.0 21.4 jit_solution(11183162762943164319)
XLA Ops:
  0.6 1.1 %shard_map.94 = (bf16[128,128]{1,0:T(8,128)(2,1)S(1)}, bf16[1088,128]{1,0:T(8,128)(2,1)S(1)}, bf16[128,512]{1,0:T(8,128)(2,1)S(1)}, f32[8,128]{1,0:T(8,128)S(1)}, s32[1,128]{1,0:T(1,128)S(1)}) custom-call(bf16[128,512]{1,0:T(8,128)(2,1)} %q_in.1, bf16[128,512]{1,0:T(8,128)(2,1)} %g_in.1, bf16[128,512]{1,0:T(8,128)(2,1)} %o_in.1, f32[8,128]{1,0:T(8,128)} %log_in.1, ...), custom_call_target="tpu_custom_call" | custom-call | tf_op jit(solution)/shard_map/pallas_call | solution.py:257
  1.8 0.3 %shard_map.95.refs_0_ = bf16[1088,128]{1,0:T(8,128)(2,1)S(1)} custom-call(bf16[1088,128]{1,0:T(8,128)(2,1)S(1)} %get-tuple-element.16.rows_in, bf16[128,512]{1,0:T(8,128)(2,1)S(1)} %get-tuple-element.17.o_ref, f32[8,128]{1,0:T(8,128)S(1)} %get-tuple-element.18.log_ref, s32[1,128]{1,0:T(1,128)S(1)} %get-tuple-element.19.begin_ref), custom_call_target="tpu_custom_call", output_to_operand_aliasing={{}: (0, {})} | custom-call | tf_op jit(solution)/shard_map/pallas_call | solution.py:283
  2.1 0.0 collective-permute-start
  2.1 3.4 %collective-permute-start.2 = (bf16[128,128]{1,0:T(8,128)(2,1)S(1)}, bf16[128,128]{1,0:T(8,128)(2,1)S(1)}, u32[]{:S(2)}, u32[]{:S(2)}) collective-permute-start(bf16[128,128]{1,0:T(8,128)(2,1)S(1)} %get-tuple-element.20.refs_2_.refs_3_), channel_id=1, source_target_pairs={{0,16},{1,17},{2,18},{3,19},{4,20},{5,21},{6,22},{7,23},{8,24},{9,... | collective-permute-start | bytes 98312 | tf_op jit(solution)/shard_map/ppermute | solution.py:39
  5.5 0.1 collective-permute-start.1
  5.6 2.3 %collective-permute-done.2.refs_2_.refs_5_ = bf16[128,128]{1,0:T(8,128)(2,1)S(1)} collective-permute-done((bf16[128,128]{1,0:T(8,128)(2,1)S(1)}, bf16[128,128]{1,0:T(8,128)(2,1)S(1)}, u32[]{:S(2)}, u32[]{:S(2)}) %collective-permute-start.2) | collective-permute-done | bytes 32800 | tf_op jit(solution)/shard_map/ppermute | solution.py:39
  7.9 0.0 collective-permute-done.refs_1_
  7.9 0.9 %shard_map.98 = (bf16[1024,256]{1,0:T(8,128)(2,1)S(1)}, bf16[128,128]{1,0:T(8,128)(2,1)S(1)}) custom-call(bf16[1088,128]{1,0:T(8,128)(2,1)S(1)} %shard_map.95.refs_0_, bf16[1088,128]{1,0:T(8,128)(2,1)S(1)} %collective-permute-done.refs_1_, bf16[128,128]{1,0:T(8,128)(2,1)S(1)} %collective-permute-done.2.refs_2_.refs_5_), custom_call_target="tpu_custom_call" | custom-call | tf_op jit(solution)/shard_map/pallas_call | solution.py:307
  8.8 4.5 %collective-permute-start.5 = (bf16[128,128]{1,0:T(8,128)(2,1)S(1)}, bf16[128,128]{1,0:T(8,128)(2,1)S(1)}, u32[]{:S(2)}, u32[]{:S(2)}) collective-permute-start(bf16[128,128]{1,0:T(8,128)(2,1)S(1)} %get-tuple-element.28), channel_id=1, source_target_pairs={{16,0},{17,1},{18,2},{19,3},{20,4},{21,5},{22,6},{23,7},{24,8},{25... | collective-permute-start | bytes 98312 | tf_op jit(solution)/shard_map/ppermute | solution.py:39
  13.4 0.0 collective-permute-done.1.refs_2_.refs_4_
  13.4 0.9 %shard_map.97 = (bf16[1024,256]{1,0:T(8,128)(2,1)S(1)}, bf16[128,128]{1,0:T(8,128)(2,1)S(1)}) custom-call(bf16[1088,128]{1,0:T(8,128)(2,1)S(1)} %shard_map.95.refs_0_, bf16[1088,128]{1,0:T(8,128)(2,1)S(1)} %collective-permute-done.refs_1_, bf16[128,128]{1,0:T(8,128)(2,1)S(1)} %collective-permute-done.1.refs_2_.refs_4_), custom_call_target="tpu_custom_call" | custom-call | tf_op jit(solution)/shard_map/pallas_call | solution.py:300
  14.3 2.2 %collective-permute-start.4 = (bf16[128,128]{1,0:T(8,128)(2,1)S(1)}, bf16[128,128]{1,0:T(8,128)(2,1)S(1)}, u32[]{:S(2)}, u32[]{:S(2)}) collective-permute-start(bf16[128,128]{1,0:T(8,128)(2,1)S(1)} %get-tuple-element.27), channel_id=1, source_target_pairs={{1,0},{2,1},{3,2},{4,3},{5,4},{6,5},{7,6},{9,8},{10,9},{11,10},{12... | collective-permute-start | bytes 98312 | tf_op jit(solution)/shard_map/ppermute | solution.py:20
  16.5 0.9 %shard_map.96 = (bf16[1024,256]{1,0:T(8,128)(2,1)S(1)}, f32[128,128]{1,0:T(8,128)S(1)}) custom-call(bf16[1088,128]{1,0:T(8,128)(2,1)S(1)} %shard_map.95.refs_0_, bf16[1088,128]{1,0:T(8,128)(2,1)S(1)} %collective-permute-done.refs_1_, bf16[128,128]{1,0:T(8,128)(2,1)S(1)} %get-tuple-element.20.refs_2_.refs_3_), custom_call_target="tpu_custom_call" | custom-call | tf_op jit(solution)/shard_map/pallas_call | solution.py:293
  17.5 0.5 %shard_map.99 = (f32[128,512]{1,0:T(8,128)S(1)}, bf16[128,512]{1,0:T(8,128)(2,1)S(1)}) custom-call(bf16[1024,256]{1,0:T(8,128)(2,1)S(1)} %get-tuple-element.21.refs_0_, bf16[1024,256]{1,0:T(8,128)(2,1)S(1)} %get-tuple-element.22.refs_1_, bf16[1024,256]{1,0:T(8,128)(2,1)S(1)} %get-tuple-element.23.refs_2_, ...), custom_call_target="tpu_custom_call" | custom-call | tf_op jit(solution)/shard_map/pallas_call | solution.py:314
  17.9 0.1 collective-permute-start.3
  18.0 0.0 collective-permute-done.5
  18.0 2.1 %collective-permute-done.4 = bf16[128,128]{1,0:T(8,128)(2,1)S(1)} collective-permute-done((bf16[128,128]{1,0:T(8,128)(2,1)S(1)}, bf16[128,128]{1,0:T(8,128)(2,1)S(1)}, u32[]{:S(2)}, u32[]{:S(2)}) %collective-permute-start.4) | collective-permute-done | bytes 32800 | tf_op jit(solution)/shard_map/ppermute | solution.py:20
  20.1 0.6 %slice_bitcast_fusion = (bf16[128,64]{0,1:T(8,128)(2,1)}, bf16[128,64]{0,1:T(8,128)(2,1)}) fusion(bf16[128,128]{1,0:T(8,128)(2,1)S(1)} %add_convert_fusion.1), kind=kLoop, calls=%fused_computation.2 | loop fusion | bytes 65536 | tf_op jit(solution)/shard_map/transpose | solution.py:328
  20.8 0.0 collective-permute-done.3
  20.8 0.7 %add_convert_fusion = bf16[128,512]{1,0:T(8,128)(2,1)} fusion(f32[128,512]{1,0:T(8,128)S(1)} %get-tuple-element.24, bf16[128,512]{1,0:T(8,128)(2,1)S(1)} %collective-permute-done.3), kind=kLoop, calls=%fused_computation | loop fusion | flops 196608 | bytes 524288 | tf_op jit(solution)/shard_map/convert_element_type | solution.py:322
  (1 shorter events, 0.0 us)
Async XLA Ops:
  2.1 5.8 %collective-permute-start = (bf16[1088,128]{1,0:T(8,128)(2,1)S(1)}, bf16[1088,128]{1,0:T(8,128)(2,1)S(1)}, u32[]{:S(2)}, u32[]{:S(2)}) collective-permute-start(bf16[1088,128]{1,0:T(8,128)(2,1)S(1)} %shard_map.95.refs_0_), channel_id=1, source_target_pairs={{0,8},{8,0},{16,24},{24,16},{1,9},{9,1},{17,25},{25,17},{2,10},{10... | collective-permute-start | bytes 835592 | tf_op jit(solution)/shard_map/ppermute | solution.py:25
  2.1 5.8 %collective-permute-start.2 = (bf16[128,128]{1,0:T(8,128)(2,1)S(1)}, bf16[128,128]{1,0:T(8,128)(2,1)S(1)}, u32[]{:S(2)}, u32[]{:S(2)}) collective-permute-start(bf16[128,128]{1,0:T(8,128)(2,1)S(1)} %get-tuple-element.20.refs_2_.refs_3_), channel_id=1, source_target_pairs={{0,16},{1,17},{2,18},{3,19},{4,20},{5,21},{6,22},{7,23},{8,24},{9,... | collective-permute-start | bytes 98312 | tf_op jit(solution)/shard_map/ppermute | solution.py:39
  5.5 7.9 %collective-permute-start.1 = (bf16[128,128]{1,0:T(8,128)(2,1)S(1)}, bf16[128,128]{1,0:T(8,128)(2,1)S(1)}, u32[]{:S(2)}, u32[]{:S(2)}) collective-permute-start(bf16[128,128]{1,0:T(8,128)(2,1)S(1)} %get-tuple-element.20.refs_2_.refs_3_), channel_id=1, source_target_pairs={{0,1},{1,2},{2,3},{3,4},{4,5},{5,6},{6,7},{7,0},{8,9},{9,10},{10,1... | collective-permute-start | bytes 98312 | tf_op jit(solution)/shard_map/ppermute | solution.py:20
  8.8 9.2 %collective-permute-start.5 = (bf16[128,128]{1,0:T(8,128)(2,1)S(1)}, bf16[128,128]{1,0:T(8,128)(2,1)S(1)}, u32[]{:S(2)}, u32[]{:S(2)}) collective-permute-start(bf16[128,128]{1,0:T(8,128)(2,1)S(1)} %get-tuple-element.28), channel_id=1, source_target_pairs={{16,0},{17,1},{18,2},{19,3},{20,4},{21,5},{22,6},{23,7},{24,8},{25... | collective-permute-start | bytes 98312 | tf_op jit(solution)/shard_map/ppermute | solution.py:39
  14.3 5.8 %collective-permute-start.4 = (bf16[128,128]{1,0:T(8,128)(2,1)S(1)}, bf16[128,128]{1,0:T(8,128)(2,1)S(1)}, u32[]{:S(2)}, u32[]{:S(2)}) collective-permute-start(bf16[128,128]{1,0:T(8,128)(2,1)S(1)} %get-tuple-element.27), channel_id=1, source_target_pairs={{1,0},{2,1},{3,2},{4,3},{5,4},{6,5},{7,6},{9,8},{10,9},{11,10},{12... | collective-permute-start | bytes 98312 | tf_op jit(solution)/shard_map/ppermute | solution.py:20
  17.9 2.8 %collective-permute-start.3 = (bf16[128,512]{1,0:T(8,128)(2,1)S(1)}, bf16[128,512]{1,0:T(8,128)(2,1)S(1)}, u32[]{:S(2)}, u32[]{:S(2)}) collective-permute-start(bf16[128,512]{1,0:T(8,128)(2,1)S(1)} %get-tuple-element.25), channel_id=1, source_target_pairs={{0,8},{8,0},{16,24},{24,16},{1,9},{9,1},{17,25},{25,17},{2,10},{10... | collective-permute-start | bytes 393224 | tf_op jit(solution)/shard_map/ppermute | solution.py:25

commit v8 on v7

--- a/solution.py
+++ b/solution.py
@@ -227,6 +227,25 @@
         other_ref[:, span] = both[:, rows:].T.astype(jnp.bfloat16)
 
 
+def end_body(query_ref, query_back_ref, total_ref, *refs):
+    term_refs, (q_out, k_out, v_out, q_buf, kv_buf, sems) = refs[:-6], refs[-6:]
+    width = k_out.shape[0]
+    query = query_ref[...] + query_back_ref[...].astype(jnp.float32)
+    q_buf[...] = query.astype(q_buf.dtype)
+    copies = [pltpu.make_async_copy(q_buf, q_out, sems.at[0])]
+    copies[0].start()
+    total = total_ref[...]
+    for ref in term_refs:
+        total = total + ref[...].astype(jnp.float32)
+    kv_buf[...] = total.astype(kv_buf.dtype)
+    copies.append(pltpu.make_async_copy(kv_buf.at[:width, :], k_out, sems.at[1]))
+    copies.append(pltpu.make_async_copy(kv_buf.at[width:, :], v_out, sems.at[2]))
+    for copy in copies[1:]:
+        copy.start()
+    for copy in copies:
+        copy.wait()
+
+
 def in_vmem(count):
     return [pl.BlockSpec(memory_space=pltpu.VMEM) for _ in range(count)]
 
@@ -319,13 +338,26 @@
         compiler_params=params,
     )(*held(own_grads, past_grads, rest_grads, mine, past, *seen))
     query_back = exchanged(query_other, "team", 1)
-    query_grad = (query_mine + query_back.astype(jnp.float32)).astype(jnp.bfloat16)
     got = [around(past_piece, "blk", -1)]
     got += [skewed(piece, k, False) for k, piece in zip(steps, sent)]
-    for term in got:
-        total = total + term.astype(jnp.float32)
-    total = total.astype(jnp.bfloat16)
-    return (query_grad, total[:width].T, total[width:].T)
+    half_grad = jax.ShapeDtypeStruct((width, rows), jnp.bfloat16)
+    query_grad, key_grad, value_grad = pl.pallas_call(
+        end_body,
+        out_shape=[
+            jax.ShapeDtypeStruct((rows, features), jnp.bfloat16),
+            half_grad,
+            half_grad,
+        ],
+        in_specs=in_vmem(3 + len(got)),
+        out_specs=[pl.BlockSpec(memory_space=pltpu.HBM)] * 3,
+        scratch_shapes=[
+            low(rows, features),
+            low(lanes, rows),
+            pltpu.SemaphoreType.DMA((3,)),
+        ],
+        compiler_params=params,
+    )(*held(query_mine, query_back, total, *got))
+    return (query_grad, key_grad.T, value_grad.T)
 
 
 def solution(mesh):

time: 21.7 us -> 23.9 us (1.10)
  the two profiles are of different devices: /device:TPU:26 before, /device:TPU:0 now
where the time goes in v8:
time: 23.9 us; the launch traced here: 23.6 us
  waiting for transfers between devices  9.3 us (39%)
  starting transfers between devices  9.11 us (38%)
  Pallas kernels  4.48 us (19%)
  between operations  0.71 us (3%)
    ppermute x2, waiting for transfers between devices, around(): return lax.ppermute(x, axis, pairs)  6.08 us
    ppermute x2, starting transfers between devices, skewed(): return lax.ppermute(x, ('team', 'blk'), pairs)  5.66 us
    ppermute x2, waiting for transfers between devices, skewed(): return lax.ppermute(x, ('team', 'blk'), pairs)  3.21 us
    ppermute x2, starting transfers between devices, around(): return lax.ppermute(x, axis, pairs)  2.87 us
    pallas_call x1, Pallas kernels, per_device(): pl.pallas_call(load_body, out_shape=[low(lanes, rows), low(heads * (rows...  1.12 us
    pallas_call x1, Pallas kernels, per_device(): pl.pallas_call(own_body, out_shape=[low(heads * rows, 2 * rows), full(lan...  0.92 us
    pallas_call x1, Pallas kernels, per_device(): pl.pallas_call(functools.partial(rest_body, steps), out_shape=[low(heads...  0.92 us
    pallas_call x1, Pallas kernels, per_device(): pl.pallas_call(end_body, out_shape=[jax.ShapeDtypeStruct((rows, features)...  0.71 us
  transfers between devices with their start and end apart: 6, of which 3 were waited for; matrix products, arithmetic and copies ran while one was open for 0% of the time, Pallas kernels for 8%

profile of v8, /device:TPU:0, one launch (start us, length us, event | category | flops | bytes accessed | tf_op | source)
XLA Modules:
  0.0 23.6 jit_solution(13678527295477624322)
XLA Ops:
  0.6 1.1 %shard_map.94 = (bf16[128,128]{1,0:T(8,128)(2,1)S(1)}, bf16[1088,128]{1,0:T(8,128)(2,1)S(1)}, bf16[128,512]{1,0:T(8,128)(2,1)S(1)}, f32[8,128]{1,0:T(8,128)S(1)}, s32[1,128]{1,0:T(1,128)S(1)}) custom-call(bf16[128,512]{1,0:T(8,128)(2,1)} %q_in.1, bf16[128,512]{1,0:T(8,128)(2,1)} %g_in.1, bf16[128,512]{1,0:T(8,128)(2,1)} %o_in.1, f32[8,128]{1,0:T(8,128)} %log_in.1, ...), custom_call_target="tpu_custom_call" | custom-call | tf_op jit(solution)/shard_map/pallas_call | solution.py:276
  1.8 0.3 %shard_map.95.refs_0_ = bf16[1088,128]{1,0:T(8,128)(2,1)S(1)} custom-call(bf16[1088,128]{1,0:T(8,128)(2,1)S(1)} %get-tuple-element.19.rows_in, bf16[128,512]{1,0:T(8,128)(2,1)S(1)} %get-tuple-element.20.o_ref, f32[8,128]{1,0:T(8,128)S(1)} %get-tuple-element.21.log_ref, s32[1,128]{1,0:T(1,128)S(1)} %get-tuple-element.22.begin_ref), custom_call_target="tpu_custom_call", output_to_operand_aliasing={{}: (0, {})} | custom-call | tf_op jit(solution)/shard_map/pallas_call | solution.py:302
  2.1 0.5 %collective-permute-start = (bf16[1088,128]{1,0:T(8,128)(2,1)S(1)}, bf16[1088,128]{1,0:T(8,128)(2,1)S(1)}, u32[]{:S(2)}, u32[]{:S(2)}) collective-permute-start(bf16[1088,128]{1,0:T(8,128)(2,1)S(1)} %shard_map.95.refs_0_), channel_id=1, source_target_pairs={{0,8},{8,0},{16,24},{24,16},{1,9},{9,1},{17,25},{25,17},{2,10},{10... | collective-permute-start | bytes 835592 | tf_op jit(solution)/shard_map/ppermute | solution.py:25
  2.6 4.4 %collective-permute-start.2 = (bf16[128,128]{1,0:T(8,128)(2,1)S(1)}, bf16[128,128]{1,0:T(8,128)(2,1)S(1)}, u32[]{:S(2)}, u32[]{:S(2)}) collective-permute-start(bf16[128,128]{1,0:T(8,128)(2,1)S(1)} %get-tuple-element.23.refs_2_.refs_3_), channel_id=1, source_target_pairs={{0,16},{1,17},{2,18},{3,19},{4,20},{5,21},{6,22},{7,23},{8,24},{9,... | collective-permute-start | bytes 98312 | tf_op jit(solution)/shard_map/ppermute | solution.py:39
  7.0 1.6 %collective-permute-start.1 = (bf16[128,128]{1,0:T(8,128)(2,1)S(1)}, bf16[128,128]{1,0:T(8,128)(2,1)S(1)}, u32[]{:S(2)}, u32[]{:S(2)}) collective-permute-start(bf16[128,128]{1,0:T(8,128)(2,1)S(1)} %get-tuple-element.23.refs_2_.refs_3_), channel_id=1, source_target_pairs={{0,1},{1,2},{2,3},{3,4},{4,5},{5,6},{6,7},{7,0},{8,9},{9,10},{10,1... | collective-permute-start | bytes 98312 | tf_op jit(solution)/shard_map/ppermute | solution.py:20
  8.6 0.0 collective-permute-done.refs_1_
  8.6 0.9 %shard_map.96 = (bf16[1024,256]{1,0:T(8,128)(2,1)S(1)}, f32[128,128]{1,0:T(8,128)S(1)}) custom-call(bf16[1088,128]{1,0:T(8,128)(2,1)S(1)} %shard_map.95.refs_0_, bf16[1088,128]{1,0:T(8,128)(2,1)S(1)} %collective-permute-done.refs_1_, bf16[128,128]{1,0:T(8,128)(2,1)S(1)} %get-tuple-element.23.refs_2_.refs_3_), custom_call_target="tpu_custom_call" | custom-call | tf_op jit(solution)/shard_map/pallas_call | solution.py:312
  9.5 0.0 collective-permute-done.2.refs_2_.refs_5_
  9.5 0.9 %shard_map.98 = (bf16[1024,256]{1,0:T(8,128)(2,1)S(1)}, bf16[128,128]{1,0:T(8,128)(2,1)S(1)}) custom-call(bf16[1088,128]{1,0:T(8,128)(2,1)S(1)} %shard_map.95.refs_0_, bf16[1088,128]{1,0:T(8,128)(2,1)S(1)} %collective-permute-done.refs_1_, bf16[128,128]{1,0:T(8,128)(2,1)S(1)} %collective-permute-done.2.refs_2_.refs_5_), custom_call_target="tpu_custom_call" | custom-call | tf_op jit(solution)/shard_map/pallas_call | solution.py:326
  10.4 3.2 %collective-permute-done.1.refs_2_.refs_4_ = bf16[128,128]{1,0:T(8,128)(2,1)S(1)} collective-permute-done((bf16[128,128]{1,0:T(8,128)(2,1)S(1)}, bf16[128,128]{1,0:T(8,128)(2,1)S(1)}, u32[]{:S(2)}, u32[]{:S(2)}) %collective-permute-start.1) | collective-permute-done | bytes 32800 | tf_op jit(solution)/shard_map/ppermute | solution.py:20
  13.7 0.4 %shard_map.99 = (f32[128,512]{1,0:T(8,128)S(1)}, bf16[128,512]{1,0:T(8,128)(2,1)S(1)}) custom-call(bf16[1024,256]{1,0:T(8,128)(2,1)S(1)} %get-tuple-element.24.refs_0_, bf16[1024,256]{1,0:T(8,128)(2,1)S(1)} %get-tuple-element.25.refs_1_, bf16[1024,256]{1,0:T(8,128)(2,1)S(1)} %get-tuple-element.26.refs_2_, ...), custom_call_target="tpu_custom_call" | custom-call | tf_op jit(solution)/shard_map/pallas_call | solution.py:333
  14.1 0.1 collective-permute-start.3
  14.2 1.3 %collective-permute-start.5 = (bf16[128,128]{1,0:T(8,128)(2,1)S(1)}, bf16[128,128]{1,0:T(8,128)(2,1)S(1)}, u32[]{:S(2)}, u32[]{:S(2)}) collective-permute-start(bf16[128,128]{1,0:T(8,128)(2,1)S(1)} %get-tuple-element.31), channel_id=1, source_target_pairs={{16,0},{17,1},{18,2},{19,3},{20,4},{21,5},{22,6},{23,7},{24,8},{25... | collective-permute-start | bytes 98312 | tf_op jit(solution)/shard_map/ppermute | solution.py:39
  15.5 1.3 %collective-permute-start.4 = (bf16[128,128]{1,0:T(8,128)(2,1)S(1)}, bf16[128,128]{1,0:T(8,128)(2,1)S(1)}, u32[]{:S(2)}, u32[]{:S(2)}) collective-permute-start(bf16[128,128]{1,0:T(8,128)(2,1)S(1)} %get-tuple-element.30), channel_id=1, source_target_pairs={{1,0},{2,1},{3,2},{4,3},{5,4},{6,5},{7,6},{9,8},{10,9},{11,10},{12... | collective-permute-start | bytes 98312 | tf_op jit(solution)/shard_map/ppermute | solution.py:20
  16.8 3.2 %collective-permute-done.5.refs_1_ = bf16[128,128]{1,0:T(8,128)(2,1)S(1)} collective-permute-done((bf16[128,128]{1,0:T(8,128)(2,1)S(1)}, bf16[128,128]{1,0:T(8,128)(2,1)S(1)}, u32[]{:S(2)}, u32[]{:S(2)}) %collective-permute-start.5) | collective-permute-done | bytes 32800 | tf_op jit(solution)/shard_map/ppermute | solution.py:39
  20.0 2.9 %collective-permute-done.4.refs_0_ = bf16[128,128]{1,0:T(8,128)(2,1)S(1)} collective-permute-done((bf16[128,128]{1,0:T(8,128)(2,1)S(1)}, bf16[128,128]{1,0:T(8,128)(2,1)S(1)}, u32[]{:S(2)}, u32[]{:S(2)}) %collective-permute-start.4) | collective-permute-done | bytes 32800 | tf_op jit(solution)/shard_map/ppermute | solution.py:20
  22.9 0.0 collective-permute-done.3.query_back_ref
  22.9 0.7 %shard_map.100 = (bf16[128,512]{1,0:T(8,128)(2,1)}, bf16[64,128]{1,0:T(8,128)(2,1)}, bf16[64,128]{1,0:T(8,128)(2,1)}) custom-call(f32[128,512]{1,0:T(8,128)S(1)} %get-tuple-element.27.query_ref, bf16[128,512]{1,0:T(8,128)(2,1)S(1)} %collective-permute-done.3.query_back_ref, f32[128,128]{1,0:T(8,128)S(1)} %get-tuple-element.29.total_ref, ...), custom_call_target="tpu_custom_call" | custom-call | tf_op jit(solution)/shard_map/pallas_call | solution.py:344
  (1 shorter events, 0.0 us)
Async XLA Ops:
  2.1 6.5 %collective-permute-start = (bf16[1088,128]{1,0:T(8,128)(2,1)S(1)}, bf16[1088,128]{1,0:T(8,128)(2,1)S(1)}, u32[]{:S(2)}, u32[]{:S(2)}) collective-permute-start(bf16[1088,128]{1,0:T(8,128)(2,1)S(1)} %shard_map.95.refs_0_), channel_id=1, source_target_pairs={{0,8},{8,0},{16,24},{24,16},{1,9},{9,1},{17,25},{25,17},{2,10},{10... | collective-permute-start | bytes 835592 | tf_op jit(solution)/shard_map/ppermute | solution.py:25
  2.6 6.9 %collective-permute-start.2 = (bf16[128,128]{1,0:T(8,128)(2,1)S(1)}, bf16[128,128]{1,0:T(8,128)(2,1)S(1)}, u32[]{:S(2)}, u32[]{:S(2)}) collective-permute-start(bf16[128,128]{1,0:T(8,128)(2,1)S(1)} %get-tuple-element.23.refs_2_.refs_3_), channel_id=1, source_target_pairs={{0,16},{1,17},{2,18},{3,19},{4,20},{5,21},{6,22},{7,23},{8,24},{9,... | collective-permute-start | bytes 98312 | tf_op jit(solution)/shard_map/ppermute | solution.py:39
  7.0 6.7 %collective-permute-start.1 = (bf16[128,128]{1,0:T(8,128)(2,1)S(1)}, bf16[128,128]{1,0:T(8,128)(2,1)S(1)}, u32[]{:S(2)}, u32[]{:S(2)}) collective-permute-start(bf16[128,128]{1,0:T(8,128)(2,1)S(1)} %get-tuple-element.23.refs_2_.refs_3_), channel_id=1, source_target_pairs={{0,1},{1,2},{2,3},{3,4},{4,5},{5,6},{6,7},{7,0},{8,9},{9,10},{10,1... | collective-permute-start | bytes 98312 | tf_op jit(solution)/shard_map/ppermute | solution.py:20
  14.1 8.8 %collective-permute-start.3 = (bf16[128,512]{1,0:T(8,128)(2,1)S(1)}, bf16[128,512]{1,0:T(8,128)(2,1)S(1)}, u32[]{:S(2)}, u32[]{:S(2)}) collective-permute-start(bf16[128,512]{1,0:T(8,128)(2,1)S(1)} %get-tuple-element.28), channel_id=1, source_target_pairs={{0,8},{8,0},{16,24},{24,16},{1,9},{9,1},{17,25},{25,17},{2,10},{10... | collective-permute-start | bytes 393224 | tf_op jit(solution)/shard_map/ppermute | solution.py:25
  14.2 5.8 %collective-permute-start.5 = (bf16[128,128]{1,0:T(8,128)(2,1)S(1)}, bf16[128,128]{1,0:T(8,128)(2,1)S(1)}, u32[]{:S(2)}, u32[]{:S(2)}) collective-permute-start(bf16[128,128]{1,0:T(8,128)(2,1)S(1)} %get-tuple-element.31), channel_id=1, source_target_pairs={{16,0},{17,1},{18,2},{19,3},{20,4},{21,5},{22,6},{23,7},{24,8},{25... | collective-permute-start | bytes 98312 | tf_op jit(solution)/shard_map/ppermute | solution.py:39
  15.5 7.4 %collective-permute-start.4 = (bf16[128,128]{1,0:T(8,128)(2,1)S(1)}, bf16[128,128]{1,0:T(8,128)(2,1)S(1)}, u32[]{:S(2)}, u32[]{:S(2)}) collective-permute-start(bf16[128,128]{1,0:T(8,128)(2,1)S(1)} %get-tuple-element.30), channel_id=1, source_target_pairs={{1,0},{2,1},{3,2},{4,3},{5,4},{6,5},{7,6},{9,8},{10,9},{11,10},{12... | collective-permute-start | bytes 98312 | tf_op jit(solution)/shard_map/ppermute | solution.py:20

commit v9 on v8

--- a/solution.py
+++ b/solution.py
@@ -122,8 +122,8 @@
     none = jnp.zeros_like(kv)
     k_low = jnp.where(low_key, kv * jnp.asarray(1.0 / math.sqrt(width), kv.dtype), none)
     v_high = jnp.where(low_key, none, kv)
-    key_halves = (k_low, half_turn(k_low, width))
-    value_halves = (half_turn(v_high, width), v_high)
+    key_halves = jnp.concatenate([k_low, half_turn(k_low, width)], 0)
+    value_halves = jnp.concatenate([half_turn(v_high, width), v_high], 0)
     inside = lax.broadcasted_iota(jnp.int32, (rows, 2 * rows), 0)
     key_pos = jnp.concatenate([inside + base for base in bases], 0)
     lane = lax.broadcasted_iota(jnp.int32, (1, 2 * rows), 1)
@@ -135,13 +135,14 @@
         g_pair = pair_rows(heads // 2 + pair)
         queries.append(q_pair)
         cotangents.append(g_pair)
+        scores = dot(key_halves, q_pair, NT)
+        prob_grads = dot(value_halves, g_pair, NT)
         for half in range(2):
+            span = slice(half * total, (half + 1) * total)
             head = 2 * pair + half
-            scores = dot(key_halves[half], q_pair, NT)
-            shifted = scores - log_norm[head : head + 1, :]
+            shifted = scores[span] - log_norm[head : head + 1, :]
             weights = jnp.exp(jnp.where(allowed, shifted, -jnp.inf))
-            prob_grad = dot(value_halves[half], g_pair, NT)
-            score_grad = weights * (prob_grad - delta[head : head + 1, :])
+            score_grad = weights * (prob_grads[span] - delta[head : head + 1, :])
             low = score_grad.astype(jnp.bfloat16)
             grad_ref[head * total : (head + 1) * total, :] = low
             probs[half].append(weights.astype(jnp.bfloat16))

time: 23.9 us -> 23.9 us (level)
  no operation moved by 1% of the time
where the time goes in v9:
time: 23.9 us; the launch traced here: 23.6 us
  waiting for transfers between devices  9.31 us (39%)
  starting transfers between devices  9.11 us (38%)
  Pallas kernels  4.47 us (19%)
  between operations  0.71 us (3%)
    ppermute x2, waiting for transfers between devices, around(): return lax.ppermute(x, axis, pairs)  6.1 us
    ppermute x2, starting transfers between devices, skewed(): return lax.ppermute(x, ('team', 'blk'), pairs)  5.66 us
    ppermute x2, waiting for transfers between devices, skewed(): return lax.ppermute(x, ('team', 'blk'), pairs)  3.21 us
    ppermute x2, starting transfers between devices, around(): return lax.ppermute(x, axis, pairs)  2.87 us
    pallas_call x1, Pallas kernels, per_device(): pl.pallas_call(load_body, out_shape=[low(lanes, rows), low(heads * (rows...  1.12 us
    pallas_call x1, Pallas kernels, per_device(): pl.pallas_call(functools.partial(rest_body, steps), out_shape=[low(heads...  0.91 us
    pallas_call x1, Pallas kernels, per_device(): pl.pallas_call(own_body, out_shape=[low(heads * rows, 2 * rows), full(lan...  0.91 us
    pallas_call x1, Pallas kernels, per_device(): pl.pallas_call(end_body, out_shape=[jax.ShapeDtypeStruct((rows, features)...  0.71 us
  transfers between devices with their start and end apart: 6, of which 3 were waited for; matrix products, arithmetic and copies ran while one was open for 0% of the time, Pallas kernels for 8%

profile of v9, /device:TPU:0, one launch (start us, length us, event | category | flops | bytes accessed | tf_op | source)
XLA Modules:
  0.0 23.6 jit_solution(14516342998320460222)
XLA Ops:
  0.6 1.1 %shard_map.94 = (bf16[128,128]{1,0:T(8,128)(2,1)S(1)}, bf16[1088,128]{1,0:T(8,128)(2,1)S(1)}, bf16[128,512]{1,0:T(8,128)(2,1)S(1)}, f32[8,128]{1,0:T(8,128)S(1)}, s32[1,128]{1,0:T(1,128)S(1)}) custom-call(bf16[128,512]{1,0:T(8,128)(2,1)} %q_in.1, bf16[128,512]{1,0:T(8,128)(2,1)} %g_in.1, bf16[128,512]{1,0:T(8,128)(2,1)} %o_in.1, f32[8,128]{1,0:T(8,128)} %log_in.1, ...), custom_call_target="tpu_custom_call" | custom-call | tf_op jit(solution)/shard_map/pallas_call | solution.py:277
  1.8 0.3 %shard_map.95.refs_0_ = bf16[1088,128]{1,0:T(8,128)(2,1)S(1)} custom-call(bf16[1088,128]{1,0:T(8,128)(2,1)S(1)} %get-tuple-element.19.rows_in, bf16[128,512]{1,0:T(8,128)(2,1)S(1)} %get-tuple-element.20.o_ref, f32[8,128]{1,0:T(8,128)S(1)} %get-tuple-element.21.log_ref, s32[1,128]{1,0:T(1,128)S(1)} %get-tuple-element.22.begin_ref), custom_call_target="tpu_custom_call", output_to_operand_aliasing={{}: (0, {})} | custom-call | tf_op jit(solution)/shard_map/pallas_call | solution.py:303
  2.1 0.5 %collective-permute-start = (bf16[1088,128]{1,0:T(8,128)(2,1)S(1)}, bf16[1088,128]{1,0:T(8,128)(2,1)S(1)}, u32[]{:S(2)}, u32[]{:S(2)}) collective-permute-start(bf16[1088,128]{1,0:T(8,128)(2,1)S(1)} %shard_map.95.refs_0_), channel_id=1, source_target_pairs={{0,8},{8,0},{16,24},{24,16},{1,9},{9,1},{17,25},{25,17},{2,10},{10... | collective-permute-start | bytes 835592 | tf_op jit(solution)/shard_map/ppermute | solution.py:25
  2.6 4.4 %collective-permute-start.2 = (bf16[128,128]{1,0:T(8,128)(2,1)S(1)}, bf16[128,128]{1,0:T(8,128)(2,1)S(1)}, u32[]{:S(2)}, u32[]{:S(2)}) collective-permute-start(bf16[128,128]{1,0:T(8,128)(2,1)S(1)} %get-tuple-element.23.refs_2_.refs_3_), channel_id=1, source_target_pairs={{0,16},{1,17},{2,18},{3,19},{4,20},{5,21},{6,22},{7,23},{8,24},{9,... | collective-permute-start | bytes 98312 | tf_op jit(solution)/shard_map/ppermute | solution.py:39
  7.0 1.6 %collective-permute-start.1 = (bf16[128,128]{1,0:T(8,128)(2,1)S(1)}, bf16[128,128]{1,0:T(8,128)(2,1)S(1)}, u32[]{:S(2)}, u32[]{:S(2)}) collective-permute-start(bf16[128,128]{1,0:T(8,128)(2,1)S(1)} %get-tuple-element.23.refs_2_.refs_3_), channel_id=1, source_target_pairs={{0,1},{1,2},{2,3},{3,4},{4,5},{5,6},{6,7},{7,0},{8,9},{9,10},{10,1... | collective-permute-start | bytes 98312 | tf_op jit(solution)/shard_map/ppermute | solution.py:20
  8.6 0.0 collective-permute-done.refs_1_
  8.6 0.9 %shard_map.96 = (bf16[1024,256]{1,0:T(8,128)(2,1)S(1)}, f32[128,128]{1,0:T(8,128)S(1)}) custom-call(bf16[1088,128]{1,0:T(8,128)(2,1)S(1)} %shard_map.95.refs_0_, bf16[1088,128]{1,0:T(8,128)(2,1)S(1)} %collective-permute-done.refs_1_, bf16[128,128]{1,0:T(8,128)(2,1)S(1)} %get-tuple-element.23.refs_2_.refs_3_), custom_call_target="tpu_custom_call" | custom-call | tf_op jit(solution)/shard_map/pallas_call | solution.py:313
  9.5 0.0 collective-permute-done.2.refs_2_.refs_5_
  9.5 0.9 %shard_map.98 = (bf16[1024,256]{1,0:T(8,128)(2,1)S(1)}, bf16[128,128]{1,0:T(8,128)(2,1)S(1)}) custom-call(bf16[1088,128]{1,0:T(8,128)(2,1)S(1)} %shard_map.95.refs_0_, bf16[1088,128]{1,0:T(8,128)(2,1)S(1)} %collective-permute-done.refs_1_, bf16[128,128]{1,0:T(8,128)(2,1)S(1)} %collective-permute-done.2.refs_2_.refs_5_), custom_call_target="tpu_custom_call" | custom-call | tf_op jit(solution)/shard_map/pallas_call | solution.py:327
  10.4 3.2 %collective-permute-done.1.refs_2_.refs_4_ = bf16[128,128]{1,0:T(8,128)(2,1)S(1)} collective-permute-done((bf16[128,128]{1,0:T(8,128)(2,1)S(1)}, bf16[128,128]{1,0:T(8,128)(2,1)S(1)}, u32[]{:S(2)}, u32[]{:S(2)}) %collective-permute-start.1) | collective-permute-done | bytes 32800 | tf_op jit(solution)/shard_map/ppermute | solution.py:20
  13.7 0.4 %shard_map.99 = (f32[128,512]{1,0:T(8,128)S(1)}, bf16[128,512]{1,0:T(8,128)(2,1)S(1)}) custom-call(bf16[1024,256]{1,0:T(8,128)(2,1)S(1)} %get-tuple-element.24.refs_0_, bf16[1024,256]{1,0:T(8,128)(2,1)S(1)} %get-tuple-element.25.refs_1_, bf16[1024,256]{1,0:T(8,128)(2,1)S(1)} %get-tuple-element.26.refs_2_, ...), custom_call_target="tpu_custom_call" | custom-call | tf_op jit(solution)/shard_map/pallas_call | solution.py:334
  14.1 0.1 collective-permute-start.3
  14.2 1.3 %collective-permute-start.5 = (bf16[128,128]{1,0:T(8,128)(2,1)S(1)}, bf16[128,128]{1,0:T(8,128)(2,1)S(1)}, u32[]{:S(2)}, u32[]{:S(2)}) collective-permute-start(bf16[128,128]{1,0:T(8,128)(2,1)S(1)} %get-tuple-element.31), channel_id=1, source_target_pairs={{16,0},{17,1},{18,2},{19,3},{20,4},{21,5},{22,6},{23,7},{24,8},{25... | collective-permute-start | bytes 98312 | tf_op jit(solution)/shard_map/ppermute | solution.py:39
  15.5 1.3 %collective-permute-start.4 = (bf16[128,128]{1,0:T(8,128)(2,1)S(1)}, bf16[128,128]{1,0:T(8,128)(2,1)S(1)}, u32[]{:S(2)}, u32[]{:S(2)}) collective-permute-start(bf16[128,128]{1,0:T(8,128)(2,1)S(1)} %get-tuple-element.30), channel_id=1, source_target_pairs={{1,0},{2,1},{3,2},{4,3},{5,4},{6,5},{7,6},{9,8},{10,9},{11,10},{12... | collective-permute-start | bytes 98312 | tf_op jit(solution)/shard_map/ppermute | solution.py:20
  16.8 3.2 %collective-permute-done.5.refs_1_ = bf16[128,128]{1,0:T(8,128)(2,1)S(1)} collective-permute-done((bf16[128,128]{1,0:T(8,128)(2,1)S(1)}, bf16[128,128]{1,0:T(8,128)(2,1)S(1)}, u32[]{:S(2)}, u32[]{:S(2)}) %collective-permute-start.5) | collective-permute-done | bytes 32800 | tf_op jit(solution)/shard_map/ppermute | solution.py:39
  20.0 2.9 %collective-permute-done.4.refs_0_ = bf16[128,128]{1,0:T(8,128)(2,1)S(1)} collective-permute-done((bf16[128,128]{1,0:T(8,128)(2,1)S(1)}, bf16[128,128]{1,0:T(8,128)(2,1)S(1)}, u32[]{:S(2)}, u32[]{:S(2)}) %collective-permute-start.4) | collective-permute-done | bytes 32800 | tf_op jit(solution)/shard_map/ppermute | solution.py:20
  22.9 0.0 collective-permute-done.3.query_back_ref
  22.9 0.7 %shard_map.100 = (bf16[128,512]{1,0:T(8,128)(2,1)}, bf16[64,128]{1,0:T(8,128)(2,1)}, bf16[64,128]{1,0:T(8,128)(2,1)}) custom-call(f32[128,512]{1,0:T(8,128)S(1)} %get-tuple-element.27.query_ref, bf16[128,512]{1,0:T(8,128)(2,1)S(1)} %collective-permute-done.3.query_back_ref, f32[128,128]{1,0:T(8,128)S(1)} %get-tuple-element.29.total_ref, ...), custom_call_target="tpu_custom_call" | custom-call | tf_op jit(solution)/shard_map/pallas_call | solution.py:345
  (1 shorter events, 0.0 us)
Async XLA Ops:
  2.1 6.5 %collective-permute-start = (bf16[1088,128]{1,0:T(8,128)(2,1)S(1)}, bf16[1088,128]{1,0:T(8,128)(2,1)S(1)}, u32[]{:S(2)}, u32[]{:S(2)}) collective-permute-start(bf16[1088,128]{1,0:T(8,128)(2,1)S(1)} %shard_map.95.refs_0_), channel_id=1, source_target_pairs={{0,8},{8,0},{16,24},{24,16},{1,9},{9,1},{17,25},{25,17},{2,10},{10... | collective-permute-start | bytes 835592 | tf_op jit(solution)/shard_map/ppermute | solution.py:25
  2.6 6.9 %collective-permute-start.2 = (bf16[128,128]{1,0:T(8,128)(2,1)S(1)}, bf16[128,128]{1,0:T(8,128)(2,1)S(1)}, u32[]{:S(2)}, u32[]{:S(2)}) collective-permute-start(bf16[128,128]{1,0:T(8,128)(2,1)S(1)} %get-tuple-element.23.refs_2_.refs_3_), channel_id=1, source_target_pairs={{0,16},{1,17},{2,18},{3,19},{4,20},{5,21},{6,22},{7,23},{8,24},{9,... | collective-permute-start | bytes 98312 | tf_op jit(solution)/shard_map/ppermute | solution.py:39
  7.0 6.7 %collective-permute-start.1 = (bf16[128,128]{1,0:T(8,128)(2,1)S(1)}, bf16[128,128]{1,0:T(8,128)(2,1)S(1)}, u32[]{:S(2)}, u32[]{:S(2)}) collective-permute-start(bf16[128,128]{1,0:T(8,128)(2,1)S(1)} %get-tuple-element.23.refs_2_.refs_3_), channel_id=1, source_target_pairs={{0,1},{1,2},{2,3},{3,4},{4,5},{5,6},{6,7},{7,0},{8,9},{9,10},{10,1... | collective-permute-start | bytes 98312 | tf_op jit(solution)/shard_map/ppermute | solution.py:20
  14.1 8.8 %collective-permute-start.3 = (bf16[128,512]{1,0:T(8,128)(2,1)S(1)}, bf16[128,512]{1,0:T(8,128)(2,1)S(1)}, u32[]{:S(2)}, u32[]{:S(2)}) collective-permute-start(bf16[128,512]{1,0:T(8,128)(2,1)S(1)} %get-tuple-element.28), channel_id=1, source_target_pairs={{0,8},{8,0},{16,24},{24,16},{1,9},{9,1},{17,25},{25,17},{2,10},{10... | collective-permute-start | bytes 393224 | tf_op jit(solution)/shard_map/ppermute | solution.py:25
  14.2 5.8 %collective-permute-start.5 = (bf16[128,128]{1,0:T(8,128)(2,1)S(1)}, bf16[128,128]{1,0:T(8,128)(2,1)S(1)}, u32[]{:S(2)}, u32[]{:S(2)}) collective-permute-start(bf16[128,128]{1,0:T(8,128)(2,1)S(1)} %get-tuple-element.31), channel_id=1, source_target_pairs={{16,0},{17,1},{18,2},{19,3},{20,4},{21,5},{22,6},{23,7},{24,8},{25... | collective-permute-start | bytes 98312 | tf_op jit(solution)/shard_map/ppermute | solution.py:39
  15.5 7.4 %collective-permute-start.4 = (bf16[128,128]{1,0:T(8,128)(2,1)S(1)}, bf16[128,128]{1,0:T(8,128)(2,1)S(1)}, u32[]{:S(2)}, u32[]{:S(2)}) collective-permute-start(bf16[128,128]{1,0:T(8,128)(2,1)S(1)} %get-tuple-element.30), channel_id=1, source_target_pairs={{1,0},{2,1},{3,2},{4,3},{5,4},{6,5},{7,6},{9,8},{10,9},{11,10},{12... | collective-permute-start | bytes 98312 | tf_op jit(solution)/shard_map/ppermute | solution.py:20

commit v10 on v9

--- a/solution.py
+++ b/solution.py
@@ -86,10 +86,10 @@
     prod = cotangents * o_ref[...].astype(jnp.float32)
     feature = lax.broadcasted_iota(jnp.int32, (heads, heads * width), 1)
     head_of = lax.broadcasted_iota(jnp.int32, (heads, heads * width), 0)
-    pick = (feature // width == head_of).astype(jnp.float32)
-    delta = lax.dot_general(
-        pick, prod, NT, precision=lax.Precision.HIGHEST, preferred_element_type=jnp.float32
-    )
+    pick = (feature // width == head_of).astype(jnp.bfloat16)
+    high = prod.astype(jnp.bfloat16)
+    rest = (prod - high.astype(jnp.float32)).astype(jnp.bfloat16)
+    delta = dot(pick, high, NT) + dot(pick, rest, NT)
     begin = jnp.broadcast_to(begin_ref[...], (heads, rows))
     begins = [(begin >> 8).astype(jnp.float32), (begin & 255).astype(jnp.float32)]
     parts = in_parts(log_ref[...]) + in_parts(delta) + begins

time: 23.9 us -> 23.8 us (level)
  no operation moved by 1% of the time
where the time goes in v10:
time: 23.8 us; the launch traced here: 23.5 us
  waiting for transfers between devices  9.31 us (39%)
  starting transfers between devices  9.12 us (38%)
  Pallas kernels  4.33 us (18%)
  between operations  0.71 us (3%)
    ppermute x2, waiting for transfers between devices, around(): return lax.ppermute(x, axis, pairs)  6.09 us
    ppermute x2, starting transfers between devices, skewed(): return lax.ppermute(x, ('team', 'blk'), pairs)  5.68 us
    ppermute x2, waiting for transfers between devices, skewed(): return lax.ppermute(x, ('team', 'blk'), pairs)  3.21 us
    ppermute x2, starting transfers between devices, around(): return lax.ppermute(x, axis, pairs)  2.87 us
    pallas_call x1, Pallas kernels, per_device(): pl.pallas_call(load_body, out_shape=[low(lanes, rows), low(heads * (rows...  1.12 us
    pallas_call x1, Pallas kernels, per_device(): pl.pallas_call(own_body, out_shape=[low(heads * rows, 2 * rows), full(lan...  0.92 us
    pallas_call x1, Pallas kernels, per_device(): pl.pallas_call(functools.partial(rest_body, steps), out_shape=[low(heads...  0.91 us
    pallas_call x1, Pallas kernels, per_device(): pl.pallas_call(end_body, out_shape=[jax.ShapeDtypeStruct((rows, features)...  0.71 us
  transfers between devices with their start and end apart: 6, of which 3 were waited for; matrix products, arithmetic and copies ran while one was open for 0% of the time, Pallas kernels for 8%

profile of v10, /device:TPU:0, one launch (start us, length us, event | category | flops | bytes accessed | tf_op | source)
XLA Modules:
  0.0 23.5 jit_solution(1564808280352358584)
XLA Ops:
  0.6 1.1 %shard_map.94 = (bf16[128,128]{1,0:T(8,128)(2,1)S(1)}, bf16[1088,128]{1,0:T(8,128)(2,1)S(1)}, bf16[128,512]{1,0:T(8,128)(2,1)S(1)}, f32[8,128]{1,0:T(8,128)S(1)}, s32[1,128]{1,0:T(1,128)S(1)}) custom-call(bf16[128,512]{1,0:T(8,128)(2,1)} %q_in.1, bf16[128,512]{1,0:T(8,128)(2,1)} %g_in.1, bf16[128,512]{1,0:T(8,128)(2,1)} %o_in.1, f32[8,128]{1,0:T(8,128)} %log_in.1, ...), custom_call_target="tpu_custom_call" | custom-call | tf_op jit(solution)/shard_map/pallas_call | solution.py:277
  1.8 0.2 shard_map.95.refs_0_
  1.9 0.5 %collective-permute-start = (bf16[1088,128]{1,0:T(8,128)(2,1)S(1)}, bf16[1088,128]{1,0:T(8,128)(2,1)S(1)}, u32[]{:S(2)}, u32[]{:S(2)}) collective-permute-start(bf16[1088,128]{1,0:T(8,128)(2,1)S(1)} %shard_map.95.refs_0_), channel_id=1, source_target_pairs={{0,8},{8,0},{16,24},{24,16},{1,9},{9,1},{17,25},{25,17},{2,10},{10... | collective-permute-start | bytes 835592 | tf_op jit(solution)/shard_map/ppermute | solution.py:25
  2.5 4.4 %collective-permute-start.2 = (bf16[128,128]{1,0:T(8,128)(2,1)S(1)}, bf16[128,128]{1,0:T(8,128)(2,1)S(1)}, u32[]{:S(2)}, u32[]{:S(2)}) collective-permute-start(bf16[128,128]{1,0:T(8,128)(2,1)S(1)} %get-tuple-element.23.refs_2_.refs_3_), channel_id=1, source_target_pairs={{0,16},{1,17},{2,18},{3,19},{4,20},{5,21},{6,22},{7,23},{8,24},{9,... | collective-permute-start | bytes 98312 | tf_op jit(solution)/shard_map/ppermute | solution.py:39
  6.8 1.6 %collective-permute-start.1 = (bf16[128,128]{1,0:T(8,128)(2,1)S(1)}, bf16[128,128]{1,0:T(8,128)(2,1)S(1)}, u32[]{:S(2)}, u32[]{:S(2)}) collective-permute-start(bf16[128,128]{1,0:T(8,128)(2,1)S(1)} %get-tuple-element.23.refs_2_.refs_3_), channel_id=1, source_target_pairs={{0,1},{1,2},{2,3},{3,4},{4,5},{5,6},{6,7},{7,0},{8,9},{9,10},{10,1... | collective-permute-start | bytes 98312 | tf_op jit(solution)/shard_map/ppermute | solution.py:20
  8.4 0.0 collective-permute-done.refs_1_
  8.4 0.9 %shard_map.96 = (bf16[1024,256]{1,0:T(8,128)(2,1)S(1)}, f32[128,128]{1,0:T(8,128)S(1)}) custom-call(bf16[1088,128]{1,0:T(8,128)(2,1)S(1)} %shard_map.95.refs_0_, bf16[1088,128]{1,0:T(8,128)(2,1)S(1)} %collective-permute-done.refs_1_, bf16[128,128]{1,0:T(8,128)(2,1)S(1)} %get-tuple-element.23.refs_2_.refs_3_), custom_call_target="tpu_custom_call" | custom-call | tf_op jit(solution)/shard_map/pallas_call | solution.py:313
  9.3 0.0 collective-permute-done.2.refs_2_.refs_5_
  9.4 0.9 %shard_map.98 = (bf16[1024,256]{1,0:T(8,128)(2,1)S(1)}, bf16[128,128]{1,0:T(8,128)(2,1)S(1)}) custom-call(bf16[1088,128]{1,0:T(8,128)(2,1)S(1)} %shard_map.95.refs_0_, bf16[1088,128]{1,0:T(8,128)(2,1)S(1)} %collective-permute-done.refs_1_, bf16[128,128]{1,0:T(8,128)(2,1)S(1)} %collective-permute-done.2.refs_2_.refs_5_), custom_call_target="tpu_custom_call" | custom-call | tf_op jit(solution)/shard_map/pallas_call | solution.py:327
  10.3 3.2 %collective-permute-done.1.refs_2_.refs_4_ = bf16[128,128]{1,0:T(8,128)(2,1)S(1)} collective-permute-done((bf16[128,128]{1,0:T(8,128)(2,1)S(1)}, bf16[128,128]{1,0:T(8,128)(2,1)S(1)}, u32[]{:S(2)}, u32[]{:S(2)}) %collective-permute-start.1) | collective-permute-done | bytes 32800 | tf_op jit(solution)/shard_map/ppermute | solution.py:20
  13.6 0.4 %shard_map.99 = (f32[128,512]{1,0:T(8,128)S(1)}, bf16[128,512]{1,0:T(8,128)(2,1)S(1)}) custom-call(bf16[1024,256]{1,0:T(8,128)(2,1)S(1)} %get-tuple-element.24.refs_0_, bf16[1024,256]{1,0:T(8,128)(2,1)S(1)} %get-tuple-element.25.refs_1_, bf16[1024,256]{1,0:T(8,128)(2,1)S(1)} %get-tuple-element.26.refs_2_, ...), custom_call_target="tpu_custom_call" | custom-call | tf_op jit(solution)/shard_map/pallas_call | solution.py:334
  14.0 0.1 collective-permute-start.3
  14.1 1.3 %collective-permute-start.5 = (bf16[128,128]{1,0:T(8,128)(2,1)S(1)}, bf16[128,128]{1,0:T(8,128)(2,1)S(1)}, u32[]{:S(2)}, u32[]{:S(2)}) collective-permute-start(bf16[128,128]{1,0:T(8,128)(2,1)S(1)} %get-tuple-element.31), channel_id=1, source_target_pairs={{16,0},{17,1},{18,2},{19,3},{20,4},{21,5},{22,6},{23,7},{24,8},{25... | collective-permute-start | bytes 98312 | tf_op jit(solution)/shard_map/ppermute | solution.py:39
  15.4 1.3 %collective-permute-start.4 = (bf16[128,128]{1,0:T(8,128)(2,1)S(1)}, bf16[128,128]{1,0:T(8,128)(2,1)S(1)}, u32[]{:S(2)}, u32[]{:S(2)}) collective-permute-start(bf16[128,128]{1,0:T(8,128)(2,1)S(1)} %get-tuple-element.30), channel_id=1, source_target_pairs={{1,0},{2,1},{3,2},{4,3},{5,4},{6,5},{7,6},{9,8},{10,9},{11,10},{12... | collective-permute-start | bytes 98312 | tf_op jit(solution)/shard_map/ppermute | solution.py:20
  16.7 3.2 %collective-permute-done.5.refs_1_ = bf16[128,128]{1,0:T(8,128)(2,1)S(1)} collective-permute-done((bf16[128,128]{1,0:T(8,128)(2,1)S(1)}, bf16[128,128]{1,0:T(8,128)(2,1)S(1)}, u32[]{:S(2)}, u32[]{:S(2)}) %collective-permute-start.5) | collective-permute-done | bytes 32800 | tf_op jit(solution)/shard_map/ppermute | solution.py:39
  19.9 2.9 %collective-permute-done.4.refs_0_ = bf16[128,128]{1,0:T(8,128)(2,1)S(1)} collective-permute-done((bf16[128,128]{1,0:T(8,128)(2,1)S(1)}, bf16[128,128]{1,0:T(8,128)(2,1)S(1)}, u32[]{:S(2)}, u32[]{:S(2)}) %collective-permute-start.4) | collective-permute-done | bytes 32800 | tf_op jit(solution)/shard_map/ppermute | solution.py:20
  22.8 0.0 collective-permute-done.3.query_back_ref
  22.8 0.7 %shard_map.100 = (bf16[128,512]{1,0:T(8,128)(2,1)}, bf16[64,128]{1,0:T(8,128)(2,1)}, bf16[64,128]{1,0:T(8,128)(2,1)}) custom-call(f32[128,512]{1,0:T(8,128)S(1)} %get-tuple-element.27.query_ref, bf16[128,512]{1,0:T(8,128)(2,1)S(1)} %collective-permute-done.3.query_back_ref, f32[128,128]{1,0:T(8,128)S(1)} %get-tuple-element.29.total_ref, ...), custom_call_target="tpu_custom_call" | custom-call | tf_op jit(solution)/shard_map/pallas_call | solution.py:345
  (1 shorter events, 0.0 us)
Async XLA Ops:
  1.9 6.5 %collective-permute-start = (bf16[1088,128]{1,0:T(8,128)(2,1)S(1)}, bf16[1088,128]{1,0:T(8,128)(2,1)S(1)}, u32[]{:S(2)}, u32[]{:S(2)}) collective-permute-start(bf16[1088,128]{1,0:T(8,128)(2,1)S(1)} %shard_map.95.refs_0_), channel_id=1, source_target_pairs={{0,8},{8,0},{16,24},{24,16},{1,9},{9,1},{17,25},{25,17},{2,10},{10... | collective-permute-start | bytes 835592 | tf_op jit(solution)/shard_map/ppermute | solution.py:25
  2.5 6.9 %collective-permute-start.2 = (bf16[128,128]{1,0:T(8,128)(2,1)S(1)}, bf16[128,128]{1,0:T(8,128)(2,1)S(1)}, u32[]{:S(2)}, u32[]{:S(2)}) collective-permute-start(bf16[128,128]{1,0:T(8,128)(2,1)S(1)} %get-tuple-element.23.refs_2_.refs_3_), channel_id=1, source_target_pairs={{0,16},{1,17},{2,18},{3,19},{4,20},{5,21},{6,22},{7,23},{8,24},{9,... | collective-permute-start | bytes 98312 | tf_op jit(solution)/shard_map/ppermute | solution.py:39
  6.8 6.7 %collective-permute-start.1 = (bf16[128,128]{1,0:T(8,128)(2,1)S(1)}, bf16[128,128]{1,0:T(8,128)(2,1)S(1)}, u32[]{:S(2)}, u32[]{:S(2)}) collective-permute-start(bf16[128,128]{1,0:T(8,128)(2,1)S(1)} %get-tuple-element.23.refs_2_.refs_3_), channel_id=1, source_target_pairs={{0,1},{1,2},{2,3},{3,4},{4,5},{5,6},{6,7},{7,0},{8,9},{9,10},{10,1... | collective-permute-start | bytes 98312 | tf_op jit(solution)/shard_map/ppermute | solution.py:20
  14.0 8.7 %collective-permute-start.3 = (bf16[128,512]{1,0:T(8,128)(2,1)S(1)}, bf16[128,512]{1,0:T(8,128)(2,1)S(1)}, u32[]{:S(2)}, u32[]{:S(2)}) collective-permute-start(bf16[128,512]{1,0:T(8,128)(2,1)S(1)} %get-tuple-element.28), channel_id=1, source_target_pairs={{0,8},{8,0},{16,24},{24,16},{1,9},{9,1},{17,25},{25,17},{2,10},{10... | collective-permute-start | bytes 393224 | tf_op jit(solution)/shard_map/ppermute | solution.py:25
  14.1 5.8 %collective-permute-start.5 = (bf16[128,128]{1,0:T(8,128)(2,1)S(1)}, bf16[128,128]{1,0:T(8,128)(2,1)S(1)}, u32[]{:S(2)}, u32[]{:S(2)}) collective-permute-start(bf16[128,128]{1,0:T(8,128)(2,1)S(1)} %get-tuple-element.31), channel_id=1, source_target_pairs={{16,0},{17,1},{18,2},{19,3},{20,4},{21,5},{22,6},{23,7},{24,8},{25... | collective-permute-start | bytes 98312 | tf_op jit(solution)/shard_map/ppermute | solution.py:39
  15.4 7.4 %collective-permute-start.4 = (bf16[128,128]{1,0:T(8,128)(2,1)S(1)}, bf16[128,128]{1,0:T(8,128)(2,1)S(1)}, u32[]{:S(2)}, u32[]{:S(2)}) collective-permute-start(bf16[128,128]{1,0:T(8,128)(2,1)S(1)} %get-tuple-element.30), channel_id=1, source_target_pairs={{1,0},{2,1},{3,2},{4,3},{5,4},{6,5},{7,6},{9,8},{10,9},{11,10},{12... | collective-permute-start | bytes 98312 | tf_op jit(solution)/shard_map/ppermute | solution.py:20

commit v11 on v10

--- a/solution.py
+++ b/solution.py
@@ -163,7 +163,7 @@
 
 
 def slab_of(terms, number, rows):
-    return terms[number * rows : (number + 1) * rows, :].T
+    return terms[number * rows : (number + 1) * rows, :]
 
 
 def own_body(*refs):
@@ -238,7 +238,7 @@
     total = total_ref[...]
     for ref in term_refs:
         total = total + ref[...].astype(jnp.float32)
-    kv_buf[...] = total.astype(kv_buf.dtype)
+    kv_buf[...] = total.T.astype(kv_buf.dtype)
     copies.append(pltpu.make_async_copy(kv_buf.at[:width, :], k_out, sems.at[1]))
     copies.append(pltpu.make_async_copy(kv_buf.at[width:, :], v_out, sems.at[2]))
     for copy in copies[1:]:
@@ -312,21 +312,21 @@
     seen = [skewed(mine, k, True) for k in steps]
     own_grads, total = pl.pallas_call(
         own_body,
-        out_shape=[low(heads * rows, 2 * rows), full(lanes, rows)],
+        out_shape=[low(heads * rows, 2 * rows), full(rows, lanes)],
         in_specs=in_vmem(FRONT + 1),
         out_specs=in_vmem(2),
         compiler_params=params,
     )(*held(*front, mine))
     past_grads, past_piece = pl.pallas_call(
         past_body,
-        out_shape=[low(heads * rows, 2 * rows), low(lanes, rows)],
+        out_shape=[low(heads * rows, 2 * rows), low(rows, lanes)],
         in_specs=in_vmem(FRONT + 1),
         out_specs=in_vmem(2),
         compiler_params=params,
     )(*held(*front, past))
     rest_grads, *sent = pl.pallas_call(
         functools.partial(rest_body, steps),
-        out_shape=[low(heads * (half - 1) * rows, 2 * rows)] + [low(lanes, rows)] * (half - 1),
+        out_shape=[low(heads * (half - 1) * rows, 2 * rows)] + [low(rows, lanes)] * (half - 1),
         in_specs=in_vmem(FRONT + half - 1),
         out_specs=in_vmem(half),
         compiler_params=params,

time: 23.8 us -> 23.8 us (level)
  transfers between devices with their start and end apart: 6 -> 6, of which waited for: 3 -> 3; matrix products, arithmetic and copies ran while one was open for 0% -> 0% of each run, Pallas kernels for 8% -> 7%
where the time goes in v11:
time: 23.8 us; the launch traced here: 23.5 us
  waiting for transfers between devices  9.45 us (40%)
  starting transfers between devices  9.12 us (38%)
  Pallas kernels  4.23 us (18%)
  between operations  0.7 us (3%)
    ppermute x2, waiting for transfers between devices, around(): return lax.ppermute(x, axis, pairs)  6.23 us
    ppermute x2, starting transfers between devices, skewed(): return lax.ppermute(x, ('team', 'blk'), pairs)  5.68 us
    ppermute x2, waiting for transfers between devices, skewed(): return lax.ppermute(x, ('team', 'blk'), pairs)  3.21 us
    ppermute x2, starting transfers between devices, around(): return lax.ppermute(x, axis, pairs)  2.87 us
    pallas_call x1, Pallas kernels, per_device(): pl.pallas_call(load_body, out_shape=[low(lanes, rows), low(heads * (rows...  1.12 us
    pallas_call x1, Pallas kernels, per_device(): pl.pallas_call(own_body, out_shape=[low(heads * rows, 2 * rows), full(row...  0.86 us
    pallas_call x1, Pallas kernels, per_device(): pl.pallas_call(functools.partial(rest_body, steps), out_shape=[low(heads...  0.84 us
    pallas_call x1, Pallas kernels, per_device(): pl.pallas_call(end_body, out_shape=[jax.ShapeDtypeStruct((rows, features)...  0.74 us
  transfers between devices with their start and end apart: 6, of which 3 were waited for; matrix products, arithmetic and copies ran while one was open for 0% of the time, Pallas kernels for 7%

profile of v11, /device:TPU:0, one launch (start us, length us, event | category | flops | bytes accessed | tf_op | source)
XLA Modules:
  0.0 23.5 jit_solution(2429406827215737162)
XLA Ops:
  0.6 1.1 %shard_map.94 = (bf16[128,128]{1,0:T(8,128)(2,1)S(1)}, bf16[1088,128]{1,0:T(8,128)(2,1)S(1)}, bf16[128,512]{1,0:T(8,128)(2,1)S(1)}, f32[8,128]{1,0:T(8,128)S(1)}, s32[1,128]{1,0:T(1,128)S(1)}) custom-call(bf16[128,512]{1,0:T(8,128)(2,1)} %q_in.1, bf16[128,512]{1,0:T(8,128)(2,1)} %g_in.1, bf16[128,512]{1,0:T(8,128)(2,1)} %o_in.1, f32[8,128]{1,0:T(8,128)} %log_in.1, ...), custom_call_target="tpu_custom_call" | custom-call | tf_op jit(solution)/shard_map/pallas_call | solution.py:277
  1.8 0.2 shard_map.95.refs_0_
  1.9 0.5 %collective-permute-start = (bf16[1088,128]{1,0:T(8,128)(2,1)S(1)}, bf16[1088,128]{1,0:T(8,128)(2,1)S(1)}, u32[]{:S(2)}, u32[]{:S(2)}) collective-permute-start(bf16[1088,128]{1,0:T(8,128)(2,1)S(1)} %shard_map.95.refs_0_), channel_id=1, source_target_pairs={{0,8},{8,0},{16,24},{24,16},{1,9},{9,1},{17,25},{25,17},{2,10},{10... | collective-permute-start | bytes 835592 | tf_op jit(solution)/shard_map/ppermute | solution.py:25
  2.5 4.4 %collective-permute-start.2 = (bf16[128,128]{1,0:T(8,128)(2,1)S(1)}, bf16[128,128]{1,0:T(8,128)(2,1)S(1)}, u32[]{:S(2)}, u32[]{:S(2)}) collective-permute-start(bf16[128,128]{1,0:T(8,128)(2,1)S(1)} %get-tuple-element.23.refs_2_.refs_3_), channel_id=1, source_target_pairs={{0,16},{1,17},{2,18},{3,19},{4,20},{5,21},{6,22},{7,23},{8,24},{9,... | collective-permute-start | bytes 98312 | tf_op jit(solution)/shard_map/ppermute | solution.py:39
  6.8 1.6 %collective-permute-start.1 = (bf16[128,128]{1,0:T(8,128)(2,1)S(1)}, bf16[128,128]{1,0:T(8,128)(2,1)S(1)}, u32[]{:S(2)}, u32[]{:S(2)}) collective-permute-start(bf16[128,128]{1,0:T(8,128)(2,1)S(1)} %get-tuple-element.23.refs_2_.refs_3_), channel_id=1, source_target_pairs={{0,1},{1,2},{2,3},{3,4},{4,5},{5,6},{6,7},{7,0},{8,9},{9,10},{10,1... | collective-permute-start | bytes 98312 | tf_op jit(solution)/shard_map/ppermute | solution.py:20
  8.4 0.0 collective-permute-done.refs_1_
  8.4 0.9 %shard_map.96 = (bf16[1024,256]{1,0:T(8,128)(2,1)S(1)}, f32[128,128]{1,0:T(8,128)S(1)}) custom-call(bf16[1088,128]{1,0:T(8,128)(2,1)S(1)} %shard_map.95.refs_0_, bf16[1088,128]{1,0:T(8,128)(2,1)S(1)} %collective-permute-done.refs_1_, bf16[128,128]{1,0:T(8,128)(2,1)S(1)} %get-tuple-element.23.refs_2_.refs_3_), custom_call_target="tpu_custom_call" | custom-call | tf_op jit(solution)/shard_map/pallas_call | solution.py:313
  9.3 0.0 collective-permute-done.2.refs_2_.refs_5_
  9.3 0.8 %shard_map.98 = (bf16[1024,256]{1,0:T(8,128)(2,1)S(1)}, bf16[128,128]{1,0:T(8,128)(2,1)S(1)}) custom-call(bf16[1088,128]{1,0:T(8,128)(2,1)S(1)} %shard_map.95.refs_0_, bf16[1088,128]{1,0:T(8,128)(2,1)S(1)} %collective-permute-done.refs_1_, bf16[128,128]{1,0:T(8,128)(2,1)S(1)} %collective-permute-done.2.refs_2_.refs_5_), custom_call_target="tpu_custom_call" | custom-call | tf_op jit(solution)/shard_map/pallas_call | solution.py:327
  10.1 3.4 %collective-permute-done.1.refs_2_.refs_4_ = bf16[128,128]{1,0:T(8,128)(2,1)S(1)} collective-permute-done((bf16[128,128]{1,0:T(8,128)(2,1)S(1)}, bf16[128,128]{1,0:T(8,128)(2,1)S(1)}, u32[]{:S(2)}, u32[]{:S(2)}) %collective-permute-start.1) | collective-permute-done | bytes 32800 | tf_op jit(solution)/shard_map/ppermute | solution.py:20
  13.6 0.4 %shard_map.99 = (f32[128,512]{1,0:T(8,128)S(1)}, bf16[128,512]{1,0:T(8,128)(2,1)S(1)}) custom-call(bf16[1024,256]{1,0:T(8,128)(2,1)S(1)} %get-tuple-element.24.refs_0_, bf16[1024,256]{1,0:T(8,128)(2,1)S(1)} %get-tuple-element.25.refs_1_, bf16[1024,256]{1,0:T(8,128)(2,1)S(1)} %get-tuple-element.26.refs_2_, ...), custom_call_target="tpu_custom_call" | custom-call | tf_op jit(solution)/shard_map/pallas_call | solution.py:334
  14.0 0.1 collective-permute-start.3
  14.1 1.3 %collective-permute-start.5 = (bf16[128,128]{1,0:T(8,128)(2,1)S(1)}, bf16[128,128]{1,0:T(8,128)(2,1)S(1)}, u32[]{:S(2)}, u32[]{:S(2)}) collective-permute-start(bf16[128,128]{1,0:T(8,128)(2,1)S(1)} %get-tuple-element.31), channel_id=1, source_target_pairs={{16,0},{17,1},{18,2},{19,3},{20,4},{21,5},{22,6},{23,7},{24,8},{25... | collective-permute-start | bytes 98312 | tf_op jit(solution)/shard_map/ppermute | solution.py:39
  15.4 1.3 %collective-permute-start.4 = (bf16[128,128]{1,0:T(8,128)(2,1)S(1)}, bf16[128,128]{1,0:T(8,128)(2,1)S(1)}, u32[]{:S(2)}, u32[]{:S(2)}) collective-permute-start(bf16[128,128]{1,0:T(8,128)(2,1)S(1)} %get-tuple-element.30), channel_id=1, source_target_pairs={{1,0},{2,1},{3,2},{4,3},{5,4},{6,5},{7,6},{9,8},{10,9},{11,10},{12... | collective-permute-start | bytes 98312 | tf_op jit(solution)/shard_map/ppermute | solution.py:20
  16.7 3.2 %collective-permute-done.5.refs_1_ = bf16[128,128]{1,0:T(8,128)(2,1)S(1)} collective-permute-done((bf16[128,128]{1,0:T(8,128)(2,1)S(1)}, bf16[128,128]{1,0:T(8,128)(2,1)S(1)}, u32[]{:S(2)}, u32[]{:S(2)}) %collective-permute-start.5) | collective-permute-done | bytes 32800 | tf_op jit(solution)/shard_map/ppermute | solution.py:39
  19.9 2.9 %collective-permute-done.4.refs_0_ = bf16[128,128]{1,0:T(8,128)(2,1)S(1)} collective-permute-done((bf16[128,128]{1,0:T(8,128)(2,1)S(1)}, bf16[128,128]{1,0:T(8,128)(2,1)S(1)}, u32[]{:S(2)}, u32[]{:S(2)}) %collective-permute-start.4) | collective-permute-done | bytes 32800 | tf_op jit(solution)/shard_map/ppermute | solution.py:20
  22.8 0.0 collective-permute-done.3.query_back_ref
  22.8 0.7 %shard_map.100 = (bf16[128,512]{1,0:T(8,128)(2,1)}, bf16[64,128]{1,0:T(8,128)(2,1)}, bf16[64,128]{1,0:T(8,128)(2,1)}) custom-call(f32[128,512]{1,0:T(8,128)S(1)} %get-tuple-element.27.query_ref, bf16[128,512]{1,0:T(8,128)(2,1)S(1)} %collective-permute-done.3.query_back_ref, f32[128,128]{1,0:T(8,128)S(1)} %get-tuple-element.29.total_ref, ...), custom_call_target="tpu_custom_call" | custom-call | tf_op jit(solution)/shard_map/pallas_call | solution.py:345
  (1 shorter events, 0.0 us)
Async XLA Ops:
  1.9 6.5 %collective-permute-start = (bf16[1088,128]{1,0:T(8,128)(2,1)S(1)}, bf16[1088,128]{1,0:T(8,128)(2,1)S(1)}, u32[]{:S(2)}, u32[]{:S(2)}) collective-permute-start(bf16[1088,128]{1,0:T(8,128)(2,1)S(1)} %shard_map.95.refs_0_), channel_id=1, source_target_pairs={{0,8},{8,0},{16,24},{24,16},{1,9},{9,1},{17,25},{25,17},{2,10},{10... | collective-permute-start | bytes 835592 | tf_op jit(solution)/shard_map/ppermute | solution.py:25
  2.5 6.8 %collective-permute-start.2 = (bf16[128,128]{1,0:T(8,128)(2,1)S(1)}, bf16[128,128]{1,0:T(8,128)(2,1)S(1)}, u32[]{:S(2)}, u32[]{:S(2)}) collective-permute-start(bf16[128,128]{1,0:T(8,128)(2,1)S(1)} %get-tuple-element.23.refs_2_.refs_3_), channel_id=1, source_target_pairs={{0,16},{1,17},{2,18},{3,19},{4,20},{5,21},{6,22},{7,23},{8,24},{9,... | collective-permute-start | bytes 98312 | tf_op jit(solution)/shard_map/ppermute | solution.py:39
  6.8 6.7 %collective-permute-start.1 = (bf16[128,128]{1,0:T(8,128)(2,1)S(1)}, bf16[128,128]{1,0:T(8,128)(2,1)S(1)}, u32[]{:S(2)}, u32[]{:S(2)}) collective-permute-start(bf16[128,128]{1,0:T(8,128)(2,1)S(1)} %get-tuple-element.23.refs_2_.refs_3_), channel_id=1, source_target_pairs={{0,1},{1,2},{2,3},{3,4},{4,5},{5,6},{6,7},{7,0},{8,9},{9,10},{10,1... | collective-permute-start | bytes 98312 | tf_op jit(solution)/shard_map/ppermute | solution.py:20
  14.0 8.7 %collective-permute-start.3 = (bf16[128,512]{1,0:T(8,128)(2,1)S(1)}, bf16[128,512]{1,0:T(8,128)(2,1)S(1)}, u32[]{:S(2)}, u32[]{:S(2)}) collective-permute-start(bf16[128,512]{1,0:T(8,128)(2,1)S(1)} %get-tuple-element.28), channel_id=1, source_target_pairs={{0,8},{8,0},{16,24},{24,16},{1,9},{9,1},{17,25},{25,17},{2,10},{10... | collective-permute-start | bytes 393224 | tf_op jit(solution)/shard_map/ppermute | solution.py:25
  14.1 5.8 %collective-permute-start.5 = (bf16[128,128]{1,0:T(8,128)(2,1)S(1)}, bf16[128,128]{1,0:T(8,128)(2,1)S(1)}, u32[]{:S(2)}, u32[]{:S(2)}) collective-permute-start(bf16[128,128]{1,0:T(8,128)(2,1)S(1)} %get-tuple-element.31), channel_id=1, source_target_pairs={{16,0},{17,1},{18,2},{19,3},{20,4},{21,5},{22,6},{23,7},{24,8},{25... | collective-permute-start | bytes 98312 | tf_op jit(solution)/shard_map/ppermute | solution.py:39
  15.4 7.4 %collective-permute-start.4 = (bf16[128,128]{1,0:T(8,128)(2,1)S(1)}, bf16[128,128]{1,0:T(8,128)(2,1)S(1)}, u32[]{:S(2)}, u32[]{:S(2)}) collective-permute-start(bf16[128,128]{1,0:T(8,128)(2,1)S(1)} %get-tuple-element.30), channel_id=1, source_target_pairs={{1,0},{2,1},{3,2},{4,3},{5,4},{6,5},{7,6},{9,8},{10,9},{11,10},{12... | collective-permute-start | bytes 98312 | tf_op jit(solution)/shard_map/ppermute | solution.py:20
